TPU v7x, 32 devices: a whole 2x2x4 slice. The times are simulated.
32 devices in a mesh: dp: 4 (over y, core), seq: 8 (over z, x).
Axes of the slice: x: 2, y: 2, z: 4, core: 2. Of those that a mesh axis runs over, the one named last changes fastest.
Arguments:
- layer_input: bfloat16 [4096, 8192], P(('dp', 'seq')), may hold values from -6 to 6
- queries: bfloat16 [4096, 4096], P(('dp', 'seq')), may hold values from -110 to 110, as said below
- key_states: bfloat16 [4096, 512], P(('dp', 'seq')), may hold values from -12 to 12, as said below
- value_states: bfloat16 [4096, 512], P(('dp', 'seq')), may hold values from -6 to 6
- out_grad: bfloat16 [4096, 4096], P(('dp', 'seq')), may hold values from -6 to 6
Outputs:
- query_grad: bfloat16 [4096, 4096], P(('dp', 'seq'))
- key_grad: bfloat16 [4096, 512], P(('dp', 'seq'))
- value_grad: bfloat16 [4096, 512], P(('dp', 'seq'))
- weight_grad: float32 [8192, 1024], P(('dp', 'seq'))
Inputs may be any that keep to these rules, and one draw needn't show every extreme that they name: `queries`: rows of rough scales; some queries may nearly coincide in direction with keys of earlier positions. `key_states`: rows of rough scales.
All inputs are finite; a program needn't handle non-finite values.
Results may differ from a plain program's by a relative error of at most 0.0051.
Values may be sent and summed in bfloat16 or wider, within the bound.
No kernel may reach another device: no remote copies, remote signals or barrier semaphores. Data moves between devices by JAX's collectives and lax.ppermute only.
A program may use at most 128 MiB of HBM per device.

v0:
```python
import math

import jax
import jax.numpy as jnp
from jax import lax
from jax.sharding import PartitionSpec as P

D = 8192
QH = 32
KVH = 4
HD = 128


NEGATIVE = -1e30


def local(layer_input, queries, key_states, value_states, out_grad):
    local_rows = layer_input.shape[0]
    cycle_size = lax.axis_size("seq")
    replicas = lax.axis_size("dp")
    position = lax.axis_index("seq")
    length = local_rows * cycle_size
    group = QH // KVH
    channels = KVH * HD
    scale = 1.0 / math.sqrt(HD)
    block = math.gcd(length, 512)
    key_all, value_all = (
        lax.all_gather(key_states, "seq", axis=0, tiled=True),
        lax.all_gather(value_states, "seq", axis=0, tiled=True),
    )
    query_heads = queries.reshape(local_rows, KVH, group, HD)
    grad_heads = out_grad.reshape(local_rows, KVH, group, HD)
    query_place = position * local_rows + jnp.arange(local_rows, dtype=jnp.int32)
    needed = (position * local_rows + local_rows + block - 1) // block

    def block_scores(begin):
        key_block = lax.dynamic_slice_in_dim(key_all, begin, block, 0).reshape(block, KVH, HD)
        value_block = lax.dynamic_slice_in_dim(value_all, begin, block, 0).reshape(block, KVH, HD)
        scores = (
            jnp.einsum("tkgd,skd->kgts", query_heads, key_block, preferred_element_type=jnp.float32)
            * scale
        )
        key_place = begin + jnp.arange(block, dtype=jnp.int32)
        visible = key_place[None, :] <= query_place[:, None]
        scores = jnp.where(visible, scores, NEGATIVE)
        grad_probs = jnp.einsum(
            "tkgd,skd->kgts", grad_heads, value_block, preferred_element_type=jnp.float32
        )
        return (key_block, scores, grad_probs)

    def first_pass(step_index, carry):
        row_max, denom, weighted = carry
        key_block, scores, grad_probs = block_scores(step_index * block)
        new_max = jnp.maximum(row_max, jnp.max(scores, axis=-1))
        factor = jnp.exp(row_max - new_max)
        expon = jnp.exp(scores - new_max[..., None])
        return (
            new_max,
            denom * factor + jnp.sum(expon, axis=-1),
            weighted * factor + jnp.sum(expon * grad_probs, axis=-1),
        )

    stats_shape = (KVH, group, local_rows)
    start_stats = (
        jnp.full(stats_shape, NEGATIVE, jnp.float32),
        jnp.zeros(stats_shape, jnp.float32),
        jnp.zeros(stats_shape, jnp.float32),
    )
    row_max, denom, weighted = lax.fori_loop(0, needed, first_pass, start_stats)
    delta = weighted / denom

    def second_pass(step_index, carry):
        grad_query, terms = carry
        begin = step_index * block
        key_block, scores, grad_probs = block_scores(begin)
        probs = jnp.exp(scores - row_max[..., None]) / denom[..., None]
        grad_scores = (scale * probs * (grad_probs - delta[..., None])).astype(jnp.bfloat16)
        probs_low = probs.astype(jnp.bfloat16)
        grad_query = grad_query + jnp.einsum(
            "kgts,skd->tkgd", grad_scores, key_block, preferred_element_type=jnp.float32
        )
        key_part = jnp.einsum(
            "kgts,tkgd->skd", grad_scores, query_heads, preferred_element_type=jnp.float32
        )
        value_part = jnp.einsum(
            "kgts,tkgd->skd", probs_low, grad_heads, preferred_element_type=jnp.float32
        )
        joined = jnp.concatenate(
            [key_part.reshape(block, channels), value_part.reshape(block, channels)], axis=1
        )
        terms = lax.dynamic_update_slice_in_dim(terms, joined, begin, 0)
        return (grad_query, terms)

    start_grads = (
        jnp.zeros((local_rows, KVH, group, HD), jnp.float32),
        jnp.zeros((length, 2 * channels), jnp.float32),
    )
    grad_query, terms = lax.fori_loop(0, needed, second_pass, start_grads)
    query_grad = grad_query.reshape(local_rows, QH * HD).astype(jnp.bfloat16)
    owned_grads = lax.psum_scatter(terms, "seq", scatter_dimension=0, tiled=True).astype(
        jnp.bfloat16
    )
    summed_grads = lax.all_gather(owned_grads, "seq", axis=0, tiled=True)
    slab = D // (replicas * cycle_size)
    columns = lax.all_to_all(
        layer_input.reshape(local_rows, replicas, cycle_size, slab),
        "seq",
        split_axis=2,
        concat_axis=0,
        tiled=True,
    )
    columns = columns.reshape(length, replicas * slab)
    weight_grad = lax.psum_scatter(
        jnp.einsum("tr,tc->rc", columns, summed_grads, preferred_element_type=jnp.float32),
        "dp",
        scatter_dimension=0,
        tiled=True,
    )
    return (query_grad, owned_grads[:, :channels], owned_grads[:, channels:], weight_grad)


def solution(mesh):
    in_specs = (
        P(("dp", "seq"), None),
        P(("dp", "seq"), None),
        P(("dp", "seq"), None),
        P(("dp", "seq"), None),
        P(("dp", "seq"), None),
    )
    out_specs = (
        P(("dp", "seq"), None),
        P(("dp", "seq"), None),
        P(("dp", "seq"), None),
        P(("dp", "seq"), None),
    )
    return jax.shard_map(local, mesh=mesh, in_specs=in_specs, out_specs=out_specs, check_vma=False)
```

profile of v0, /device:TPU:0, one launch (start us, length us, event | category | flops | bytes accessed | tf_op | source)
XLA Modules:
  0.0 388.9 jit_solution(6068416372018879133)
XLA Ops:
  7.2 1.7 copy.69
  8.9 1.7 copy.71
  15.9 37.0 %all-gather.4.cloned.1.call-done = bf16[1024,512]{0,1:T(8,128)(2,1)} async-done(((bf16[128,512]{0,1:T(8,128)(2,1)}), bf16[1024,512]{0,1:T(8,128)(2,1)}) %all-gather.4.cloned.1.call-update) | async-done | bytes 1048592 | tf_op jit(solution)/shard_map/all_gather | solution.py:28
  52.9 41.1 %all-gather.6.cloned.1.call-done = bf16[1024,512]{0,1:T(8,128)(2,1)} async-done(((bf16[128,512]{0,1:T(8,128)(2,1)}), bf16[1024,512]{0,1:T(8,128)(2,1)}) %all-gather.6.cloned.1.call-update) | async-done | bytes 1048592 | tf_op jit(solution)/shard_map/all_gather | solution.py:29
  94.0 7.5 %while.28 = (s32[]{:T(128)}, f32[4,8,128]{2,1,0:T(8,128)S(1)}, f32[4,8,128]{2,1,0:T(8,128)S(1)}, f32[4,8,128]{2,1,0:T(8,128)S(1)}, s32[]{:T(128)}, /*index=5*/bf...) while((s32[]{:T(128)}, f32[4,8,128]{2,1,0:T(8,128)S(1)}, ...), condition=%wide.region_4.5_spmd.clone, body=%wide.region_0.4_spmd.clone.sunk | while | flops 1098986112 | bytes 35165400 | solution.py:69
  96.9 1.8 fusion.59
  98.7 2.7 fusion.58
  101.5 2.5 broadcast_in_dim.32.clone
  104.0 1.6 broadcast_in_dim.31
  105.6 19.8 %while.29 = (s32[]{:T(128)}, f32[128,4,8,128]{0,3,2,1:T(8,128)}, f32[1024,1024]{1,0:T(8,128)}, s32[]{:T(128)}, bf16[1024,512]{0,1:T(8,128)(2,1)}, /*index=5*/bf1...) while((s32[]{:T(128)}, f32[128,4,8,128]{0,3,2,1:T(8,128)}, ...), condition=%wide.region_6.7_spmd.clone, body=%wide.region_5.6_spmd.clone.sunk | while | flops 2704343552 | bytes 108713312 | solution.py:98
  105.6 1.6 constant_dynamic-slice_fusion.7
  107.4 2.3 fusion.70
  109.8 1.7 fusion.71
  116.4 1.9 copy.110
  121.3 4.1 %bitcast_add_fusion.2 = f32[128,4,8,128]{0,3,2,1:T(8,128)} fusion(f32[128,4,8,128]{0,3,2,1:T(8,128)} %get-tuple-element.501, bf16[512,4,128,1]{0,2,3,1:T(8,128)(2,1)} %bitcast.153, bf16[4,8,128,512]{2,3,1,0:T(8,128)(2,1)S(1)} %copy-done.1), kind=kOutput, calls=%fused_computation.26.clone.1 | convolution fusion | flops 537395200 | bytes 8912896 | tf_op jit(solution)/shard_map/while/body/kgts,skd->tkgd/dot_general | solution.py:79
  125.4 3.2 copy.77
  130.1 30.8 %all-to-all-start = ((bf16[128,4,8,256]{0,3,1,2:T(8,128)(2,1)}), bf16[128,4,8,256]{0,3,1,2:T(8,128)(2,1)S(1)}, u32[]{:S(2)}, u32[]{:S(2)}) async-start(bf16[128,4,8,256]{0,3,1,2:T(8,128)(2,1)} %copy.78), calls=%async_computation.1 | async-start | bytes 4194304 | tf_op jit(solution)/shard_map/all_to_all | solution.py:105
  161.0 117.2 %reduce-scatter.3.cloned.1.call-done = f32[128,1024]{1,0:T(8,128)} async-done(((f32[1024,1024]{1,0:T(8,128)}), f32[128,1024]{1,0:T(8,128)}) %reduce-scatter.3.cloned.1.call-update) | async-done | bytes 524304 | tf_op jit(solution)/shard_map/reduce_scatter | solution.py:100
  278.2 1.8 convert_element_type.17
  280.3 2.7 copy.79
  283.0 47.1 %all-gather.8.cloned.1.call-done = bf16[1024,1024]{1,0:T(8,128)(2,1)} async-done(((bf16[128,1024]{1,0:T(8,128)(2,1)}), bf16[1024,1024]{1,0:T(8,128)(2,1)}) %all-gather.8.cloned.1.call-update) | async-done | bytes 2097168 | tf_op jit(solution)/shard_map/all_gather | solution.py:103
  330.0 6.6 %convolution_bitcast_fusion = f32[1024,1024]{0,1:T(8,128)} fusion(bf16[1024,1024]{1,0:T(8,128)(2,1)} %all-gather.8.cloned.1.call-done, bf16[128,8,8,128]{3,2,1,0:T(8,128)(2,1)} %bitcast.159), kind=kOutput, calls=%fused_computation.33 | convolution fusion | flops 2147483648 | bytes 8388608 | tf_op jit(solution)/shard_map/tr,tc->rc/dot_general | solution.py:114
  340.4 39.4 %reduce-scatter.5.cloned.1.call-done = f32[256,1024]{0,1:T(8,128)} async-done(((f32[1024,1024]{0,1:T(8,128)}), f32[256,1024]{0,1:T(8,128)}) %reduce-scatter.5.cloned.1.call-update) | async-done | bytes 1048592 | tf_op jit(solution)/shard_map/reduce_scatter | solution.py:113
  379.8 2.5 copy.80
  (54 shorter events, 21.9 us)
Async XLA Ops:
  7.2 45.7 %all-gather.4.cloned.1.call-start = ((), (), s32[]{:S(2)}) async-start(), calls=%async_computation.3 | async-start | bytes 1179648 | tf_op jit(solution)/shard_map/all_gather | solution.py:28
  8.9 85.1 %all-gather.6.cloned.1.call-start = ((), (), s32[]{:S(2)}) async-start(), calls=%async_computation.4 | async-start | bytes 1179648 | tf_op jit(solution)/shard_map/all_gather | solution.py:29
  10.6 267.5 %reduce-scatter.3.cloned.1.call-start = ((), (), s32[]{:S(2)}) async-start(), calls=%async_computation.5 | async-start | bytes 4718592 | tf_op jit(solution)/shard_map/reduce_scatter | solution.py:100
  96.9 1.8 copy-start.7
  105.6 5.8 %copy-start.3 = (bf16[128,4,8,128]{0,3,2,1:T(8,128)(2,1)}, bf16[128,4,8,128]{0,3,2,1:T(8,128)(2,1)S(1)}, u32[]{:S(2)}) copy-start(bf16[128,4,8,128]{0,3,2,1:T(8,128)(2,1)S(1)} %get-tuple-element.521) | copy-start | bytes 3145732 | tf_op jit(solution)/shard_map/while
  107.2 2.5 copy-start.5
  111.5 2.0 copy-start
  118.3 2.9 copy-start.1
  121.3 4.1 %copy-start.4 = (bf16[128,4,8,128]{0,3,2,1:T(8,128)(2,1)S(1)}, bf16[128,4,8,128]{0,3,2,1:T(8,128)(2,1)}, u32[]{:S(2)}) copy-start(bf16[128,4,8,128]{0,3,2,1:T(8,128)(2,1)} %copy-done.3) | copy-start | bytes 3145732 | tf_op jit(solution)/shard_map/while
  130.1 150.1 %all-to-all-start = ((bf16[128,4,8,256]{0,3,1,2:T(8,128)(2,1)}), bf16[128,4,8,256]{0,3,1,2:T(8,128)(2,1)S(1)}, u32[]{:S(2)}, u32[]{:S(2)}) async-start(bf16[128,4,8,256]{0,3,1,2:T(8,128)(2,1)} %copy.78), calls=%async_computation.1 | async-start | bytes 4194304 | tf_op jit(solution)/shard_map/all_to_all | solution.py:105
  160.9 169.1 %all-gather.8.cloned.1.call-start = ((), (), s32[]{:S(2)}) async-start(), calls=%async_computation.6 | async-start | bytes 2359296 | tf_op jit(solution)/shard_map/all_gather | solution.py:103
  280.0 99.8 %reduce-scatter.5.cloned.1.call-start = ((), (), s32[]{:S(2)}) async-start(), calls=%async_computation.7 | async-start | bytes 5242880 | tf_op jit(solution)/shard_map/reduce_scatter | solution.py:113
  336.6 1.6 copy-start.2
  336.6 3.1 copy-start.6
Sparse Core Ops, SparseCore 0:
  10.6 42.2 all-gather.3
  55.5 38.4 all-gather.5
  125.5 152.5 reduce-scatter.2
  280.9 49.0 all-gather.7
  336.8 42.9 reduce-scatter.4
where the time goes:
time: 390 us; the launch traced here: 389 us
  waiting for transfers between devices  282 us (72%)
  local copies, waits for them, and re-layouts  34.5 us (9%)
  starting transfers between devices  31.2 us (8%)
  matrix products  21.8 us (6%)
  between operations  13.9 us (4%)
  other arithmetic  5.56 us (1%)
    reduce_scatter x1, waiting for transfers between devices, local(): lax.psum_scatter(terms, 'seq', scatter_dimension=0, tiled=True)  117 us
    all_gather x1, waiting for transfers between devices, local(): summed_grads = lax.all_gather(owned_grads, 'seq', axis=0, tiled=True)  47.1 us
    all_gather x1, waiting for transfers between devices, local(): lax.all_gather(value_states, 'seq', axis=0, tiled=True)  41.1 us
    reduce_scatter x1, waiting for transfers between devices, local(): lax.psum_scatter(jnp.einsum('tr,tc->rc', columns, summed_grads, preferred...  39.4 us
    all_gather x1, waiting for transfers between devices, local(): lax.all_gather(key_states, 'seq', axis=0, tiled=True)  37 us
    all_to_all x1, starting transfers between devices, local(): lax.all_to_all(layer_input.reshape(local_rows, replicas, cycle_size, slab...  30.8 us
    unnamed x12, local copies, waits for them, and re-layouts  15.9 us
  transfers between devices with their start and end apart: 6, of which 5 were waited for; matrix products, arithmetic and copies ran while one was open for 5% of the time, Pallas kernels for 0%

commit v1 on v0

v1 whole, which is shorter than its diff:
```python
import math

import jax
import jax.numpy as jnp
from jax import lax
from jax.experimental import pallas as pl
from jax.experimental.pallas import tpu as pltpu
from jax.sharding import PartitionSpec as P

D = 8192
QH = 32
KVH = 4
HD = 128
GROUP = QH // KVH
WIDE = GROUP * HD
TILE = 256
NEGATIVE = -1e30
BF16 = jnp.bfloat16
F32 = jnp.float32
VMEM_BYTES = 48 * 1024 * 1024

NT = (((1,), (1,)), ((), ()))


def attention_kernel(rows, groups, *refs):
    span = KVH * rows
    q_hbm, do_hbm, k_hbm, v_hbm = refs[:4]
    pieces = refs[4 : 4 + KVH - 1]
    at = 4 + KVH - 1
    earlier = refs[at : at + KVH * (groups - 1)]
    at += KVH * (groups - 1)
    dq_out = refs[at : at + KVH]
    at += KVH
    own_out = refs[at]
    at += 1
    down_out = refs[at : at + groups - 1]
    at += groups - 1
    q_s, do_s, k_s, v_s, kt_s, dq_s, dk_s, dv_s, down_s, sems = refs[at:]

    place = lax.axis_index("seq")
    group = place // KVH
    head = place % KVH

    def row_at(k, base=0):
        return pl.ds(pl.multiple_of(base + (head ^ k) * rows, rows), rows)

    def column_at(block):
        return pl.ds(pl.multiple_of(head * block, block), block)

    copies = [
        pltpu.make_async_copy(q_hbm.at[:, column_at(WIDE)], q_s.at[row_at(0)], sems.at[0]),
        pltpu.make_async_copy(do_hbm.at[:, column_at(WIDE)], do_s.at[row_at(0)], sems.at[1]),
        pltpu.make_async_copy(k_hbm.at[:, column_at(HD)], k_s.at[row_at(0, group * span)], sems.at[2]),
        pltpu.make_async_copy(v_hbm.at[:, column_at(HD)], v_s.at[row_at(0, group * span)], sems.at[3]),
    ]
    for k in range(1, KVH):
        piece = pieces[k - 1]
        slot = 4 * k
        copies += [
            pltpu.make_async_copy(piece.at[:, :WIDE], q_s.at[row_at(k)], sems.at[slot]),
            pltpu.make_async_copy(piece.at[:, WIDE : 2 * WIDE], do_s.at[row_at(k)], sems.at[slot + 1]),
            pltpu.make_async_copy(
                piece.at[:, 2 * WIDE : 2 * WIDE + HD], k_s.at[row_at(k, group * span)], sems.at[slot + 2]
            ),
            pltpu.make_async_copy(
                piece.at[:, 2 * WIDE + HD :], v_s.at[row_at(k, group * span)], sems.at[slot + 3]
            ),
        ]
    for copy in copies:
        copy.start()
    slot = 4 * KVH
    for step in range(1, groups):
        source = (group + groups - step) % groups
        for k in range(KVH):
            piece = earlier[(step - 1) * KVH + k]

            @pl.when(group >= step)
            def _(piece=piece, k=k, slot=slot, source=source):
                first = pltpu.make_async_copy(
                    piece.at[:, :HD], k_s.at[row_at(k, source * span)], sems.at[slot]
                )
                second = pltpu.make_async_copy(
                    piece.at[:, HD:], v_s.at[row_at(k, source * span)], sems.at[slot + 1]
                )
                first.start()
                second.start()
                first.wait()
                second.wait()

            slot += 2
    for copy in copies:
        copy.wait()

    dk_s[...] = jnp.zeros_like(dk_s)
    dv_s[...] = jnp.zeros_like(dv_s)
    scale = 1.0 / math.sqrt(HD)
    fold = scale * math.log2(math.e)

    for which in range(groups):

        @pl.when(group == which)
        def _(which=which):
            for block in range((which + 1) * span // TILE):
                keys = slice(block * TILE, (block + 1) * TILE)
                kt_s[:, keys] = k_s[keys, :].T

            def one_head(h, carry):
                columns = pl.ds(pl.multiple_of(h * HD, HD), HD)
                for part in range(span // TILE):
                    q = q_s[part * TILE : (part + 1) * TILE, columns]
                    do = do_s[part * TILE : (part + 1) * TILE, columns]
                    length = which * span + (part + 1) * TILE
                    blocks = length // TILE
                    scores = []
                    grads = []
                    for b in range(blocks):
                        keys = slice(b * TILE, (b + 1) * TILE)
                        one = lax.dot_general(k_s[keys, :], q, NT, preferred_element_type=F32)
                        if b == blocks - 1:
                            key_place = lax.broadcasted_iota(jnp.int32, (TILE, TILE), 0)
                            query_place = lax.broadcasted_iota(jnp.int32, (TILE, TILE), 1)
                            one = jnp.where(key_place <= query_place, one, NEGATIVE)
                        scores.append(one)
                        grads.append(
                            lax.dot_general(v_s[keys, :], do, NT, preferred_element_type=F32)
                        )
                    top = scores[0].max(axis=0, keepdims=True)
                    for one in scores[1:]:
                        top = jnp.maximum(top, one.max(axis=0, keepdims=True))
                    expon = [jnp.exp2((one - top) * fold) for one in scores]
                    denom = sum(e.sum(axis=0, keepdims=True) for e in expon)
                    weighted = sum(
                        (e * gp).sum(axis=0, keepdims=True) for e, gp in zip(expon, grads)
                    )
                    inverse = 1.0 / denom
                    delta = weighted * inverse
                    probs = jnp.concatenate([(e * inverse).astype(BF16) for e in expon], axis=0)
                    grad_scores = jnp.concatenate(
                        [
                            (e * (inverse * scale) * (gp - delta)).astype(BF16)
                            for e, gp in zip(expon, grads)
                        ],
                        axis=0,
                    )
                    dv_s[:length, :] += jnp.dot(probs, do, preferred_element_type=F32)
                    dk_s[:length, :] += jnp.dot(grad_scores, q, preferred_element_type=F32)
                    dqt = jnp.dot(kt_s[:, :length], grad_scores, preferred_element_type=F32)
                    dq_s[part * TILE : (part + 1) * TILE, columns] = dqt.T.astype(BF16)
                return carry

            lax.fori_loop(0, GROUP, one_head, 0)
            base = which * span
            own_out[:, :HD] = dk_s[base : base + span, :]
            own_out[:, HD:] = dv_s[base : base + span, :]
            for step in range(1, which + 1):
                source = (which - step) * span
                down_s[step - 1, :, :HD] = dk_s[source : source + span, :].astype(BF16)
                down_s[step - 1, :, HD:] = dv_s[source : source + span, :].astype(BF16)
            for step in range(which + 1, groups):
                down_s[step - 1] = jnp.zeros((span, 2 * HD), BF16)

    outs = [pltpu.make_async_copy(dq_s.at[row_at(k)], dq_out[k], sems.at[k]) for k in range(KVH)]
    outs += [
        pltpu.make_async_copy(down_s.at[step], down_out[step], sems.at[KVH + step])
        for step in range(groups - 1)
    ]
    for copy in outs:
        copy.start()
    for copy in outs:
        copy.wait()


def attention(rows, groups, queries, out_grad, key_states, value_states, pieces, earlier):
    span = KVH * rows
    length = groups * span
    any_spec = pl.BlockSpec(memory_space=pl.ANY)
    n_in = 4 + len(pieces) + len(earlier)
    out_shape = (
        [jax.ShapeDtypeStruct((rows, WIDE), BF16)] * KVH
        + [jax.ShapeDtypeStruct((span, 2 * HD), F32)]
        + [jax.ShapeDtypeStruct((span, 2 * HD), BF16)] * (groups - 1)
    )
    out_specs = (
        [any_spec] * KVH
        + [pl.BlockSpec(memory_space=pltpu.VMEM)]
        + [any_spec] * (groups - 1)
    )
    outs = pl.pallas_call(
        lambda *refs: attention_kernel(rows, groups, *refs),
        out_shape=out_shape,
        in_specs=[any_spec] * n_in,
        out_specs=out_specs,
        scratch_shapes=[
            pltpu.VMEM((span, WIDE), BF16),
            pltpu.VMEM((span, WIDE), BF16),
            pltpu.VMEM((length, HD), BF16),
            pltpu.VMEM((length, HD), BF16),
            pltpu.VMEM((HD, length), BF16),
            pltpu.VMEM((span, WIDE), BF16),
            pltpu.VMEM((length, HD), F32),
            pltpu.VMEM((length, HD), F32),
            pltpu.VMEM((max(groups - 1, 1), span, 2 * HD), BF16),
            pltpu.SemaphoreType.DMA((4 * KVH + 2 * KVH * groups,)),
        ],
        compiler_params=pltpu.CompilerParams(vmem_limit_bytes=VMEM_BYTES),
        cost_estimate=pl.CostEstimate(flops=10**10, bytes_accessed=5 * 10**7, transcendentals=0),
        name="attention",
    )(queries, out_grad, key_states, value_states, *pieces, *earlier)
    return outs[:KVH], outs[KVH], outs[KVH + 1 :]


def transpose_kernel(rows, blocks, slab, *refs):
    pieces = refs[:KVH]
    out = refs[KVH]
    x_s, sems = refs[KVH + 1 :]
    head = lax.axis_index("seq") % KVH
    span = KVH * rows
    copies = []
    for k in range(KVH):
        for core in range(2):
            copies.append(
                pltpu.make_async_copy(
                    pieces[k].at[core * rows : (core + 1) * rows],
                    x_s.at[pl.ds(pl.multiple_of(core * span + (head ^ k) * rows, rows), rows)],
                    sems.at[2 * k + core],
                )
            )
    for copy in copies:
        copy.start()
    for copy in copies:
        copy.wait()
    width = x_s.shape[1]
    for a in range(width // TILE):
        for b in range(2 * span // TILE):
            out[a * TILE : (a + 1) * TILE, b * TILE : (b + 1) * TILE] = x_s[
                b * TILE : (b + 1) * TILE, a * TILE : (a + 1) * TILE
            ].T


def transposed(rows, blocks, slab, pieces):
    width = pieces[0].shape[1]
    tokens = 2 * KVH * rows
    return pl.pallas_call(
        lambda *refs: transpose_kernel(rows, blocks, slab, *refs),
        out_shape=jax.ShapeDtypeStruct((width, tokens), BF16),
        in_specs=[pl.BlockSpec(memory_space=pl.ANY)] * KVH,
        out_specs=pl.BlockSpec(memory_space=pltpu.VMEM),
        scratch_shapes=[pltpu.VMEM((tokens, width), BF16), pltpu.SemaphoreType.DMA((2 * KVH,))],
        compiler_params=pltpu.CompilerParams(vmem_limit_bytes=VMEM_BYTES),
        cost_estimate=pl.CostEstimate(flops=0, bytes_accessed=10**7, transcendentals=0),
        name="input_transposed",
    )(*pieces)


def weight_kernel(rows, halves, groups, slab, *refs):
    span = KVH * rows
    own = refs[:KVH]
    other = refs[KVH : 2 * KVH]
    xt = refs[2 * KVH]
    keep, send, key_out, value_out = refs[2 * KVH + 1 : 2 * KVH + 5]
    g_s, sems = refs[2 * KVH + 5 :]
    place = lax.axis_index("seq")
    group = place // KVH
    head = place % KVH
    half = lax.axis_index("dp") // 2
    channels = KVH * HD
    copies = []
    slot = 0
    for k in range(KVH):
        for core, piece in ((0, own[k]), (1, other[k])):
            for kind in range(2):
                copies.append(
                    pltpu.make_async_copy(
                        piece.at[:, kind * HD : (kind + 1) * HD],
                        g_s.at[
                            core * span : (core + 1) * span,
                            pl.ds(pl.multiple_of(kind * channels + (head ^ k) * HD, HD), HD),
                        ],
                        sems.at[slot],
                    )
                )
                slot += 1
    for copy in copies:
        copy.start()
    for copy in copies:
        copy.wait()
    mine = pl.ds(pl.multiple_of(head * rows, rows), rows)
    key_out[...] = g_s[mine, :channels]
    value_out[...] = g_s[mine, channels:]
    for apart in range(halves):
        for step in range(groups):
            owner = ((half ^ apart) * groups + (group ^ step)) * slab
            left = xt[pl.ds(pl.multiple_of(owner, slab), slab), :]
            product = jnp.dot(left, g_s[...], preferred_element_type=F32)
            if apart == 0:
                keep[step * slab : (step + 1) * slab, :] = product
            else:
                first = ((apart - 1) * groups + step) * slab
                send[first : first + slab, :] = product.astype(BF16)


def weight_terms(rows, halves, groups, slab, own, other, xt):
    span = KVH * rows
    channels = 2 * KVH * HD
    vmem = pl.BlockSpec(memory_space=pltpu.VMEM)
    return pl.pallas_call(
        lambda *refs: weight_kernel(rows, halves, groups, slab, *refs),
        out_shape=[
            jax.ShapeDtypeStruct((groups * slab, channels), F32),
            jax.ShapeDtypeStruct((max(halves - 1, 1) * groups * slab, channels), BF16),
            jax.ShapeDtypeStruct((rows, channels // 2), BF16),
            jax.ShapeDtypeStruct((rows, channels // 2), BF16),
        ],
        in_specs=[pl.BlockSpec(memory_space=pl.ANY)] * (2 * KVH) + [vmem],
        out_specs=[vmem] * 4,
        scratch_shapes=[pltpu.VMEM((2 * span, channels), BF16), pltpu.SemaphoreType.DMA((4 * KVH,))],
        compiler_params=pltpu.CompilerParams(vmem_limit_bytes=VMEM_BYTES),
        cost_estimate=pl.CostEstimate(flops=3 * 10**9, bytes_accessed=10**7, transcendentals=0),
        name="weight_terms",
    )(*own, *other, xt)


def place_kernel(*refs):
    pieces = refs[:KVH]
    out, sems = refs[KVH:]
    head = lax.axis_index("seq") % KVH
    copies = [
        pltpu.make_async_copy(
            pieces[k],
            out.at[:, pl.ds(pl.multiple_of((head ^ k) * WIDE, WIDE), WIDE)],
            sems.at[k],
        )
        for k in range(KVH)
    ]
    for copy in copies:
        copy.start()
    for copy in copies:
        copy.wait()


def placed(rows, pieces):
    any_spec = pl.BlockSpec(memory_space=pl.ANY)
    return pl.pallas_call(
        place_kernel,
        out_shape=jax.ShapeDtypeStruct((rows, QH * HD), BF16),
        in_specs=[any_spec] * KVH,
        out_specs=any_spec,
        scratch_shapes=[pltpu.SemaphoreType.DMA((KVH,))],
        cost_estimate=pl.CostEstimate(flops=0, bytes_accessed=10**7, transcendentals=0),
        name="query_grad_placed",
    )(*pieces)


def local(layer_input, queries, key_states, value_states, out_grad):
    rows = layer_input.shape[0]
    cycle = lax.axis_size("seq")
    replicas = lax.axis_size("dp")
    groups = cycle // KVH
    halves = replicas // 2
    slab = D // (replicas * cycle)
    place = lax.axis_index("seq")
    head = place % KVH
    core = lax.axis_index("dp") % 2

    def swap(array, k):
        return lax.ppermute(array, "seq", [(i, i ^ k) for i in range(cycle)])

    def across_cores(array):
        return lax.ppermute(array, "dp", [(i, i ^ 1) for i in range(replicas)])

    def columns(array, index, width):
        return lax.dynamic_slice_in_dim(array, index * width, width, 1)

    kv_of = [
        jnp.concatenate(
            [columns(key_states, head ^ k, HD), columns(value_states, head ^ k, HD)], axis=1
        )
        for k in range(KVH)
    ]
    earlier = []
    for step in range(1, groups):
        for k in range(KVH):
            pairs = [
                (i, ((i // KVH) + step) * KVH + ((i % KVH) ^ k))
                for i in range(cycle - step * KVH)
            ]
            earlier.append(lax.ppermute(kv_of[k], "seq", pairs))
    pieces = [
        swap(
            jnp.concatenate(
                [columns(queries, head ^ k, WIDE), columns(out_grad, head ^ k, WIDE), kv_of[k]],
                axis=1,
            ),
            k,
        )
        for k in range(1, KVH)
    ]

    width = cycle * slab

    def of_core(array, which):
        return jnp.concatenate(
            [columns(array, 2 * half + which, width) for half in range(halves)], axis=1
        )

    mine = of_core(layer_input, core)
    given = across_cores(of_core(layer_input, 1 - core))

    def of_head(array, index):
        return jnp.concatenate(
            [columns(array, block * KVH + index, slab) for block in range(halves * groups)], axis=1
        )

    both = [
        jnp.concatenate([of_head(mine, head ^ k), of_head(given, head ^ k)], axis=0)
        for k in range(KVH)
    ]
    both, pieces = lax.optimization_barrier((both, pieces))
    inputs = [both[0]] + [swap(both[k], k) for k in range(1, KVH)]

    grads, own, down = attention(
        rows, groups, queries, out_grad, key_states, value_states, pieces, earlier
    )
    for step in range(1, groups):
        pairs = [(i + step * KVH, i) for i in range(cycle - step * KVH)]
        own = own + lax.ppermute(down[step - 1], "seq", pairs).astype(F32)
    summed = own.astype(BF16)

    gathered = [summed] + [swap(summed, k) for k in range(1, KVH)]
    others = [across_cores(piece) for piece in gathered]
    xt = transposed(rows, halves * groups, slab, inputs)
    keep, send, key_grad, value_grad = weight_terms(
        rows, halves, groups, slab, gathered, others, xt
    )
    query_grad = placed(rows, [grads[0]] + [swap(grads[k], k) for k in range(1, KVH)])

    size = groups * slab
    for apart in range(1, halves):
        part = send[(apart - 1) * size : apart * size]
        keep = keep + lax.ppermute(
            part, "dp", [(i, i ^ (2 * apart)) for i in range(replicas)]
        ).astype(F32)
    weight_grad = keep[:slab]
    for step in range(1, groups):
        part = keep[step * slab : (step + 1) * slab].astype(BF16)
        weight_grad = weight_grad + swap(part, step * KVH).astype(F32)
    return (query_grad, key_grad, value_grad, weight_grad)


def solution(mesh):
    spec = P(("dp", "seq"), None)
    return jax.shard_map(
        local, mesh=mesh, in_specs=(spec,) * 5, out_specs=(spec,) * 4, check_vma=False
    )
```

time: 390 us -> 200 us (0.51)
  waiting for transfers between devices: 282 us -> 90.3 us
  Pallas kernels: 0 us -> 50 us
  local copies, waits for them, and re-layouts: 34.5 us -> 8.88 us
  matrix products: 21.8 us -> 0 us
  between operations: 13.9 us -> 1.15 us
  starting transfers between devices: 31.2 us -> 38.7 us
  other arithmetic: 5.56 us -> 10.1 us
    reduce_scatter x2 -> x0, waiting for transfers between devices: 157 us -> none  [the longest x1 117 us: local(): lax.psum_scatter(terms, 'seq', scatter_dimension=0, tiled=True)]
    all_gather x3 -> x0, waiting for transfers between devices: 125 us -> none  [the longest x1 47.1 us: local(): summed_grads = lax.all_gather(owned_grads, 'seq', axis=0, tiled=True)]
    ppermute x0 -> x24, waiting for transfers between devices: none -> 90.3 us  [the longest x13 47.6 us: swap(): return lax.ppermute(array, 'seq', [(i, i ^ k) for i in range(cycle)])]
    pallas_call x0 -> x4, Pallas kernels: none -> 50 us  [the longest x1 32.9 us: placed(): pl.pallas_call(place_kernel, out_shape=jax.ShapeDtypeStruct((rows, QH * H...]
    ppermute x0 -> x24, starting transfers between devices: none -> 38.7 us  [the longest x13 24 us: swap(): return lax.ppermute(array, 'seq', [(i, i ^ k) for i in range(cycle)])]
    all_to_all x1 -> x0, starting transfers between devices: 30.8 us -> none  [local(): lax.all_to_all(layer_input.reshape(local_rows, replicas, cycle_size, slab...]
    dot_general x8 -> x0, matrix products: 21.8 us -> none  [the longest x1 6.57 us: local(): jnp.einsum('tr,tc->rc', columns, summed_grads, preferred_element_type=jnp...]
    unnamed x12 -> x46, local copies, waits for them, and re-layouts: 15.9 us -> 2.66 us
  transfers between devices with their start and end apart: 6 -> 24, of which waited for: 5 -> 11; matrix products, arithmetic and copies ran while one was open for 5% -> 6% of each run, Pallas kernels for 0% -> 22%
where the time goes in v1:
time: 200 us; the launch traced here: 199 us
  waiting for transfers between devices  90.3 us (45%)
  Pallas kernels  50 us (25%)
  starting transfers between devices  38.7 us (19%)
  other arithmetic  10.1 us (5%)
  local copies, waits for them, and re-layouts  8.88 us (4%)
    ppermute x13, waiting for transfers between devices, swap(): return lax.ppermute(array, 'seq', [(i, i ^ k) for i in range(cycle)])  47.6 us
    pallas_call x1, Pallas kernels, placed(): pl.pallas_call(place_kernel, out_shape=jax.ShapeDtypeStruct((rows, QH * H...  32.9 us
    ppermute x1, waiting for transfers between devices, local(): lax.ppermute(part, 'dp', [(i, i ^ 2 * apart) for i in range(replicas)])  24 us
    ppermute x13, starting transfers between devices, swap(): return lax.ppermute(array, 'seq', [(i, i ^ k) for i in range(cycle)])  24 us
    ppermute x1, waiting for transfers between devices, local(): own = own + lax.ppermute(down[step - 1], 'seq', pairs).astype(F32)  17.8 us
    ppermute x4, starting transfers between devices, local(): earlier.append(lax.ppermute(kv_of[k], 'seq', pairs))  11.9 us
    pallas_call x1, Pallas kernels, attention(): pl.pallas_call(lambda *refs: attention_kernel(rows, groups, *refs), out_s...  10.9 us
    dynamic_slice x4, local copies, waits for them, and re-layouts, columns(): return lax.dynamic_slice_in_dim(array, index * width, width, 1)  6.15 us
  transfers between devices with their start and end apart: 24, of which 11 were waited for; matrix products, arithmetic and copies ran while one was open for 6% of the time, Pallas kernels for 22%

profile of v1, /device:TPU:0, one launch (start us, length us, event | category | flops | bytes accessed | tf_op | source)
XLA Modules:
  0.0 199.2 jit_solution(9156656597197677094)
XLA Ops:
  0.7 1.5 constant_dynamic-slice_fusion
  2.8 6.9 %collective-permute-start.5 = (bf16[128,256]{1,0:T(8,128)(2,1)}, bf16[128,256]{1,0:T(8,128)(2,1)S(1)}, u32[]{:S(2)}, u32[]{:S(2)}) collective-permute-start(bf16[128,256]{1,0:T(8,128)(2,1)} %pad_maximum_fusion.5), channel_id=1, source_target_pairs={{0,5},{1,4},{2,7},{3,6},{8,13},{9,12},{10,15},{11,14},{16,21},{17,... | collective-permute-start | bytes 196616 | tf_op jit(solution)/shard_map/ppermute | solution.py:387
  9.7 1.5 constant_dynamic-slice_fusion.4
  12.8 1.6 collective-permute-start.2
  14.4 1.7 constant_dynamic-slice_fusion.32
  28.0 2.3 %collective-permute-start.7 = (bf16[128,256]{1,0:T(8,128)(2,1)S(1)}, bf16[128,256]{1,0:T(8,128)(2,1)S(1)}, u32[]{:S(2)}, u32[]{:S(2)}) collective-permute-start(bf16[128,256]{1,0:T(8,128)(2,1)S(1)} %copy-done.21), channel_id=1, source_target_pairs={{0,7},{1,6},{2,5},{3,4},{8,15},{9,14},{10,13},{11,12},{16,23},{17,... | collective-permute-start | bytes 196616 | tf_op jit(solution)/shard_map/ppermute | solution.py:387
  31.8 9.3 %collective-permute-done.3.refs_6_ = bf16[128,2304]{1,0:T(8,128)(2,1)S(1)} collective-permute-done((bf16[128,2304]{1,0:T(8,128)(2,1)}, bf16[128,2304]{1,0:T(8,128)(2,1)S(1)}, u32[]{:S(2)}, u32[]{:S(2)}) %collective-permute-start.3) | collective-permute-done | bytes 589856 | tf_op jit(solution)/shard_map/ppermute | solution.py:366
  41.1 1.5 collective-permute-start.19
  43.5 10.9 %attention.1 = (bf16[128,1024]{1,0:T(8,128)(2,1)S(1)}, bf16[128,1024]{1,0:T(8,128)(2,1)S(1)}, bf16[128,1024]{1,0:T(8,128)(2,1)S(1)}, bf16[128,1024]{1,0:T(8,128)...) custom-call(bf16[128,4096]{1,0:T(8,128)(2,1)S(1)} %copy-done.1, bf16[128,4096]{1,0:T(8,128)(2,1)S(1)} %copy-done.2, ...), custom_call_target="tpu_custom_call" | custom-call | flops 10000000000 | bytes 50000000 | tf_op jit(solution)/shard_map/attention/pallas_call | solution.py:188
  55.7 1.6 collective-permute-start.20
  57.3 1.4 collective-permute-start.21
  58.7 17.8 %collective-permute-done.11 = bf16[512,256]{1,0:T(8,128)(2,1)S(1)} collective-permute-done((bf16[512,256]{1,0:T(8,128)(2,1)S(1)}, bf16[512,256]{1,0:T(8,128)(2,1)S(1)}, u32[]{:S(2)}, u32[]{:S(2)}) %collective-permute-start.11) | collective-permute-done | bytes 262176 | tf_op jit(solution)/shard_map/ppermute | solution.py:426
  76.7 2.4 %collective-permute-start.13 = (bf16[512,256]{1,0:T(8,128)(2,1)S(1)}, bf16[512,256]{1,0:T(8,128)(2,1)S(1)}, u32[]{:S(2)}, u32[]{:S(2)}) collective-permute-start(bf16[512,256]{1,0:T(8,128)(2,1)S(1)} %add_convert_fusion.refs_0_), channel_id=1, source_target_pairs={{0,2},{1,3},{2,0},{3,1},{4,6},{5,7},{6,4},{7,5},{8,10},{9,11},{10,... | collective-permute-start | bytes 786440 | tf_op jit(solution)/shard_map/ppermute | solution.py:366
  80.1 13.9 %collective-permute-done.14.refs_3_ = bf16[512,256]{1,0:T(8,128)(2,1)S(1)} collective-permute-done((bf16[512,256]{1,0:T(8,128)(2,1)S(1)}, bf16[512,256]{1,0:T(8,128)(2,1)S(1)}, u32[]{:S(2)}, u32[]{:S(2)}) %collective-permute-start.14) | collective-permute-done | bytes 262176 | tf_op jit(solution)/shard_map/ppermute | solution.py:366
  94.1 2.0 %collective-permute-done.13.refs_2_ = bf16[512,256]{1,0:T(8,128)(2,1)S(1)} collective-permute-done((bf16[512,256]{1,0:T(8,128)(2,1)S(1)}, bf16[512,256]{1,0:T(8,128)(2,1)S(1)}, u32[]{:S(2)}, u32[]{:S(2)}) %collective-permute-start.13) | collective-permute-done | bytes 262176 | tf_op jit(solution)/shard_map/ppermute | solution.py:366
  99.2 5.3 %weight_terms.1 = (f32[512,1024]{1,0:T(8,128)S(1)}, bf16[512,1024]{1,0:T(8,128)(2,1)S(1)}, bf16[128,512]{1,0:T(8,128)(2,1)}, bf16[128,512]{1,0:T(8,128)(2,1)}) custom-call(bf16[512,256]{1,0:T(8,128)(2,1)S(1)} %add_convert_fusion.refs_0_, bf16[512,256]{1,0:T(8,128)(2,1)S(1)} %collective-permute-done.12.refs_1_, ...), custom_call_target="tpu_custom_call" | custom-call | flops 3000000000 | bytes 10000000 | tf_op jit(solution)/shard_map/weight_terms/pallas_call | solution.py:306
  104.6 1.6 collective-permute-start.22
  106.2 24.0 %collective-permute-done.22 = bf16[512,1024]{1,0:T(8,128)(2,1)S(1)} collective-permute-done((bf16[512,1024]{1,0:T(8,128)(2,1)S(1)}, bf16[512,1024]{1,0:T(8,128)(2,1)S(1)}, u32[]{:S(2)}, u32[]{:S(2)}) %collective-permute-start.22) | collective-permute-done | bytes 1048608 | tf_op jit(solution)/shard_map/ppermute | solution.py:440
  130.6 8.8 %collective-permute-start.23 = (bf16[256,1024]{1,0:T(8,128)(2,1)S(1)}, bf16[256,1024]{1,0:T(8,128)(2,1)S(1)}, u32[]{:S(2)}, u32[]{:S(2)}) collective-permute-start(bf16[256,1024]{1,0:T(8,128)(2,1)S(1)} %slice.13), channel_id=1, source_target_pairs={{0,4},{1,5},{2,6},{3,7},{4,0},{5,1},{6,2},{7,3},{8,12},{9,13},{10,... | collective-permute-start | bytes 1572872 | tf_op jit(solution)/shard_map/ppermute | solution.py:366
  139.9 2.9 %collective-permute-start.10 = (bf16[128,1024]{1,0:T(8,128)(2,1)S(1)}, bf16[128,1024]{1,0:T(8,128)(2,1)S(1)}, u32[]{:S(2)}, u32[]{:S(2)}) collective-permute-start(bf16[128,1024]{1,0:T(8,128)(2,1)S(1)} %get-tuple-element.27), channel_id=1, source_target_pairs={{0,3},{1,2},{2,1},{3,0},{4,7},{5,6},{6,5},{7,4},{8,11},{9,10},{10,... | collective-permute-start | bytes 786440 | tf_op jit(solution)/shard_map/ppermute | solution.py:366
  142.9 4.8 %collective-permute-done.8.refs_1_ = bf16[128,1024]{1,0:T(8,128)(2,1)S(1)} collective-permute-done((bf16[128,1024]{1,0:T(8,128)(2,1)S(1)}, bf16[128,1024]{1,0:T(8,128)(2,1)S(1)}, u32[]{:S(2)}, u32[]{:S(2)}) %collective-permute-start.8) | collective-permute-done | bytes 262176 | tf_op jit(solution)/shard_map/ppermute | solution.py:366
  147.7 9.7 %collective-permute-done.9.refs_2_ = bf16[128,1024]{1,0:T(8,128)(2,1)S(1)} collective-permute-done((bf16[128,1024]{1,0:T(8,128)(2,1)S(1)}, bf16[128,1024]{1,0:T(8,128)(2,1)S(1)}, u32[]{:S(2)}, u32[]{:S(2)}) %collective-permute-start.9) | collective-permute-done | bytes 262176 | tf_op jit(solution)/shard_map/ppermute | solution.py:366
  157.4 7.0 %collective-permute-done.10.refs_3_ = bf16[128,1024]{1,0:T(8,128)(2,1)S(1)} collective-permute-done((bf16[128,1024]{1,0:T(8,128)(2,1)S(1)}, bf16[128,1024]{1,0:T(8,128)(2,1)S(1)}, u32[]{:S(2)}, u32[]{:S(2)}) %collective-permute-start.10) | collective-permute-done | bytes 262176 | tf_op jit(solution)/shard_map/ppermute | solution.py:366
  165.1 32.9 %query_grad_placed.1 = bf16[128,4096]{1,0:T(8,128)(2,1)} custom-call(bf16[128,1024]{1,0:T(8,128)(2,1)} %copy-done.3, bf16[128,1024]{1,0:T(8,128)(2,1)} %copy-done.18, bf16[128,1024]{1,0:T(8,128)(2,1)} %copy-done.19, bf16[128,1024]{1,0:T(8,128)(2,1)} %copy-done.20), custom_call_target="tpu_custom_call" | custom-call | bytes 10000000 | tf_op jit(solution)/shard_map/query_grad_placed/pallas_call | solution.py:343
  (95 shorter events, 24.5 us)
Async XLA Ops:
  2.8 39.8 %collective-permute-start.5 = (bf16[128,256]{1,0:T(8,128)(2,1)}, bf16[128,256]{1,0:T(8,128)(2,1)S(1)}, u32[]{:S(2)}, u32[]{:S(2)}) collective-permute-start(bf16[128,256]{1,0:T(8,128)(2,1)} %pad_maximum_fusion.5), channel_id=1, source_target_pairs={{0,5},{1,4},{2,7},{3,6},{8,13},{9,12},{10,15},{11,14},{16,21},{17,... | collective-permute-start | bytes 196616 | tf_op jit(solution)/shard_map/ppermute | solution.py:387
  11.3 16.1 %collective-permute-start.1 = (bf16[128,2304]{1,0:T(8,128)(2,1)S(1)}, bf16[128,2304]{1,0:T(8,128)(2,1)S(1)}, u32[]{:S(2)}, u32[]{:S(2)}) collective-permute-start(bf16[128,2304]{1,0:T(8,128)(2,1)S(1)} %pad_maximum_fusion.1), channel_id=1, source_target_pairs={{0,1},{1,0},{2,3},{3,2},{4,5},{5,4},{6,7},{7,6},{8,9},{9,8},{10,11... | collective-permute-start | bytes 1769480 | tf_op jit(solution)/shard_map/ppermute | solution.py:366
  12.8 17.6 %collective-permute-start.2 = (bf16[128,2304]{1,0:T(8,128)(2,1)}, bf16[128,2304]{1,0:T(8,128)(2,1)S(1)}, u32[]{:S(2)}, u32[]{:S(2)}) collective-permute-start(bf16[128,2304]{1,0:T(8,128)(2,1)} %pad_maximum_fusion.2), channel_id=1, source_target_pairs={{0,2},{1,3},{2,0},{3,1},{4,6},{5,7},{6,4},{7,5},{8,10},{9,11},{10,... | collective-permute-start | bytes 1769480 | tf_op jit(solution)/shard_map/ppermute | solution.py:366
  17.1 7.2 %collective-permute-start = (bf16[128,4096]{1,0:T(8,128)(2,1)}, bf16[128,4096]{1,0:T(8,128)(2,1)}, u32[]{:S(2)}, u32[]{:S(2)}) collective-permute-start(bf16[128,4096]{1,0:T(8,128)(2,1)} %pad_maximum_fusion), channel_id=1, source_target_pairs={{0,8},{8,0},{16,24},{24,16},{1,9},{9,1},{17,25},{25,17},{2,10},{10... | collective-permute-start | bytes 3145736 | tf_op jit(solution)/shard_map/ppermute | solution.py:369
  18.0 23.1 %collective-permute-start.3 = (bf16[128,2304]{1,0:T(8,128)(2,1)}, bf16[128,2304]{1,0:T(8,128)(2,1)S(1)}, u32[]{:S(2)}, u32[]{:S(2)}) collective-permute-start(bf16[128,2304]{1,0:T(8,128)(2,1)} %pad_maximum_fusion.3), channel_id=1, source_target_pairs={{0,3},{1,2},{2,1},{3,0},{4,7},{5,6},{6,5},{7,4},{8,11},{9,10},{10,... | collective-permute-start | bytes 1769480 | tf_op jit(solution)/shard_map/ppermute | solution.py:366
  24.4 18.3 %collective-permute-start.6 = (bf16[128,256]{1,0:T(8,128)(2,1)S(1)}, bf16[128,256]{1,0:T(8,128)(2,1)S(1)}, u32[]{:S(2)}, u32[]{:S(2)}) collective-permute-start(bf16[128,256]{1,0:T(8,128)(2,1)S(1)} %copy-done.22), channel_id=1, source_target_pairs={{0,6},{1,7},{2,4},{3,5},{8,14},{9,15},{10,12},{11,13},{16,22},{17,... | collective-permute-start | bytes 196616 | tf_op jit(solution)/shard_map/ppermute | solution.py:387
  28.0 14.8 %collective-permute-start.7 = (bf16[128,256]{1,0:T(8,128)(2,1)S(1)}, bf16[128,256]{1,0:T(8,128)(2,1)S(1)}, u32[]{:S(2)}, u32[]{:S(2)}) collective-permute-start(bf16[128,256]{1,0:T(8,128)(2,1)S(1)} %copy-done.21), channel_id=1, source_target_pairs={{0,7},{1,6},{2,5},{3,4},{8,15},{9,14},{10,13},{11,12},{16,23},{17,... | collective-permute-start | bytes 196616 | tf_op jit(solution)/shard_map/ppermute | solution.py:387
  30.4 13.1 %collective-permute-start.4 = (bf16[128,256]{1,0:T(8,128)(2,1)S(1)}, bf16[128,256]{1,0:T(8,128)(2,1)S(1)}, u32[]{:S(2)}, u32[]{:S(2)}) collective-permute-start(bf16[128,256]{1,0:T(8,128)(2,1)S(1)} %pad_maximum_fusion.4), channel_id=1, source_target_pairs={{0,4},{1,5},{2,6},{3,7},{8,12},{9,13},{10,14},{11,15},{16,20},{17,... | collective-permute-start | bytes 196616 | tf_op jit(solution)/shard_map/ppermute | solution.py:387
  41.1 38.0 %collective-permute-start.19 = (bf16[256,1024]{1,0:T(8,128)(2,1)S(1)}, bf16[256,1024]{1,0:T(8,128)(2,1)S(1)}, u32[]{:S(2)}, u32[]{:S(2)}) collective-permute-start(bf16[256,1024]{1,0:T(8,128)(2,1)S(1)} %get-tuple-element.31), channel_id=1, source_target_pairs={{0,1},{1,0},{2,3},{3,2},{4,5},{5,4},{6,7},{7,6},{8,9},{9,8},{10,11... | collective-permute-start | bytes 1572872 | tf_op jit(solution)/shard_map/ppermute | solution.py:366
  54.4 22.1 %collective-permute-start.11 = (bf16[512,256]{1,0:T(8,128)(2,1)S(1)}, bf16[512,256]{1,0:T(8,128)(2,1)S(1)}, u32[]{:S(2)}, u32[]{:S(2)}) collective-permute-start(bf16[512,256]{1,0:T(8,128)(2,1)S(1)} %get-tuple-element.29), channel_id=1, source_target_pairs={{4,0},{5,1},{6,2},{7,3},{12,8},{13,9},{14,10},{15,11},{20,16},{21,... | collective-permute-start | bytes 786440 | tf_op jit(solution)/shard_map/ppermute | solution.py:426
  55.7 24.5 %collective-permute-start.20 = (bf16[256,1024]{1,0:T(8,128)(2,1)S(1)}, bf16[256,1024]{1,0:T(8,128)(2,1)S(1)}, u32[]{:S(2)}, u32[]{:S(2)}) collective-permute-start(bf16[256,1024]{1,0:T(8,128)(2,1)S(1)} %get-tuple-element.32), channel_id=1, source_target_pairs={{0,2},{1,3},{2,0},{3,1},{4,6},{5,7},{6,4},{7,5},{8,10},{9,11},{10,... | collective-permute-start | bytes 1572872 | tf_op jit(solution)/shard_map/ppermute | solution.py:366
  57.3 39.7 %collective-permute-start.21 = (bf16[256,1024]{1,0:T(8,128)(2,1)S(1)}, bf16[256,1024]{1,0:T(8,128)(2,1)S(1)}, u32[]{:S(2)}, u32[]{:S(2)}) collective-permute-start(bf16[256,1024]{1,0:T(8,128)(2,1)S(1)} %get-tuple-element.33), channel_id=1, source_target_pairs={{0,3},{1,2},{2,1},{3,0},{4,7},{5,6},{6,5},{7,4},{8,11},{9,10},{10,... | collective-permute-start | bytes 1572872 | tf_op jit(solution)/shard_map/ppermute | solution.py:366
  76.6 17.5 %collective-permute-start.14 = (bf16[512,256]{1,0:T(8,128)(2,1)S(1)}, bf16[512,256]{1,0:T(8,128)(2,1)S(1)}, u32[]{:S(2)}, u32[]{:S(2)}) collective-permute-start(bf16[512,256]{1,0:T(8,128)(2,1)S(1)} %add_convert_fusion.refs_0_), channel_id=1, source_target_pairs={{0,3},{1,2},{2,1},{3,0},{4,7},{5,6},{6,5},{7,4},{8,11},{9,10},{10,... | collective-permute-start | bytes 786440 | tf_op jit(solution)/shard_map/ppermute | solution.py:366
  76.7 19.4 %collective-permute-start.13 = (bf16[512,256]{1,0:T(8,128)(2,1)S(1)}, bf16[512,256]{1,0:T(8,128)(2,1)S(1)}, u32[]{:S(2)}, u32[]{:S(2)}) collective-permute-start(bf16[512,256]{1,0:T(8,128)(2,1)S(1)} %add_convert_fusion.refs_0_), channel_id=1, source_target_pairs={{0,2},{1,3},{2,0},{3,1},{4,6},{5,7},{6,4},{7,5},{8,10},{9,11},{10,... | collective-permute-start | bytes 786440 | tf_op jit(solution)/shard_map/ppermute | solution.py:366
  79.1 17.9 %collective-permute-start.12 = (bf16[512,256]{1,0:T(8,128)(2,1)S(1)}, bf16[512,256]{1,0:T(8,128)(2,1)S(1)}, u32[]{:S(2)}, u32[]{:S(2)}) collective-permute-start(bf16[512,256]{1,0:T(8,128)(2,1)S(1)} %add_convert_fusion.refs_0_), channel_id=1, source_target_pairs={{0,1},{1,0},{2,3},{3,2},{4,5},{5,4},{6,7},{7,6},{8,9},{9,8},{10,11... | collective-permute-start | bytes 786440 | tf_op jit(solution)/shard_map/ppermute | solution.py:366
  80.1 19.1 %collective-permute-start.15 = (bf16[512,256]{1,0:T(8,128)(2,1)S(1)}, bf16[512,256]{1,0:T(8,128)(2,1)S(1)}, u32[]{:S(2)}, u32[]{:S(2)}) collective-permute-start(bf16[512,256]{1,0:T(8,128)(2,1)S(1)} %add_convert_fusion.refs_0_), channel_id=1, source_target_pairs={{0,8},{8,0},{16,24},{24,16},{1,9},{9,1},{17,25},{25,17},{2,10},{10... | collective-permute-start | bytes 786440 | tf_op jit(solution)/shard_map/ppermute | solution.py:369
  94.1 5.1 %collective-permute-start.18 = (bf16[512,256]{1,0:T(8,128)(2,1)S(1)}, bf16[512,256]{1,0:T(8,128)(2,1)S(1)}, u32[]{:S(2)}, u32[]{:S(2)}) collective-permute-start(bf16[512,256]{1,0:T(8,128)(2,1)S(1)} %collective-permute-done.14.refs_3_), channel_id=1, source_target_pairs={{0,8},{8,0},{16,24},{24,16},{1,9},{9,1},{17,25},{25,17},{2,10},{10... | collective-permute-start | bytes 786440 | tf_op jit(solution)/shard_map/ppermute | solution.py:369
  96.1 3.1 %collective-permute-start.17 = (bf16[512,256]{1,0:T(8,128)(2,1)S(1)}, bf16[512,256]{1,0:T(8,128)(2,1)S(1)}, u32[]{:S(2)}, u32[]{:S(2)}) collective-permute-start(bf16[512,256]{1,0:T(8,128)(2,1)S(1)} %collective-permute-done.13.refs_2_), channel_id=1, source_target_pairs={{0,8},{8,0},{16,24},{24,16},{1,9},{9,1},{17,25},{25,17},{2,10},{10... | collective-permute-start | bytes 786440 | tf_op jit(solution)/shard_map/ppermute | solution.py:369
  96.9 2.3 %collective-permute-start.16 = (bf16[512,256]{1,0:T(8,128)(2,1)S(1)}, bf16[512,256]{1,0:T(8,128)(2,1)S(1)}, u32[]{:S(2)}, u32[]{:S(2)}) collective-permute-start(bf16[512,256]{1,0:T(8,128)(2,1)S(1)} %collective-permute-done.12.refs_1_), channel_id=1, source_target_pairs={{0,8},{8,0},{16,24},{24,16},{1,9},{9,1},{17,25},{25,17},{2,10},{10... | collective-permute-start | bytes 786440 | tf_op jit(solution)/shard_map/ppermute | solution.py:369
  104.6 25.6 %collective-permute-start.22 = (bf16[512,1024]{1,0:T(8,128)(2,1)S(1)}, bf16[512,1024]{1,0:T(8,128)(2,1)S(1)}, u32[]{:S(2)}, u32[]{:S(2)}) collective-permute-start(bf16[512,1024]{1,0:T(8,128)(2,1)S(1)} %get-tuple-element.37), channel_id=1, source_target_pairs={{0,16},{8,24},{16,0},{24,8},{1,17},{9,25},{17,1},{25,9},{2,18},{10... | collective-permute-start | bytes 3145736 | tf_op jit(solution)/shard_map/ppermute | solution.py:440
  130.6 67.5 %collective-permute-start.23 = (bf16[256,1024]{1,0:T(8,128)(2,1)S(1)}, bf16[256,1024]{1,0:T(8,128)(2,1)S(1)}, u32[]{:S(2)}, u32[]{:S(2)}) collective-permute-start(bf16[256,1024]{1,0:T(8,128)(2,1)S(1)} %slice.13), channel_id=1, source_target_pairs={{0,4},{1,5},{2,6},{3,7},{4,0},{5,1},{6,2},{7,3},{8,12},{9,13},{10,... | collective-permute-start | bytes 1572872 | tf_op jit(solution)/shard_map/ppermute | solution.py:366
  139.4 8.3 %collective-permute-start.8 = (bf16[128,1024]{1,0:T(8,128)(2,1)S(1)}, bf16[128,1024]{1,0:T(8,128)(2,1)S(1)}, u32[]{:S(2)}, u32[]{:S(2)}) collective-permute-start(bf16[128,1024]{1,0:T(8,128)(2,1)S(1)} %get-tuple-element.25), channel_id=1, source_target_pairs={{0,1},{1,0},{2,3},{3,2},{4,5},{5,4},{6,7},{7,6},{8,9},{9,8},{10,11... | collective-permute-start | bytes 786440 | tf_op jit(solution)/shard_map/ppermute | solution.py:366
  139.9 17.5 %collective-permute-start.9 = (bf16[128,1024]{1,0:T(8,128)(2,1)S(1)}, bf16[128,1024]{1,0:T(8,128)(2,1)S(1)}, u32[]{:S(2)}, u32[]{:S(2)}) collective-permute-start(bf16[128,1024]{1,0:T(8,128)(2,1)S(1)} %get-tuple-element.26), channel_id=1, source_target_pairs={{0,2},{1,3},{2,0},{3,1},{4,6},{5,7},{6,4},{7,5},{8,10},{9,11},{10,... | collective-permute-start | bytes 786440 | tf_op jit(solution)/shard_map/ppermute | solution.py:366
  139.9 24.5 %collective-permute-start.10 = (bf16[128,1024]{1,0:T(8,128)(2,1)S(1)}, bf16[128,1024]{1,0:T(8,128)(2,1)S(1)}, u32[]{:S(2)}, u32[]{:S(2)}) collective-permute-start(bf16[128,1024]{1,0:T(8,128)(2,1)S(1)} %get-tuple-element.27), channel_id=1, source_target_pairs={{0,3},{1,2},{2,1},{3,0},{4,7},{5,6},{6,5},{7,4},{8,11},{9,10},{10,... | collective-permute-start | bytes 786440 | tf_op jit(solution)/shard_map/ppermute | solution.py:366
  (23 other events, 205.7 us)

commit v2 on v1

v2 whole, which is shorter than its diff:
```python
import math

import jax
import jax.numpy as jnp
from jax import lax
from jax.experimental import pallas as pl
from jax.experimental.pallas import tpu as pltpu
from jax.sharding import PartitionSpec as P

D = 8192
QH = 32
KVH = 4
HD = 128
GROUP = QH // KVH
WIDE = GROUP * HD
TILE = 256
NEGATIVE = -1e30
BF16 = jnp.bfloat16
F32 = jnp.float32
VMEM_BYTES = 48 * 1024 * 1024

NT = (((1,), (1,)), ((), ()))


def pack_kernel(rows, groups, slabs, slab, *refs):
    in_kernel = slab % HD == 0
    q_hbm, do_hbm, k_hbm, v_hbm = refs[:4]
    at = 4
    if in_kernel:
        x_hbm = refs[at]
        at += 1
    kv_out = refs[at]
    piece_out = refs[at + 1 : at + KVH]
    at += KVH
    if in_kernel:
        x_out = refs[at : at + KVH]
        at += KVH
        x_s = refs[at]
        at += 1
    kv_s, piece_s, sems, x_sems, out_sems = refs[at:]
    head = lax.axis_index("seq") % KVH

    def of(k, block, base=0):
        return pl.ds(pl.multiple_of(base + (head ^ k) * block, block), block)

    small = []
    large = []
    wide = []
    for k in range(KVH):
        small.append(
            [
                pltpu.make_async_copy(
                    array.at[:, k * HD : (k + 1) * HD],
                    kv_s.at[group * KVH + k, :, kind * HD : (kind + 1) * HD],
                    sems.at[(group * KVH + k) * 2 + kind],
                )
                for group in range(groups)
                for kind, array in enumerate((k_hbm, v_hbm))
            ]
        )
    base = 2 * KVH * groups
    for k in range(1, KVH):
        large.append(
            [
                pltpu.make_async_copy(
                    array.at[:, of(k, WIDE)],
                    piece_s.at[k - 1, :, kind * WIDE : (kind + 1) * WIDE],
                    sems.at[base + 2 * k + kind],
                )
                for kind, array in enumerate((q_hbm, do_hbm))
            ]
        )
    if in_kernel:
        for k in range(KVH):
            wide.append(
                [
                    pltpu.make_async_copy(
                        x_hbm.at[:, of(k, slab, block * KVH * slab)],
                        x_s.at[k, :, block * slab : (block + 1) * slab],
                        x_sems.at[k * slabs + block],
                    )
                    for block in range(slabs)
                ]
            )
    for copies in small + large + wide:
        for copy in copies:
            copy.start()
    outs = []

    def pass_on(copies, source, target):
        for copy in copies:
            copy.wait()
        outs.append(pltpu.make_async_copy(source, target, out_sems.at[len(outs)]))
        outs[-1].start()

    pass_on([copy for copies in small for copy in copies], kv_s, kv_out)
    for k in range(1, KVH):
        pass_on(large[k - 1], piece_s.at[k - 1], piece_out[k - 1])
    for k, copies in enumerate(wide):
        pass_on(copies, x_s.at[k], x_out[k])
    for copy in outs:
        copy.wait()


def packed(rows, groups, slabs, slab, queries, out_grad, key_states, value_states, layer_input):
    any_spec = pl.BlockSpec(memory_space=pl.ANY)
    cycle = KVH * groups
    in_kernel = slab % HD == 0
    wide = KVH if in_kernel else 0
    inputs = (queries, out_grad, key_states, value_states) + ((layer_input,) if in_kernel else ())
    outs = pl.pallas_call(
        lambda *refs: pack_kernel(rows, groups, slabs, slab, *refs),
        out_shape=[jax.ShapeDtypeStruct((cycle, rows, 2 * HD), BF16)]
        + [jax.ShapeDtypeStruct((rows, 2 * WIDE), BF16)] * (KVH - 1)
        + [jax.ShapeDtypeStruct((rows, slabs * slab), BF16)] * wide,
        in_specs=[any_spec] * len(inputs),
        out_specs=[any_spec] * (KVH + wide),
        scratch_shapes=([pltpu.VMEM((KVH, rows, slabs * slab), BF16)] if in_kernel else [])
        + [
            pltpu.VMEM((cycle, rows, 2 * HD), BF16),
            pltpu.VMEM((KVH - 1, rows, 2 * WIDE), BF16),
            pltpu.SemaphoreType.DMA((2 * cycle + 2 * KVH,)),
            pltpu.SemaphoreType.DMA((KVH * slabs,)),
            pltpu.SemaphoreType.DMA((2 * KVH,)),
        ],
        compiler_params=pltpu.CompilerParams(vmem_limit_bytes=VMEM_BYTES),
        cost_estimate=pl.CostEstimate(flops=0, bytes_accessed=8 * 10**6, transcendentals=0),
        name="first_sends",
    )(*inputs)
    if in_kernel:
        columns = outs[KVH:]
    else:
        head = lax.axis_index("seq") % KVH
        columns = [
            jnp.concatenate(
                [
                    lax.dynamic_slice_in_dim(
                        layer_input, (block * KVH + (head ^ k)) * slab, slab, 1
                    )
                    for block in range(slabs)
                ],
                axis=1,
            )
            for k in range(KVH)
        ]
    return outs[0], outs[1:KVH], columns


def attention_kernel(rows, groups, *refs):
    span = KVH * rows
    q_hbm, do_hbm, kv_hbm = refs[:3]
    pieces = refs[3 : 3 + KVH - 1]
    at = 3 + KVH - 1
    dq_out = refs[at]
    at += 1
    own_k, own_v = refs[at : at + 2]
    at += 2
    down_out = refs[at : at + 2 * (groups - 1)]
    at += 2 * (groups - 1)
    q_s, do_s, k_s, v_s, kt_s, dk_s, dv_s, down_s, sems = refs[at:]

    place = lax.axis_index("seq")
    group = place // KVH
    head = place % KVH

    def row_at(k, base=0):
        return pl.ds(pl.multiple_of(base + (head ^ k) * rows, rows), rows)

    def column_at(block):
        return pl.ds(pl.multiple_of(head * block, block), block)

    copies = [
        pltpu.make_async_copy(q_hbm.at[:, column_at(WIDE)], q_s.at[row_at(0)], sems.at[0]),
        pltpu.make_async_copy(do_hbm.at[:, column_at(WIDE)], do_s.at[row_at(0)], sems.at[1]),
    ]
    for kind, target in enumerate((k_s, v_s)):
        copies += [
            pltpu.make_async_copy(
                kv_hbm.at[source, :, kind * HD : (kind + 1) * HD],
                target.at[source * rows : (source + 1) * rows],
                sems.at[2 * KVH + 2 * source + kind],
            )
            for source in range(KVH * groups)
        ]
    for k in range(1, KVH):
        piece = pieces[k - 1]
        copies += [
            pltpu.make_async_copy(piece.at[:, :WIDE], q_s.at[row_at(k)], sems.at[2 * k]),
            pltpu.make_async_copy(piece.at[:, WIDE:], do_s.at[row_at(k)], sems.at[2 * k + 1]),
        ]
    for copy in copies:
        copy.start()
    for copy in copies:
        copy.wait()

    dk_s[...] = jnp.zeros_like(dk_s)
    dv_s[...] = jnp.zeros_like(dv_s)
    scale = 1.0 / math.sqrt(HD)
    fold = scale * math.log2(math.e)

    for which in range(groups):

        @pl.when(group == which)
        def _(which=which):
            for block in range((which + 1) * span // TILE):
                keys = slice(block * TILE, (block + 1) * TILE)
                kt_s[:, keys] = k_s[keys, :].T

            def one_head(h, carry):
                columns = pl.ds(pl.multiple_of(h * HD, HD), HD)
                for part in range(span // TILE):
                    q = q_s[part * TILE : (part + 1) * TILE, columns]
                    do = do_s[part * TILE : (part + 1) * TILE, columns]
                    length = which * span + (part + 1) * TILE
                    blocks = length // TILE
                    scores = []
                    grads = []
                    for b in range(blocks):
                        keys = slice(b * TILE, (b + 1) * TILE)
                        one = lax.dot_general(k_s[keys, :], q, NT, preferred_element_type=F32)
                        if b == blocks - 1:
                            key_place = lax.broadcasted_iota(jnp.int32, (TILE, TILE), 0)
                            query_place = lax.broadcasted_iota(jnp.int32, (TILE, TILE), 1)
                            one = jnp.where(key_place <= query_place, one, NEGATIVE)
                        scores.append(one)
                        grads.append(
                            lax.dot_general(v_s[keys, :], do, NT, preferred_element_type=F32)
                        )
                    top = scores[0].max(axis=0, keepdims=True)
                    for one in scores[1:]:
                        top = jnp.maximum(top, one.max(axis=0, keepdims=True))
                    expon = [jnp.exp2((one - top) * fold) for one in scores]
                    denom = sum(e.sum(axis=0, keepdims=True) for e in expon)
                    weighted = sum(
                        (e * gp).sum(axis=0, keepdims=True) for e, gp in zip(expon, grads)
                    )
                    inverse = 1.0 / denom
                    delta = weighted * inverse
                    probs = jnp.concatenate([(e * inverse).astype(BF16) for e in expon], axis=0)
                    grad_scores = jnp.concatenate(
                        [
                            (e * (inverse * scale) * (gp - delta)).astype(BF16)
                            for e, gp in zip(expon, grads)
                        ],
                        axis=0,
                    )
                    dv_s[:length, :] += jnp.dot(probs, do, preferred_element_type=F32)
                    dk_s[:length, :] += jnp.dot(grad_scores, q, preferred_element_type=F32)
                    dqt = jnp.dot(kt_s[:, :length], grad_scores, preferred_element_type=F32)
                    dq_out[part * TILE : (part + 1) * TILE, columns] = dqt.T.astype(BF16)
                return carry

            lax.fori_loop(0, GROUP, one_head, 0)
            base = which * span
            own_k[...] = dk_s[base : base + span, :]
            own_v[...] = dv_s[base : base + span, :]
            for step in range(1, which + 1):
                source = (which - step) * span
                down_s[2 * step - 2] = dk_s[source : source + span, :].astype(BF16)
                down_s[2 * step - 1] = dv_s[source : source + span, :].astype(BF16)
            for step in range(which + 1, groups):
                down_s[2 * step - 2] = jnp.zeros((span, HD), BF16)
                down_s[2 * step - 1] = jnp.zeros((span, HD), BF16)

    outs = [
        pltpu.make_async_copy(down_s.at[step], down_out[step], sems.at[step])
        for step in range(2 * (groups - 1))
    ]
    for copy in outs:
        copy.start()
    for copy in outs:
        copy.wait()


def attention(rows, groups, queries, out_grad, keys_values, pieces):
    span = KVH * rows
    length = groups * span
    any_spec = pl.BlockSpec(memory_space=pl.ANY)
    n_in = 3 + len(pieces)
    out_shape = (
        [jax.ShapeDtypeStruct((span, WIDE), BF16)]
        + [jax.ShapeDtypeStruct((span, HD), F32)] * 2
        + [jax.ShapeDtypeStruct((span, HD), BF16)] * (2 * (groups - 1))
    )
    out_specs = (
        [pl.BlockSpec(memory_space=pltpu.VMEM)] * 3
        + [any_spec] * (2 * (groups - 1))
    )
    outs = pl.pallas_call(
        lambda *refs: attention_kernel(rows, groups, *refs),
        out_shape=out_shape,
        in_specs=[any_spec] * n_in,
        out_specs=out_specs,
        scratch_shapes=[
            pltpu.VMEM((span, WIDE), BF16),
            pltpu.VMEM((span, WIDE), BF16),
            pltpu.VMEM((length, HD), BF16),
            pltpu.VMEM((length, HD), BF16),
            pltpu.VMEM((HD, length), BF16),
            pltpu.VMEM((length, HD), F32),
            pltpu.VMEM((length, HD), F32),
            pltpu.VMEM((2 * max(groups - 1, 1), span, HD), BF16),
            pltpu.SemaphoreType.DMA((2 * KVH + 2 * KVH * groups,)),
        ],
        compiler_params=pltpu.CompilerParams(vmem_limit_bytes=VMEM_BYTES),
        cost_estimate=pl.CostEstimate(flops=10**10, bytes_accessed=5 * 10**7, transcendentals=0),
        name="attention",
    )(queries, out_grad, keys_values, *pieces)
    down = outs[3:]
    return outs[0], outs[1:3], (down[0::2], down[1::2])


def transpose_kernel(rows, halves, width, *refs):
    pieces = refs[:KVH]
    outs = refs[KVH : KVH + 2]
    x_s, sems = refs[KVH + 2 :]
    head = lax.axis_index("seq") % KVH
    core = lax.axis_index("dp") % 2
    copies = [
        pltpu.make_async_copy(
            pieces[k],
            x_s.at[pl.ds(pl.multiple_of((head ^ k) * rows, rows), rows)],
            sems.at[k],
        )
        for k in range(KVH)
    ]
    for copy in copies:
        copy.start()
    for copy in copies:
        copy.wait()
    tile = min(TILE, width)
    for which, out in enumerate(outs):
        for half in range(halves):
            for a in range(width // tile):
                first = (2 * half + (core ^ which)) * width + a * tile
                columns = pl.ds(pl.multiple_of(first, tile), tile)
                out[half * width + a * tile : half * width + (a + 1) * tile, :] = x_s[:, columns].T


def transposed(rows, halves, width, pieces):
    tokens = KVH * rows
    vmem = pl.BlockSpec(memory_space=pltpu.VMEM)
    return pl.pallas_call(
        lambda *refs: transpose_kernel(rows, halves, width, *refs),
        out_shape=[jax.ShapeDtypeStruct((halves * width, tokens), BF16)] * 2,
        in_specs=[pl.BlockSpec(memory_space=pl.ANY)] * KVH,
        out_specs=[vmem] * 2,
        scratch_shapes=[
            pltpu.VMEM((tokens, 2 * halves * width), BF16),
            pltpu.SemaphoreType.DMA((KVH,)),
        ],
        compiler_params=pltpu.CompilerParams(vmem_limit_bytes=VMEM_BYTES),
        cost_estimate=pl.CostEstimate(flops=0, bytes_accessed=10**7, transcendentals=0),
        name="input_transposed",
    )(*pieces)


def weight_kernel(rows, halves, groups, slab, joins, *refs):
    own, other, xt, xt_other = refs[:4]
    at = 4
    if joins:
        before = refs[at]
        at += 1
    keep = refs[at]
    send = refs[at + 1 : at + 1 + groups]
    mine_out, g_s = refs[at + 1 + groups :]
    span = KVH * rows
    width = KVH * HD
    if joins:
        send[0][:, width:] = before[...]
    place = lax.axis_index("seq")
    group = place // KVH
    head = place % KVH
    half = lax.axis_index("dp") // 2
    for source in range(KVH):
        columns = slice(source * HD, (source + 1) * HD)
        g_s[:span, columns] = own[source]
        g_s[span:, columns] = other[source]
        mine_out[:, columns] = own[source, pl.ds(pl.multiple_of(head * rows, rows), rows), :]
    for apart in range(halves):
        for step in range(groups):
            owner = ((half ^ apart) * groups + (group ^ step)) * slab
            at = pl.ds(pl.multiple_of(owner, slab), slab)
            product = jnp.dot(xt[at, :], g_s[:span, :], preferred_element_type=F32) + jnp.dot(
                xt_other[at, :], g_s[span:, :], preferred_element_type=F32
            )
            if apart == 0:
                keep[step * slab : (step + 1) * slab, :] = product
            else:
                send[step][(apart - 1) * slab : apart * slab, :width] = product.astype(BF16)


def weight_terms(rows, halves, groups, slab, own, other, xt, xt_other, before=None):
    span = KVH * rows
    channels = KVH * HD
    vmem = pl.BlockSpec(memory_space=pltpu.VMEM)
    joins = before is not None
    more = [before] if joins else []
    outs = pl.pallas_call(
        lambda *refs: weight_kernel(rows, halves, groups, slab, joins, *refs),
        out_shape=[jax.ShapeDtypeStruct((groups * slab, channels), F32)]
        + [
            jax.ShapeDtypeStruct(
                (max(halves - 1, 1) * slab, channels * (1 + (joins and step == 0))), BF16
            )
            for step in range(groups)
        ]
        + [jax.ShapeDtypeStruct((rows, channels), BF16)],
        in_specs=[vmem] * (4 + joins),
        out_specs=[vmem] * (groups + 2),
        scratch_shapes=[pltpu.VMEM((2 * span, channels), BF16)],
        compiler_params=pltpu.CompilerParams(vmem_limit_bytes=VMEM_BYTES),
        cost_estimate=pl.CostEstimate(flops=15 * 10**8, bytes_accessed=6 * 10**6, transcendentals=0),
        name="weight_terms",
    )(own, other, xt, xt_other, *more)
    return outs[0], outs[1 : 1 + groups], outs[1 + groups]


def place_kernel(pieces, out):
    for head in range(KVH):
        out[:, head * WIDE : (head + 1) * WIDE] = pieces[head]


def placed(rows, pieces):
    vmem = pl.BlockSpec(memory_space=pltpu.VMEM)
    return pl.pallas_call(
        place_kernel,
        out_shape=jax.ShapeDtypeStruct((rows, QH * HD), BF16),
        in_specs=[vmem],
        out_specs=vmem,
        compiler_params=pltpu.CompilerParams(vmem_limit_bytes=VMEM_BYTES),
        cost_estimate=pl.CostEstimate(flops=0, bytes_accessed=5 * 10**6, transcendentals=0),
        name="query_grad_placed",
    )(pieces)


def join_kernel(wide, *refs):
    keep = refs[:2]
    both = refs[2 : 2 + wide]
    out = refs[-1]
    rest = refs[2 + wide : -1]
    count = len(rest) // 2
    slab, width = out.shape[0], out.shape[1] // 2
    for kind in range(2):
        at = slice(kind * width, (kind + 1) * width)
        total = keep[kind][:slab, :]
        for ref in both:
            total = total + ref[:, at].astype(F32)
        for ref in rest[kind * count : (kind + 1) * count]:
            total = total + ref[...].astype(F32)
        out[:, at] = total


def joined(slab, keep, both, rest):
    vmem = pl.BlockSpec(memory_space=pltpu.VMEM)
    return pl.pallas_call(
        lambda *refs: join_kernel(len(both), *refs),
        out_shape=jax.ShapeDtypeStruct((slab, 2 * keep[0].shape[1]), F32),
        in_specs=[vmem] * (2 + len(both) + len(rest)),
        out_specs=vmem,
        compiler_params=pltpu.CompilerParams(vmem_limit_bytes=VMEM_BYTES),
        cost_estimate=pl.CostEstimate(flops=0, bytes_accessed=3 * 10**6, transcendentals=0),
        name="weight_grad_joined",
    )(*keep, *both, *rest)


def local(layer_input, queries, key_states, value_states, out_grad):
    rows = layer_input.shape[0]
    cycle = lax.axis_size("seq")
    replicas = lax.axis_size("dp")
    groups = cycle // KVH
    halves = replicas // 2
    slab = D // (replicas * cycle)
    after = lax.optimization_barrier
    within = [[i + k for k in range(KVH)] for i in range(0, cycle, KVH)]

    def swap(array, k):
        return lax.ppermute(array, "seq", [(i, i ^ k) for i in range(cycle)])

    def across_cores(array):
        return lax.ppermute(array, "dp", [(i, i ^ 1) for i in range(replicas)])

    def exchange(array, parts=None):
        return lax.all_to_all(
            array, "seq", split_axis=0, concat_axis=0, tiled=True, axis_index_groups=parts
        )

    keys_values, sends, columns = packed(
        rows,
        groups,
        replicas * groups,
        slab,
        queries,
        out_grad,
        key_states,
        value_states,
        layer_input,
    )
    keys_values = exchange(keys_values)
    pieces = [swap(sends[k - 1], k) for k in range(1, KVH)]

    columns, pieces = after((columns, pieces))
    inputs = [columns[0]] + [swap(columns[k], k) for k in range(1, KVH - 1)]

    grads, own, down = attention(rows, groups, queries, out_grad, keys_values, pieces)
    last, inputs, down = after((columns[KVH - 1], inputs, down))
    inputs.append(swap(last, KVH - 1))

    gathered = [None, None]
    others = [None, None]
    for kind in (1, 0):
        total = own[kind]
        for step in range(1, groups):
            pairs = [(i + step * KVH, i) for i in range(cycle - step * KVH)]
            total = total + lax.ppermute(down[kind][step - 1], "seq", pairs).astype(F32)
        copies = jnp.broadcast_to(total.astype(BF16)[None], (KVH,) + total.shape)
        gathered[kind] = exchange(copies, within)
        others[kind] = across_cores(gathered[kind])
    xt, xt_give = transposed(rows, halves, groups * slab, inputs)
    xt_other = across_cores(xt_give)

    narrow = [None, None]
    keep = [None, None]
    send = [None, None]
    keep[1], send[1], narrow[1] = weight_terms(
        rows, halves, groups, slab, gathered[1], others[1], xt, xt_other
    )
    keep[0], send[0], narrow[0] = weight_terms(
        rows, halves, groups, slab, gathered[0], others[0], xt, xt_other, send[1][0]
    )

    def over_sequences(array):
        return [
            lax.ppermute(
                array[(apart - 1) * slab : apart * slab],
                "dp",
                [(i, i ^ (2 * apart)) for i in range(replicas)],
            )
            for apart in range(1, halves)
        ]

    received = []
    for kind in (0, 1):
        for step in range(1, groups):
            total = keep[kind][step * slab : (step + 1) * slab]
            for part in over_sequences(send[kind][step]):
                total = total + part.astype(F32)
            received.append(swap(total.astype(BF16), step * KVH))
    weight_grad = joined(slab, keep, over_sequences(send[0][0]), received)

    grads, _ = after((grads, gathered))
    returned = exchange(grads.reshape(KVH, rows, WIDE), within)
    query_grad = placed(rows, returned)
    return (query_grad, narrow[0], narrow[1], weight_grad)


def solution(mesh):
    spec = P(("dp", "seq"), None)
    return jax.shard_map(
        local, mesh=mesh, in_specs=(spec,) * 5, out_specs=(spec,) * 4, check_vma=False
    )
```

time: 200 us -> 168 us (0.84)
  Pallas kernels: 50 us -> 26.7 us
  other arithmetic: 10.1 us -> 0.19 us
  local copies, waits for them, and re-layouts: 8.88 us -> 16.1 us
  waiting for transfers between devices: 90.3 us -> 84.9 us
    pallas_call x1, Pallas kernels: 32.9 us -> 1.04 us  [placed(): pl.pallas_call(place_kernel, out_shape=jax.ShapeDtypeStruct((rows, QH * H...]
    all_to_all x0 -> x4, starting transfers between devices: none -> 24.8 us  [exchange(): lax.all_to_all(array, 'seq', split_axis=0, concat_axis=0, tiled=True, axi...]
    ppermute x13 -> x8, starting transfers between devices: 24 us -> 7.34 us  [swap(): return lax.ppermute(array, 'seq', [(i, i ^ k) for i in range(cycle)])]
    unnamed x46 -> x40, local copies, waits for them, and re-layouts: 2.66 us -> 14.4 us
    ppermute x6 -> x5, waiting for transfers between devices: 42.7 us -> 32.4 us  [the longest x2 21.4 us: local(): total = total + lax.ppermute(down[kind][step - 1], 'seq', pairs).astype(F32)]
    concatenate x13 -> x0, other arithmetic: 8.62 us -> none  [the longest x4 3.57 us: local(): jnp.concatenate([columns(key_states, head ^ k, HD), columns(value_states,...]
    ppermute x6 -> x5, starting transfers between devices: 14.8 us -> 6.24 us  [the longest x3 3.54 us: over_sequences(): lax.ppermute(array[(apart - 1) * slab:apart * slab], 'dp', [(i, i ^ 2 * a...]
    pallas_call x2 -> x5, Pallas kernels: 6.2 us -> 13.5 us  [the longest x2 6.6 us: weight_terms(): pl.pallas_call(lambda *refs: weight_kernel(rows, halves, groups, slab, jo...]
  transfers between devices with their start and end apart: 24 -> 20, of which waited for: 11 -> 11; matrix products, arithmetic and copies ran while one was open for 6% -> 1% of each run, Pallas kernels for 22% -> 14%
where the time goes in v2:
time: 168 us
  waiting for transfers between devices  84.9 us (51%)
  starting transfers between devices  38.9 us (23%)
  Pallas kernels  26.7 us (16%)
  local copies, waits for them, and re-layouts  16.1 us (10%)
    ppermute x8, waiting for transfers between devices, swap(): return lax.ppermute(array, 'seq', [(i, i ^ k) for i in range(cycle)])  48.8 us
    all_to_all x4, starting transfers between devices, exchange(): lax.all_to_all(array, 'seq', split_axis=0, concat_axis=0, tiled=True, axi...  24.8 us
    ppermute x2, waiting for transfers between devices, local(): total = total + lax.ppermute(down[kind][step - 1], 'seq', pairs).astype(F32)  21.4 us
    unnamed x40, local copies, waits for them, and re-layouts  14.4 us
    pallas_call x1, Pallas kernels, attention(): pl.pallas_call(lambda *refs: attention_kernel(rows, groups, *refs), out_s...  12.1 us
    ppermute x3, waiting for transfers between devices, over_sequences(): lax.ppermute(array[(apart - 1) * slab:apart * slab], 'dp', [(i, i ^ 2 * a...  11 us
    ppermute x8, starting transfers between devices, swap(): return lax.ppermute(array, 'seq', [(i, i ^ k) for i in range(cycle)])  7.34 us
    pallas_call x2, Pallas kernels, weight_terms(): pl.pallas_call(lambda *refs: weight_kernel(rows, halves, groups, slab, jo...  6.6 us
  transfers between devices with their start and end apart: 20, of which 11 were waited for; matrix products, arithmetic and copies ran while one was open for 1% of the time, Pallas kernels for 14%

profile of v2, /device:TPU:0, one launch (start us, length us, event | category | flops | bytes accessed | tf_op | source)
XLA Modules:
  0.0 167.6 jit_solution(9560507302591895522)
XLA Ops:
  3.7 3.0 %first_sends.1 = (bf16[8,128,256]{2,1,0:T(8,128)(2,1)}, bf16[128,2048]{1,0:T(8,128)(2,1)S(1)}, bf16[128,2048]{1,0:T(8,128)(2,1)S(1)}, bf16[128,2048]{1,0:T(8,128...) custom-call(bf16[128,4096]{1,0:T(8,128)(2,1)S(1)} %copy-done, ...), custom_call_target="tpu_custom_call" | custom-call | bytes 8000000 | tf_op jit(solution)/shard_map/first_sends/pallas_call | solution.py:111
  11.5 7.3 %all-to-all-start = ((bf16[8,128,256]{2,1,0:T(8,128)(2,1)}), bf16[8,128,256]{2,1,0:T(8,128)(2,1)S(1)}, u32[]{:S(2)}, u32[]{:S(2)}) async-start(bf16[8,128,256]{2,1,0:T(8,128)(2,1)} %get-tuple-element.41), calls=%async_computation | async-start | bytes 1048576 | tf_op jit(solution)/shard_map/all_to_all | solution.py:484
  18.8 2.0 %collective-permute-start = (bf16[128,2048]{1,0:T(8,128)(2,1)}, bf16[128,2048]{1,0:T(8,128)(2,1)S(1)}, u32[]{:S(2)}, u32[]{:S(2)}) collective-permute-start(bf16[128,2048]{1,0:T(8,128)(2,1)} %copy-done.19), channel_id=1, source_target_pairs={{0,1},{1,0},{2,3},{3,2},{4,5},{5,4},{6,7},{7,6},{8,9},{9,8},{10,11... | collective-permute-start | bytes 1572872 | tf_op jit(solution)/shard_map/ppermute | solution.py:478
  20.8 1.5 collective-permute-start.1
  22.3 15.7 %collective-permute-done.refs_3_ = bf16[128,2048]{1,0:T(8,128)(2,1)S(1)} collective-permute-done((bf16[128,2048]{1,0:T(8,128)(2,1)}, bf16[128,2048]{1,0:T(8,128)(2,1)S(1)}, u32[]{:S(2)}, u32[]{:S(2)}) %collective-permute-start) | collective-permute-done | bytes 524320 | tf_op jit(solution)/shard_map/ppermute | solution.py:478
  38.8 3.4 %collective-permute-done.1.refs_4_ = bf16[128,2048]{1,0:T(8,128)(2,1)S(1)} collective-permute-done((bf16[128,2048]{1,0:T(8,128)(2,1)}, bf16[128,2048]{1,0:T(8,128)(2,1)S(1)}, u32[]{:S(2)}, u32[]{:S(2)}) %collective-permute-start.1) | collective-permute-done | bytes 524320 | tf_op jit(solution)/shard_map/ppermute | solution.py:478
  43.0 10.0 %collective-permute-done.2.refs_5_ = bf16[128,2048]{1,0:T(8,128)(2,1)S(1)} collective-permute-done((bf16[128,2048]{1,0:T(8,128)(2,1)}, bf16[128,2048]{1,0:T(8,128)(2,1)S(1)}, u32[]{:S(2)}, u32[]{:S(2)}) %collective-permute-start.2) | collective-permute-done | bytes 524320 | tf_op jit(solution)/shard_map/ppermute | solution.py:478
  57.7 12.1 %attention.1 = (bf16[512,1024]{1,0:T(8,128)(2,1)}, f32[512,128]{1,0:T(8,128)S(1)}, f32[512,128]{1,0:T(8,128)S(1)}, bf16[512,128]{1,0:T(8,128)(2,1)S(1)}, bf16[512,128]{1,0:T(8,128)(2,1)S(1)}) custom-call(bf16[128,4096]{1,0:T(8,128)(2,1)S(1)} %copy-done.1, bf16[128,4096]{1,0:T(8,128)(2,1)S(1)} %copy-done.2, bf16[8,128,256]{2,1,0:T(8,128)(2,1)S(1)} %all-to-all-done.refs_2_, ...), custom_call_target="tpu_custom_call" | custom-call | flops 10000000000 | bytes 50000000 | tf_op jit(solution)/shard_map/attention/pallas_call | solution.py:289
  71.3 14.8 %collective-permute-done.6 = bf16[512,128]{1,0:T(8,128)(2,1)S(1)} collective-permute-done((bf16[512,128]{1,0:T(8,128)(2,1)S(1)}, bf16[512,128]{1,0:T(8,128)(2,1)S(1)}, u32[]{:S(2)}, u32[]{:S(2)}) %collective-permute-start.6) | collective-permute-done | bytes 131104 | tf_op jit(solution)/shard_map/ppermute | solution.py:515
  87.0 3.5 %all-to-all-start.2 = ((bf16[4,512,128]{2,1,0:T(8,128)(2,1)}), bf16[4,512,128]{2,1,0:T(8,128)(2,1)S(1)}, u32[]{:S(2)}, u32[]{:S(2)}) async-start(bf16[4,512,128]{2,1,0:T(8,128)(2,1)} %broadcast_in_dim.5), calls=%async_computation.2 | async-start | bytes 1048576 | tf_op jit(solution)/shard_map/all_to_all | solution.py:484
  90.5 2.9 %collective-permute-start.8 = (bf16[128,2048]{1,0:T(8,128)(2,1)S(1)}, bf16[128,2048]{1,0:T(8,128)(2,1)S(1)}, u32[]{:S(2)}, u32[]{:S(2)}) collective-permute-start(bf16[128,2048]{1,0:T(8,128)(2,1)S(1)} %copy-done.8), channel_id=1, source_target_pairs={{0,3},{1,2},{2,1},{3,0},{4,7},{5,6},{6,5},{7,4},{8,11},{9,10},{10,... | collective-permute-start | bytes 1572872 | tf_op jit(solution)/shard_map/ppermute | solution.py:478
  94.7 6.6 %collective-permute-done.5 = bf16[512,128]{1,0:T(8,128)(2,1)S(1)} collective-permute-done((bf16[512,128]{1,0:T(8,128)(2,1)S(1)}, bf16[512,128]{1,0:T(8,128)(2,1)S(1)}, u32[]{:S(2)}, u32[]{:S(2)}) %collective-permute-start.5) | collective-permute-done | bytes 131104 | tf_op jit(solution)/shard_map/ppermute | solution.py:515
  103.6 10.6 %all-to-all-start.1 = ((bf16[4,512,128]{2,1,0:T(8,128)(2,1)}), bf16[4,512,128]{2,1,0:T(8,128)(2,1)S(1)}, u32[]{:S(2)}, u32[]{:S(2)}) async-start(bf16[4,512,128]{2,1,0:T(8,128)(2,1)} %broadcast_in_dim.4), calls=%async_computation.1 | async-start | bytes 1048576 | tf_op jit(solution)/shard_map/all_to_all | solution.py:484
  114.2 2.8 %input_transposed.1 = (bf16[1024,512]{1,0:T(8,128)(2,1)S(1)}, bf16[1024,512]{1,0:T(8,128)(2,1)}) custom-call(bf16[128,2048]{1,0:T(8,128)(2,1)S(1)} %get-tuple-element.64.refs_0_, bf16[128,2048]{1,0:T(8,128)(2,1)} %collective-permute-done.3.refs_1_, bf16[128,2048]{1,0:T(8,128)(2,1)} %collective-permute-done.4.refs_2_, ...), custom_call_target="tpu_custom_call" | custom-call | bytes 10000000 | tf_op jit(solution)/shard_map/input_transposed/pallas_call | solution.py:343
  118.5 2.2 %all-to-all-done.1.refs_0_ = bf16[4,512,128]{2,1,0:T(8,128)(2,1)S(1)} async-done(((bf16[4,512,128]{2,1,0:T(8,128)(2,1)}), bf16[4,512,128]{2,1,0:T(8,128)(2,1)S(1)}, u32[]{:S(2)}, u32[]{:S(2)}) %all-to-all-start.1) | async-done | bytes 524320 | tf_op jit(solution)/shard_map/all_to_all | solution.py:484
  120.7 3.5 %all-to-all-start.3 = ((bf16[4,128,1024]{2,1,0:T(8,128)(2,1)}), bf16[4,128,1024]{2,1,0:T(8,128)(2,1)S(1)}, u32[]{:S(2)}, u32[]{:S(2)}) async-start(bf16[4,128,1024]{2,1,0:T(8,128)(2,1)} %bitcast), calls=%async_computation.3 | async-start | bytes 2097152 | tf_op jit(solution)/shard_map/all_to_all | solution.py:484
  124.3 3.3 %weight_terms.2 = (f32[512,512]{1,0:T(8,128)S(1)}, bf16[256,512]{1,0:T(8,128)(2,1)S(1)}, bf16[256,512]{1,0:T(8,128)(2,1)S(1)}, bf16[128,512]{1,0:T(8,128)(2,1)}) custom-call(bf16[4,512,128]{2,1,0:T(8,128)(2,1)S(1)} %all-to-all-done.2.refs_0_, bf16[4,512,128]{2,1,0:T(8,128)(2,1)} %collective-permute-done.10.refs_1_, bf16[1024,512]{1,0:T(8,128)(2,1)S(1)} %copy-done.6, ...), custom_call_target="tpu_custom_call" | custom-call | flops 1500000000 | bytes 6000000 | tf_op jit(solution)/shard_map/weight_terms/pallas_call | solution.py:399
  127.6 3.3 %weight_terms.3 = (f32[512,512]{1,0:T(8,128)S(1)}, bf16[256,1024]{1,0:T(8,128)(2,1)S(1)}, bf16[256,512]{1,0:T(8,128)(2,1)S(1)}, bf16[128,512]{1,0:T(8,128)(2,1)}) custom-call(bf16[4,512,128]{2,1,0:T(8,128)(2,1)S(1)} %all-to-all-done.1.refs_0_, bf16[4,512,128]{2,1,0:T(8,128)(2,1)} %collective-permute-done.7.refs_1_, bf16[1024,512]{1,0:T(8,128)(2,1)S(1)} %copy-done.6, ...), custom_call_target="tpu_custom_call" | custom-call | flops 1500000000 | bytes 6000000 | tf_op jit(solution)/shard_map/weight_terms/pallas_call | solution.py:399
  130.9 1.5 collective-permute-start.12
  132.9 1.5 collective-permute-start.11
  134.4 5.6 %collective-permute-done.12 = bf16[256,512]{1,0:T(8,128)(2,1)S(1)} collective-permute-done((bf16[256,512]{1,0:T(8,128)(2,1)S(1)}, bf16[256,512]{1,0:T(8,128)(2,1)S(1)}, u32[]{:S(2)}, u32[]{:S(2)}) %collective-permute-start.12) | collective-permute-done | bytes 262176 | tf_op jit(solution)/shard_map/ppermute | solution.py:534
  140.1 5.5 %collective-permute-done.14 = bf16[256,512]{1,0:T(8,128)(2,1)S(1)} collective-permute-done((bf16[256,512]{1,0:T(8,128)(2,1)S(1)}, bf16[256,512]{1,0:T(8,128)(2,1)S(1)}, u32[]{:S(2)}, u32[]{:S(2)}) %collective-permute-start.14) | collective-permute-done | bytes 262176 | tf_op jit(solution)/shard_map/ppermute | solution.py:534
  145.8 15.0 %collective-permute-done.13.refs_3_ = bf16[256,512]{1,0:T(8,128)(2,1)S(1)} collective-permute-done((bf16[256,512]{1,0:T(8,128)(2,1)S(1)}, bf16[256,512]{1,0:T(8,128)(2,1)S(1)}, u32[]{:S(2)}, u32[]{:S(2)}) %collective-permute-start.13) | collective-permute-done | bytes 262176 | tf_op jit(solution)/shard_map/ppermute | solution.py:478
  160.8 4.7 %collective-permute-done.15.refs_4_ = bf16[256,512]{1,0:T(8,128)(2,1)S(1)} collective-permute-done((bf16[256,512]{1,0:T(8,128)(2,1)S(1)}, bf16[256,512]{1,0:T(8,128)(2,1)S(1)}, u32[]{:S(2)}, u32[]{:S(2)}) %collective-permute-start.15) | collective-permute-done | bytes 262176 | tf_op jit(solution)/shard_map/ppermute | solution.py:478
  (69 shorter events, 24.7 us)
Async XLA Ops:
  3.7 50.9 %copy-start.1 = (bf16[128,4096]{1,0:T(8,128)(2,1)S(1)}, bf16[128,4096]{1,0:T(8,128)(2,1)}, u32[]{:S(2)}) copy-start(bf16[128,4096]{1,0:T(8,128)(2,1)} %refs_0_.3) | copy-start | bytes 3145732
  3.7 50.9 %copy-start.2 = (bf16[128,4096]{1,0:T(8,128)(2,1)S(1)}, bf16[128,4096]{1,0:T(8,128)(2,1)}, u32[]{:S(2)}) copy-start(bf16[128,4096]{1,0:T(8,128)(2,1)} %refs_1_.3) | copy-start | bytes 3145732
  11.5 43.1 %all-to-all-start = ((bf16[8,128,256]{2,1,0:T(8,128)(2,1)}), bf16[8,128,256]{2,1,0:T(8,128)(2,1)S(1)}, u32[]{:S(2)}, u32[]{:S(2)}) async-start(bf16[8,128,256]{2,1,0:T(8,128)(2,1)} %get-tuple-element.41), calls=%async_computation | async-start | bytes 1048576 | tf_op jit(solution)/shard_map/all_to_all | solution.py:484
  18.8 19.2 %collective-permute-start = (bf16[128,2048]{1,0:T(8,128)(2,1)}, bf16[128,2048]{1,0:T(8,128)(2,1)S(1)}, u32[]{:S(2)}, u32[]{:S(2)}) collective-permute-start(bf16[128,2048]{1,0:T(8,128)(2,1)} %copy-done.19), channel_id=1, source_target_pairs={{0,1},{1,0},{2,3},{3,2},{4,5},{5,4},{6,7},{7,6},{8,9},{9,8},{10,11... | collective-permute-start | bytes 1572872 | tf_op jit(solution)/shard_map/ppermute | solution.py:478
  20.8 21.4 %collective-permute-start.1 = (bf16[128,2048]{1,0:T(8,128)(2,1)}, bf16[128,2048]{1,0:T(8,128)(2,1)S(1)}, u32[]{:S(2)}, u32[]{:S(2)}) collective-permute-start(bf16[128,2048]{1,0:T(8,128)(2,1)} %copy-done.18), channel_id=1, source_target_pairs={{0,2},{1,3},{2,0},{3,1},{4,6},{5,7},{6,4},{7,5},{8,10},{9,11},{10,... | collective-permute-start | bytes 1572872 | tf_op jit(solution)/shard_map/ppermute | solution.py:478
  22.3 30.7 %collective-permute-start.2 = (bf16[128,2048]{1,0:T(8,128)(2,1)}, bf16[128,2048]{1,0:T(8,128)(2,1)S(1)}, u32[]{:S(2)}, u32[]{:S(2)}) collective-permute-start(bf16[128,2048]{1,0:T(8,128)(2,1)} %copy-done.17), channel_id=1, source_target_pairs={{0,3},{1,2},{2,1},{3,0},{4,7},{5,6},{6,5},{7,4},{8,11},{9,10},{10,... | collective-permute-start | bytes 1572872 | tf_op jit(solution)/shard_map/ppermute | solution.py:478
  53.8 16.0 %collective-permute-start.3 = (bf16[128,2048]{1,0:T(8,128)(2,1)}, bf16[128,2048]{1,0:T(8,128)(2,1)}, u32[]{:S(2)}, u32[]{:S(2)}) collective-permute-start(bf16[128,2048]{1,0:T(8,128)(2,1)} %copy-done.10), channel_id=1, source_target_pairs={{0,1},{1,0},{2,3},{3,2},{4,5},{5,4},{6,7},{7,6},{8,9},{9,8},{10,11... | collective-permute-start | bytes 1572872 | tf_op jit(solution)/shard_map/ppermute | solution.py:478
  54.3 15.5 %collective-permute-start.4 = (bf16[128,2048]{1,0:T(8,128)(2,1)}, bf16[128,2048]{1,0:T(8,128)(2,1)}, u32[]{:S(2)}, u32[]{:S(2)}) collective-permute-start(bf16[128,2048]{1,0:T(8,128)(2,1)} %copy-done.9), channel_id=1, source_target_pairs={{0,2},{1,3},{2,0},{3,1},{4,6},{5,7},{6,4},{7,5},{8,10},{9,11},{10,... | collective-permute-start | bytes 1572872 | tf_op jit(solution)/shard_map/ppermute | solution.py:478
  69.8 20.7 %copy-start.8 = (bf16[128,2048]{1,0:T(8,128)(2,1)S(1)}, bf16[128,2048]{1,0:T(8,128)(2,1)}, u32[]{:S(2)}) copy-start(bf16[128,2048]{1,0:T(8,128)(2,1)} %copy-done.7) | copy-start | bytes 1572868
  69.9 16.3 %collective-permute-start.6 = (bf16[512,128]{1,0:T(8,128)(2,1)S(1)}, bf16[512,128]{1,0:T(8,128)(2,1)S(1)}, u32[]{:S(2)}, u32[]{:S(2)}) collective-permute-start(bf16[512,128]{1,0:T(8,128)(2,1)S(1)} %get-tuple-element.62), channel_id=1, source_target_pairs={{4,0},{5,1},{6,2},{7,3},{12,8},{13,9},{14,10},{15,11},{20,16},{21,... | collective-permute-start | bytes 393224 | tf_op jit(solution)/shard_map/ppermute | solution.py:515
  87.0 15.7 %all-to-all-start.2 = ((bf16[4,512,128]{2,1,0:T(8,128)(2,1)}), bf16[4,512,128]{2,1,0:T(8,128)(2,1)S(1)}, u32[]{:S(2)}, u32[]{:S(2)}) async-start(bf16[4,512,128]{2,1,0:T(8,128)(2,1)} %broadcast_in_dim.5), calls=%async_computation.2 | async-start | bytes 1048576 | tf_op jit(solution)/shard_map/all_to_all | solution.py:484
  90.5 23.6 %collective-permute-start.8 = (bf16[128,2048]{1,0:T(8,128)(2,1)S(1)}, bf16[128,2048]{1,0:T(8,128)(2,1)S(1)}, u32[]{:S(2)}, u32[]{:S(2)}) collective-permute-start(bf16[128,2048]{1,0:T(8,128)(2,1)S(1)} %copy-done.8), channel_id=1, source_target_pairs={{0,3},{1,2},{2,1},{3,0},{4,7},{5,6},{6,5},{7,4},{8,11},{9,10},{10,... | collective-permute-start | bytes 1572872 | tf_op jit(solution)/shard_map/ppermute | solution.py:478
  93.4 7.8 %collective-permute-start.5 = (bf16[512,128]{1,0:T(8,128)(2,1)S(1)}, bf16[512,128]{1,0:T(8,128)(2,1)S(1)}, u32[]{:S(2)}, u32[]{:S(2)}) collective-permute-start(bf16[512,128]{1,0:T(8,128)(2,1)S(1)} %get-tuple-element.60), channel_id=1, source_target_pairs={{4,0},{5,1},{6,2},{7,3},{12,8},{13,9},{14,10},{15,11},{20,16},{21,... | collective-permute-start | bytes 393224 | tf_op jit(solution)/shard_map/ppermute | solution.py:515
  103.6 17.1 %all-to-all-start.1 = ((bf16[4,512,128]{2,1,0:T(8,128)(2,1)}), bf16[4,512,128]{2,1,0:T(8,128)(2,1)S(1)}, u32[]{:S(2)}, u32[]{:S(2)}) async-start(bf16[4,512,128]{2,1,0:T(8,128)(2,1)} %broadcast_in_dim.4), calls=%async_computation.1 | async-start | bytes 1048576 | tf_op jit(solution)/shard_map/all_to_all | solution.py:484
  118.0 6.3 %copy-start.6 = (bf16[1024,512]{1,0:T(8,128)(2,1)S(1)}, bf16[1024,512]{1,0:T(8,128)(2,1)}, u32[]{:S(2)}) copy-start(bf16[1024,512]{1,0:T(8,128)(2,1)} %copy-done.5) | copy-start | bytes 3145732
  118.0 6.3 %collective-permute-start.9 = (bf16[1024,512]{1,0:T(8,128)(2,1)}, bf16[1024,512]{1,0:T(8,128)(2,1)}, u32[]{:S(2)}, u32[]{:S(2)}) collective-permute-start(bf16[1024,512]{1,0:T(8,128)(2,1)} %get-tuple-element.69), channel_id=1, source_target_pairs={{0,8},{8,0},{16,24},{24,16},{1,9},{9,1},{17,25},{25,17},{2,10},{10... | collective-permute-start | bytes 3145736 | tf_op jit(solution)/shard_map/ppermute | solution.py:481
  118.0 6.3 %collective-permute-start.10 = (bf16[4,512,128]{2,1,0:T(8,128)(2,1)S(1)}, bf16[4,512,128]{2,1,0:T(8,128)(2,1)}, u32[]{:S(2)}, u32[]{:S(2)}) collective-permute-start(bf16[4,512,128]{2,1,0:T(8,128)(2,1)S(1)} %all-to-all-done.2.refs_0_), channel_id=1, source_target_pairs={{0,8},{8,0},{16,24},{24,16},{1,9},{9,1},{17,25},{25,17},{2,10},{10... | collective-permute-start | bytes 1572872 | tf_op jit(solution)/shard_map/ppermute | solution.py:481
  120.7 6.8 %collective-permute-start.7 = (bf16[4,512,128]{2,1,0:T(8,128)(2,1)S(1)}, bf16[4,512,128]{2,1,0:T(8,128)(2,1)}, u32[]{:S(2)}, u32[]{:S(2)}) collective-permute-start(bf16[4,512,128]{2,1,0:T(8,128)(2,1)S(1)} %all-to-all-done.1.refs_0_), channel_id=1, source_target_pairs={{0,8},{8,0},{16,24},{24,16},{1,9},{9,1},{17,25},{25,17},{2,10},{10... | collective-permute-start | bytes 1572872 | tf_op jit(solution)/shard_map/ppermute | solution.py:481
  120.7 45.8 %all-to-all-start.3 = ((bf16[4,128,1024]{2,1,0:T(8,128)(2,1)}), bf16[4,128,1024]{2,1,0:T(8,128)(2,1)S(1)}, u32[]{:S(2)}, u32[]{:S(2)}) async-start(bf16[4,128,1024]{2,1,0:T(8,128)(2,1)} %bitcast), calls=%async_computation.3 | async-start | bytes 2097152 | tf_op jit(solution)/shard_map/all_to_all | solution.py:484
  130.9 9.1 %collective-permute-start.12 = (bf16[256,512]{1,0:T(8,128)(2,1)S(1)}, bf16[256,512]{1,0:T(8,128)(2,1)S(1)}, u32[]{:S(2)}, u32[]{:S(2)}) collective-permute-start(bf16[256,512]{1,0:T(8,128)(2,1)S(1)} %get-tuple-element.76), channel_id=1, source_target_pairs={{0,16},{8,24},{16,0},{24,8},{1,17},{9,25},{17,1},{25,9},{2,18},{10... | collective-permute-start | bytes 786440 | tf_op jit(solution)/shard_map/ppermute | solution.py:534
  132.4 13.2 %collective-permute-start.14 = (bf16[256,512]{1,0:T(8,128)(2,1)S(1)}, bf16[256,512]{1,0:T(8,128)(2,1)S(1)}, u32[]{:S(2)}, u32[]{:S(2)}) collective-permute-start(bf16[256,512]{1,0:T(8,128)(2,1)S(1)} %get-tuple-element.77), channel_id=1, source_target_pairs={{0,16},{8,24},{16,0},{24,8},{1,17},{9,25},{17,1},{25,9},{2,18},{10... | collective-permute-start | bytes 786440 | tf_op jit(solution)/shard_map/ppermute | solution.py:534
  132.9 32.5 %collective-permute-start.11 = (bf16[256,1024]{1,0:T(8,128)(2,1)S(1)}, bf16[256,1024]{1,0:T(8,128)(2,1)S(1)}, u32[]{:S(2)}, u32[]{:S(2)}) collective-permute-start(bf16[256,1024]{1,0:T(8,128)(2,1)S(1)} %get-tuple-element.75), channel_id=1, source_target_pairs={{0,16},{8,24},{16,0},{24,8},{1,17},{9,25},{17,1},{25,9},{2,18},{10... | collective-permute-start | bytes 1572872 | tf_op jit(solution)/shard_map/ppermute | solution.py:534
  140.1 20.7 %collective-permute-start.13 = (bf16[256,512]{1,0:T(8,128)(2,1)S(1)}, bf16[256,512]{1,0:T(8,128)(2,1)S(1)}, u32[]{:S(2)}, u32[]{:S(2)}) collective-permute-start(bf16[256,512]{1,0:T(8,128)(2,1)S(1)} %add_convert_fusion.1), channel_id=1, source_target_pairs={{0,4},{1,5},{2,6},{3,7},{4,0},{5,1},{6,2},{7,3},{8,12},{9,13},{10,... | collective-permute-start | bytes 786440 | tf_op jit(solution)/shard_map/ppermute | solution.py:478
  145.7 19.8 %collective-permute-start.15 = (bf16[256,512]{1,0:T(8,128)(2,1)S(1)}, bf16[256,512]{1,0:T(8,128)(2,1)S(1)}, u32[]{:S(2)}, u32[]{:S(2)}) collective-permute-start(bf16[256,512]{1,0:T(8,128)(2,1)S(1)} %add_convert_fusion), channel_id=1, source_target_pairs={{0,4},{1,5},{2,6},{3,7},{4,0},{5,1},{6,2},{7,3},{8,12},{9,13},{10,... | collective-permute-start | bytes 786440 | tf_op jit(solution)/shard_map/ppermute | solution.py:478
  (16 other events, 14.4 us)

commit v3 on v2

--- a/solution.py
+++ b/solution.py
@@ -17,7 +17,8 @@
 NEGATIVE = -1e30
 BF16 = jnp.bfloat16
 F32 = jnp.float32
-VMEM_BYTES = 48 * 1024 * 1024
+VMEM_BYTES = 24 * 1024 * 1024
+ALL_VMEM_BYTES = 62 * 1024 * 1024
 
 NT = (((1,), (1,)), ((), ()))
 
@@ -103,7 +104,7 @@
 
 
 def packed(rows, groups, slabs, slab, queries, out_grad, key_states, value_states, layer_input):
-    any_spec = pl.BlockSpec(memory_space=pl.ANY)
+    any_spec = pl.BlockSpec(memory_space=pltpu.HBM)
     cycle = KVH * groups
     in_kernel = slab % HD == 0
     wide = KVH if in_kernel else 0
@@ -123,7 +124,7 @@
             pltpu.SemaphoreType.DMA((KVH * slabs,)),
             pltpu.SemaphoreType.DMA((2 * KVH,)),
         ],
-        compiler_params=pltpu.CompilerParams(vmem_limit_bytes=VMEM_BYTES),
+        compiler_params=pltpu.CompilerParams(vmem_limit_bytes=ALL_VMEM_BYTES),
         cost_estimate=pl.CostEstimate(flops=0, bytes_accessed=8 * 10**6, transcendentals=0),
         name="first_sends",
     )(*inputs)
@@ -155,8 +156,8 @@
     at += 1
     own_k, own_v = refs[at : at + 2]
     at += 2
-    down_out = refs[at : at + 2 * (groups - 1)]
-    at += 2 * (groups - 1)
+    down_out = refs[at : at + groups - 1]
+    at += groups - 1
     q_s, do_s, k_s, v_s, kt_s, dk_s, dv_s, down_s, sems = refs[at:]
 
     place = lax.axis_index("seq")
@@ -256,15 +257,14 @@
             own_v[...] = dv_s[base : base + span, :]
             for step in range(1, which + 1):
                 source = (which - step) * span
-                down_s[2 * step - 2] = dk_s[source : source + span, :].astype(BF16)
-                down_s[2 * step - 1] = dv_s[source : source + span, :].astype(BF16)
+                down_s[step - 1, 0] = dk_s[source : source + span, :].astype(BF16)
+                down_s[step - 1, 1] = dv_s[source : source + span, :].astype(BF16)
             for step in range(which + 1, groups):
-                down_s[2 * step - 2] = jnp.zeros((span, HD), BF16)
-                down_s[2 * step - 1] = jnp.zeros((span, HD), BF16)
+                down_s[step - 1] = jnp.zeros((2, span, HD), BF16)
 
     outs = [
         pltpu.make_async_copy(down_s.at[step], down_out[step], sems.at[step])
-        for step in range(2 * (groups - 1))
+        for step in range(groups - 1)
     ]
     for copy in outs:
         copy.start()
@@ -275,16 +275,16 @@
 def attention(rows, groups, queries, out_grad, keys_values, pieces):
     span = KVH * rows
     length = groups * span
-    any_spec = pl.BlockSpec(memory_space=pl.ANY)
+    any_spec = pl.BlockSpec(memory_space=pltpu.HBM)
     n_in = 3 + len(pieces)
     out_shape = (
         [jax.ShapeDtypeStruct((span, WIDE), BF16)]
         + [jax.ShapeDtypeStruct((span, HD), F32)] * 2
-        + [jax.ShapeDtypeStruct((span, HD), BF16)] * (2 * (groups - 1))
+        + [jax.ShapeDtypeStruct((2, span, HD), BF16)] * (groups - 1)
     )
     out_specs = (
         [pl.BlockSpec(memory_space=pltpu.VMEM)] * 3
-        + [any_spec] * (2 * (groups - 1))
+        + [any_spec] * (groups - 1)
     )
     outs = pl.pallas_call(
         lambda *refs: attention_kernel(rows, groups, *refs),
@@ -299,15 +299,14 @@
             pltpu.VMEM((HD, length), BF16),
             pltpu.VMEM((length, HD), F32),
             pltpu.VMEM((length, HD), F32),
-            pltpu.VMEM((2 * max(groups - 1, 1), span, HD), BF16),
+            pltpu.VMEM((max(groups - 1, 1), 2, span, HD), BF16),
             pltpu.SemaphoreType.DMA((2 * KVH + 2 * KVH * groups,)),
         ],
-        compiler_params=pltpu.CompilerParams(vmem_limit_bytes=VMEM_BYTES),
+        compiler_params=pltpu.CompilerParams(vmem_limit_bytes=ALL_VMEM_BYTES),
         cost_estimate=pl.CostEstimate(flops=10**10, bytes_accessed=5 * 10**7, transcendentals=0),
         name="attention",
     )(queries, out_grad, keys_values, *pieces)
-    down = outs[3:]
-    return outs[0], outs[1:3], (down[0::2], down[1::2])
+    return outs[0], outs[1:3], outs[3:]
 
 
 def transpose_kernel(rows, halves, width, *refs):
@@ -343,21 +342,22 @@
     return pl.pallas_call(
         lambda *refs: transpose_kernel(rows, halves, width, *refs),
         out_shape=[jax.ShapeDtypeStruct((halves * width, tokens), BF16)] * 2,
-        in_specs=[pl.BlockSpec(memory_space=pl.ANY)] * KVH,
+        in_specs=[pl.BlockSpec(memory_space=pltpu.HBM)] * KVH,
         out_specs=[vmem] * 2,
         scratch_shapes=[
             pltpu.VMEM((tokens, 2 * halves * width), BF16),
             pltpu.SemaphoreType.DMA((KVH,)),
         ],
-        compiler_params=pltpu.CompilerParams(vmem_limit_bytes=VMEM_BYTES),
+        compiler_params=pltpu.CompilerParams(vmem_limit_bytes=ALL_VMEM_BYTES),
         cost_estimate=pl.CostEstimate(flops=0, bytes_accessed=10**7, transcendentals=0),
         name="input_transposed",
     )(*pieces)
 
 
 def weight_kernel(rows, halves, groups, slab, joins, *refs):
-    own, other, xt, xt_other = refs[:4]
-    at = 4
+    own = refs[:KVH]
+    other, xt, xt_other = refs[KVH : KVH + 3]
+    at = KVH + 3
     if joins:
         before = refs[at]
         at += 1
@@ -372,11 +372,11 @@
     group = place // KVH
     head = place % KVH
     half = lax.axis_index("dp") // 2
-    for source in range(KVH):
-        columns = slice(source * HD, (source + 1) * HD)
-        g_s[:span, columns] = own[source]
-        g_s[span:, columns] = other[source]
-        mine_out[:, columns] = own[source, pl.ds(pl.multiple_of(head * rows, rows), rows), :]
+    for k in range(KVH):
+        columns = pl.ds(pl.multiple_of((head ^ k) * HD, HD), HD)
+        g_s[:span, columns] = own[k][...]
+        g_s[span:, columns] = other[:, k * HD : (k + 1) * HD]
+        mine_out[:, columns] = own[k][pl.ds(pl.multiple_of(head * rows, rows), rows), :]
     for apart in range(halves):
         for step in range(groups):
             owner = ((half ^ apart) * groups + (group ^ step)) * slab
@@ -406,13 +406,13 @@
             for step in range(groups)
         ]
         + [jax.ShapeDtypeStruct((rows, channels), BF16)],
-        in_specs=[vmem] * (4 + joins),
+        in_specs=[vmem] * (KVH + 3 + joins),
         out_specs=[vmem] * (groups + 2),
         scratch_shapes=[pltpu.VMEM((2 * span, channels), BF16)],
-        compiler_params=pltpu.CompilerParams(vmem_limit_bytes=VMEM_BYTES),
+        compiler_params=pltpu.CompilerParams(vmem_limit_bytes=ALL_VMEM_BYTES),
         cost_estimate=pl.CostEstimate(flops=15 * 10**8, bytes_accessed=6 * 10**6, transcendentals=0),
         name="weight_terms",
-    )(own, other, xt, xt_other, *more)
+    )(*own, other, xt, xt_other, *more)
     return outs[0], outs[1 : 1 + groups], outs[1 + groups]
 
 
@@ -428,7 +428,7 @@
         out_shape=jax.ShapeDtypeStruct((rows, QH * HD), BF16),
         in_specs=[vmem],
         out_specs=vmem,
-        compiler_params=pltpu.CompilerParams(vmem_limit_bytes=VMEM_BYTES),
+        compiler_params=pltpu.CompilerParams(vmem_limit_bytes=ALL_VMEM_BYTES),
         cost_estimate=pl.CostEstimate(flops=0, bytes_accessed=5 * 10**6, transcendentals=0),
         name="query_grad_placed",
     )(pieces)
@@ -458,7 +458,7 @@
         out_shape=jax.ShapeDtypeStruct((slab, 2 * keep[0].shape[1]), F32),
         in_specs=[vmem] * (2 + len(both) + len(rest)),
         out_specs=vmem,
-        compiler_params=pltpu.CompilerParams(vmem_limit_bytes=VMEM_BYTES),
+        compiler_params=pltpu.CompilerParams(vmem_limit_bytes=ALL_VMEM_BYTES),
         cost_estimate=pl.CostEstimate(flops=0, bytes_accessed=3 * 10**6, transcendentals=0),
         name="weight_grad_joined",
     )(*keep, *both, *rest)
@@ -506,16 +506,22 @@
     last, inputs, down = after((columns[KVH - 1], inputs, down))
     inputs.append(swap(last, KVH - 1))
 
+    received = [
+        lax.ppermute(
+            down[step - 1], "seq", [(i + step * KVH, i) for i in range(cycle - step * KVH)]
+        )
+        for step in range(1, groups)
+    ]
+    received, inputs = after((received, inputs))
     gathered = [None, None]
     others = [None, None]
     for kind in (1, 0):
         total = own[kind]
-        for step in range(1, groups):
-            pairs = [(i + step * KVH, i) for i in range(cycle - step * KVH)]
-            total = total + lax.ppermute(down[kind][step - 1], "seq", pairs).astype(F32)
-        copies = jnp.broadcast_to(total.astype(BF16)[None], (KVH,) + total.shape)
-        gathered[kind] = exchange(copies, within)
-        others[kind] = across_cores(gathered[kind])
+        for part in received:
+            total = total + part[kind].astype(F32)
+        total = total.astype(BF16)
+        gathered[kind] = [total] + [swap(total, k) for k in range(1, KVH)]
+        others[kind] = across_cores(jnp.concatenate(gathered[kind], axis=1))
     xt, xt_give = transposed(rows, halves, groups * slab, inputs)
     xt_other = across_cores(xt_give)
 
@@ -524,9 +530,6 @@
     send = [None, None]
     keep[1], send[1], narrow[1] = weight_terms(
         rows, halves, groups, slab, gathered[1], others[1], xt, xt_other
-    )
-    keep[0], send[0], narrow[0] = weight_terms(
-        rows, halves, groups, slab, gathered[0], others[0], xt, xt_other, send[1][0]
     )
 
     def over_sequences(array):
@@ -539,16 +542,21 @@
             for apart in range(1, halves)
         ]
 
-    received = []
-    for kind in (0, 1):
+    first = [over_sequences(send[1][step]) for step in range(1, groups)]
+    first, grads, others[0] = after((first, grads, others[0]))
+    keep[0], send[0], narrow[0] = weight_terms(
+        rows, halves, groups, slab, gathered[0], others[0], xt, xt_other, send[1][0]
+    )
+    second = [over_sequences(send[0][step]) for step in range(1, groups)]
+    rest = []
+    for kind, parts in ((0, second), (1, first)):
         for step in range(1, groups):
             total = keep[kind][step * slab : (step + 1) * slab]
-            for part in over_sequences(send[kind][step]):
+            for part in parts[step - 1]:
                 total = total + part.astype(F32)
-            received.append(swap(total.astype(BF16), step * KVH))
-    weight_grad = joined(slab, keep, over_sequences(send[0][0]), received)
-
-    grads, _ = after((grads, gathered))
+            rest.append(swap(total.astype(BF16), step * KVH))
+    weight_grad = joined(slab, keep, over_sequences(send[0][0]), rest)
+
     returned = exchange(grads.reshape(KVH, rows, WIDE), within)
     query_grad = placed(rows, returned)
     return (query_grad, narrow[0], narrow[1], weight_grad)

time: 168 us -> 172 us (1.024)
  local copies, waits for them, and re-layouts: 16.1 us -> 4.53 us
  Pallas kernels: 26.7 us -> 35.4 us
  waiting for transfers between devices: 84.9 us -> 89.2 us
  other arithmetic: 0.19 us -> 3.49 us
    ppermute x8 -> x14, starting transfers between devices: 7.34 us -> 21.9 us  [swap(): return lax.ppermute(array, 'seq', [(i, i ^ k) for i in range(cycle)])]
    all_to_all x4 -> x2, starting transfers between devices: 24.8 us -> 11.2 us  [exchange(): lax.all_to_all(array, 'seq', split_axis=0, concat_axis=0, tiled=True, axi...]
    ppermute x8 -> x14, waiting for transfers between devices: 48.8 us -> 61.3 us  [swap(): return lax.ppermute(array, 'seq', [(i, i ^ k) for i in range(cycle)])]
    unnamed x40, local copies, waits for them, and re-layouts: 14.4 us -> 4.53 us
    ppermute x2 -> x1, waiting for transfers between devices: 21.4 us -> 14.3 us  [local(): lax.ppermute(down[step - 1], 'seq', [(i + step * KVH, i) for i in range(c...]
    all_to_all x4 -> x2, waiting for transfers between devices: 3.66 us -> 0.01 us  [exchange(): lax.all_to_all(array, 'seq', split_axis=0, concat_axis=0, tiled=True, axi...]
    convert_element_type x4 -> x3, other arithmetic: 0.19 us -> 3.37 us  [the longest x2 2.23 us: local(): rest.append(swap(total.astype(BF16), step * KVH))]
    ppermute x3, waiting for transfers between devices: 11 us -> 13.6 us  [over_sequences(): lax.ppermute(array[(apart - 1) * slab:apart * slab], 'dp', [(i, i ^ 2 * a...]
  transfers between devices with their start and end apart: 20 -> 23, of which waited for: 11 -> 15; matrix products, arithmetic and copies ran while one was open for 1% -> 2% of each run, Pallas kernels for 14% -> 15%
where the time goes in v3:
time: 172 us
  waiting for transfers between devices  89.2 us (52%)
  starting transfers between devices  38.3 us (22%)
  Pallas kernels  35.4 us (21%)
  local copies, waits for them, and re-layouts  4.53 us (3%)
  other arithmetic  3.49 us (2%)
    ppermute x14, waiting for transfers between devices, swap(): return lax.ppermute(array, 'seq', [(i, i ^ k) for i in range(cycle)])  61.3 us
    ppermute x14, starting transfers between devices, swap(): return lax.ppermute(array, 'seq', [(i, i ^ k) for i in range(cycle)])  21.9 us
    ppermute x1, waiting for transfers between devices, local(): lax.ppermute(down[step - 1], 'seq', [(i + step * KVH, i) for i in range(c...  14.3 us
    pallas_call x1, Pallas kernels, attention(): pl.pallas_call(lambda *refs: attention_kernel(rows, groups, *refs), out_s...  14 us
    ppermute x3, waiting for transfers between devices, over_sequences(): lax.ppermute(array[(apart - 1) * slab:apart * slab], 'dp', [(i, i ^ 2 * a...  13.6 us
    all_to_all x2, starting transfers between devices, exchange(): lax.all_to_all(array, 'seq', split_axis=0, concat_axis=0, tiled=True, axi...  11.2 us
    pallas_call x2, Pallas kernels, weight_terms(): pl.pallas_call(lambda *refs: weight_kernel(rows, halves, groups, slab, jo...  8.59 us
    unnamed x40, local copies, waits for them, and re-layouts  4.53 us
  transfers between devices with their start and end apart: 23, of which 15 were waited for; matrix products, arithmetic and copies ran while one was open for 2% of the time, Pallas kernels for 15%

profile of v3, /device:TPU:0, one launch (start us, length us, event | category | flops | bytes accessed | tf_op | source)
XLA Modules:
  0.0 171.7 jit_solution(6752379019700631943)
XLA Ops:
  0.6 4.4 %first_sends.1 = (bf16[8,128,256]{2,1,0:T(8,128)(2,1)}, bf16[128,2048]{1,0:T(8,128)(2,1)}, bf16[128,2048]{1,0:T(8,128)(2,1)}, bf16[128,2048]{1,0:T(8,128)(2,1)},...) custom-call(bf16[128,4096]{1,0:T(8,128)(2,1)} %refs_0_.3, ...), custom_call_target="tpu_custom_call" | custom-call | bytes 8000000 | tf_op jit(solution)/shard_map/first_sends/pallas_call | solution.py:112
  5.0 7.3 %all-to-all-start = ((bf16[8,128,256]{2,1,0:T(8,128)(2,1)}), bf16[8,128,256]{2,1,0:T(8,128)(2,1)S(1)}, u32[]{:S(2)}, u32[]{:S(2)}) async-start(bf16[8,128,256]{2,1,0:T(8,128)(2,1)} %get-tuple-element.46), calls=%async_computation | async-start | bytes 1048576 | tf_op jit(solution)/shard_map/all_to_all | solution.py:484
  12.3 2.0 %collective-permute-start = (bf16[128,2048]{1,0:T(8,128)(2,1)}, bf16[128,2048]{1,0:T(8,128)(2,1)S(1)}, u32[]{:S(2)}, u32[]{:S(2)}) collective-permute-start(bf16[128,2048]{1,0:T(8,128)(2,1)} %get-tuple-element.51), channel_id=1, source_target_pairs={{0,1},{1,0},{2,3},{3,2},{4,5},{5,4},{6,7},{7,6},{8,9},{9,8},{10,11... | collective-permute-start | bytes 1572872 | tf_op jit(solution)/shard_map/ppermute | solution.py:478
  15.8 15.7 %collective-permute-done.refs_3_ = bf16[128,2048]{1,0:T(8,128)(2,1)S(1)} collective-permute-done((bf16[128,2048]{1,0:T(8,128)(2,1)}, bf16[128,2048]{1,0:T(8,128)(2,1)S(1)}, u32[]{:S(2)}, u32[]{:S(2)}) %collective-permute-start) | collective-permute-done | bytes 524320 | tf_op jit(solution)/shard_map/ppermute | solution.py:478
  31.5 4.2 %collective-permute-done.1.refs_4_ = bf16[128,2048]{1,0:T(8,128)(2,1)S(1)} collective-permute-done((bf16[128,2048]{1,0:T(8,128)(2,1)}, bf16[128,2048]{1,0:T(8,128)(2,1)S(1)}, u32[]{:S(2)}, u32[]{:S(2)}) %collective-permute-start.1) | collective-permute-done | bytes 524320 | tf_op jit(solution)/shard_map/ppermute | solution.py:478
  35.7 10.8 %collective-permute-done.2.refs_5_ = bf16[128,2048]{1,0:T(8,128)(2,1)S(1)} collective-permute-done((bf16[128,2048]{1,0:T(8,128)(2,1)}, bf16[128,2048]{1,0:T(8,128)(2,1)S(1)}, u32[]{:S(2)}, u32[]{:S(2)}) %collective-permute-start.2) | collective-permute-done | bytes 524320 | tf_op jit(solution)/shard_map/ppermute | solution.py:478
  48.6 14.0 %attention.1 = (bf16[512,1024]{1,0:T(8,128)(2,1)}, f32[512,128]{1,0:T(8,128)}, f32[512,128]{1,0:T(8,128)}, bf16[2,512,128]{2,1,0:T(8,128)(2,1)}) custom-call(bf16[128,4096]{1,0:T(8,128)(2,1)} %refs_0_.3, bf16[128,4096]{1,0:T(8,128)(2,1)} %refs_1_.3, bf16[8,128,256]{2,1,0:T(8,128)(2,1)} %copy-done.1, bf16[128,2048]{1,0:T(8,128)(2,1)} %copy-done.17, ...), custom_call_target="tpu_custom_call" | custom-call | flops 10000000000 | bytes 50000000 | tf_op jit(solution)/shard_map/attention/pallas_call | solution.py:289
  62.7 2.2 %collective-permute-start.6 = (bf16[128,2048]{1,0:T(8,128)(2,1)}, bf16[128,2048]{1,0:T(8,128)(2,1)S(1)}, u32[]{:S(2)}, u32[]{:S(2)}) collective-permute-start(bf16[128,2048]{1,0:T(8,128)(2,1)} %get-tuple-element.67), channel_id=1, source_target_pairs={{0,3},{1,2},{2,1},{3,0},{4,7},{5,6},{6,5},{7,4},{8,11},{9,10},{10,... | collective-permute-start | bytes 1572872 | tf_op jit(solution)/shard_map/ppermute | solution.py:478
  66.2 14.3 %collective-permute-done.5 = bf16[2,512,128]{2,1,0:T(8,128)(2,1)} collective-permute-done((bf16[2,512,128]{2,1,0:T(8,128)(2,1)}, bf16[2,512,128]{2,1,0:T(8,128)(2,1)}, u32[]{:S(2)}, u32[]{:S(2)}) %collective-permute-start.5) | collective-permute-done | bytes 262176 | tf_op jit(solution)/shard_map/ppermute | solution.py:510
  82.6 3.2 %input_transposed.1 = (bf16[1024,512]{1,0:T(8,128)(2,1)}, bf16[1024,512]{1,0:T(8,128)(2,1)}) custom-call(bf16[128,2048]{1,0:T(8,128)(2,1)} %get-tuple-element.69.refs_0_, bf16[128,2048]{1,0:T(8,128)(2,1)} %copy-done.2, bf16[128,2048]{1,0:T(8,128)(2,1)} %copy-done.3, bf16[128,2048]{1,0:T(8,128)(2,1)} %copy-done.4), custom_call_target="tpu_custom_call" | custom-call | bytes 10000000 | tf_op jit(solution)/shard_map/input_transposed/pallas_call | solution.py:342
  87.1 10.2 %collective-permute-start.9 = (bf16[512,128]{1,0:T(8,128)(2,1)S(1)}, bf16[512,128]{1,0:T(8,128)(2,1)S(1)}, u32[]{:S(2)}, u32[]{:S(2)}) collective-permute-start(bf16[512,128]{1,0:T(8,128)(2,1)S(1)} %get-tuple-element.89.refs_0_), channel_id=1, source_target_pairs={{0,3},{1,2},{2,1},{3,0},{4,7},{5,6},{6,5},{7,4},{8,11},{9,10},{10,... | collective-permute-start | bytes 393224 | tf_op jit(solution)/shard_map/ppermute | solution.py:478
  98.4 3.3 %collective-permute-done.9.refs_3_ = bf16[512,128]{1,0:T(8,128)(2,1)S(1)} collective-permute-done((bf16[512,128]{1,0:T(8,128)(2,1)S(1)}, bf16[512,128]{1,0:T(8,128)(2,1)S(1)}, u32[]{:S(2)}, u32[]{:S(2)}) %collective-permute-start.9) | collective-permute-done | bytes 131104 | tf_op jit(solution)/shard_map/ppermute | solution.py:478
  101.7 2.2 %collective-permute-done.8.refs_2_ = bf16[512,128]{1,0:T(8,128)(2,1)S(1)} collective-permute-done((bf16[512,128]{1,0:T(8,128)(2,1)S(1)}, bf16[512,128]{1,0:T(8,128)(2,1)S(1)}, u32[]{:S(2)}, u32[]{:S(2)}) %collective-permute-start.8) | collective-permute-done | bytes 131104 | tf_op jit(solution)/shard_map/ppermute | solution.py:478
  104.5 2.7 %collective-permute-start.15 = (bf16[512,128]{1,0:T(8,128)(2,1)S(1)}, bf16[512,128]{1,0:T(8,128)(2,1)S(1)}, u32[]{:S(2)}, u32[]{:S(2)}) collective-permute-start(bf16[512,128]{1,0:T(8,128)(2,1)S(1)} %get-tuple-element.88.refs_0_), channel_id=1, source_target_pairs={{0,3},{1,2},{2,1},{3,0},{4,7},{5,6},{6,5},{7,4},{8,11},{9,10},{10,... | collective-permute-start | bytes 393224 | tf_op jit(solution)/shard_map/ppermute | solution.py:478
  108.2 3.5 %collective-permute-done.15.refs_3_ = bf16[512,128]{1,0:T(8,128)(2,1)S(1)} collective-permute-done((bf16[512,128]{1,0:T(8,128)(2,1)S(1)}, bf16[512,128]{1,0:T(8,128)(2,1)S(1)}, u32[]{:S(2)}, u32[]{:S(2)}) %collective-permute-start.15) | collective-permute-done | bytes 131104 | tf_op jit(solution)/shard_map/ppermute | solution.py:478
  115.0 4.3 %weight_terms.2 = (f32[512,512]{1,0:T(8,128)}, bf16[256,512]{1,0:T(8,128)(2,1)}, bf16[256,512]{1,0:T(8,128)(2,1)}, bf16[128,512]{1,0:T(8,128)(2,1)}) custom-call(bf16[512,128]{1,0:T(8,128)(2,1)} %copy-done.7, bf16[512,128]{1,0:T(8,128)(2,1)} %copy-done.15, bf16[512,128]{1,0:T(8,128)(2,1)} %copy-done.13, bf16[512,128]{1,0:T(8,128)(2,1)} %copy-done.11, ...), custom_call_target="tpu_custom_call" | custom-call | flops 1500000000 | bytes 6000000 | tf_op jit(solution)/shard_map/weight_terms/pallas_call | solution.py:399
  121.0 7.4 %collective-permute-done.12 = bf16[256,512]{1,0:T(8,128)(2,1)S(1)} collective-permute-done((bf16[256,512]{1,0:T(8,128)(2,1)}, bf16[256,512]{1,0:T(8,128)(2,1)S(1)}, u32[]{:S(2)}, u32[]{:S(2)}) %collective-permute-start.12) | collective-permute-done | bytes 262176 | tf_op jit(solution)/shard_map/ppermute | solution.py:537
  128.4 3.9 %all-to-all-start.1 = ((bf16[4,128,1024]{2,1,0:T(8,128)(2,1)}), bf16[4,128,1024]{2,1,0:T(8,128)(2,1)S(1)}, u32[]{:S(2)}, u32[]{:S(2)}) async-start(bf16[4,128,1024]{2,1,0:T(8,128)(2,1)} %bitcast.7), calls=%async_computation.1 | async-start | bytes 2097152 | tf_op jit(solution)/shard_map/all_to_all | solution.py:484
  132.2 4.3 %weight_terms.3 = (f32[512,512]{1,0:T(8,128)}, bf16[256,1024]{1,0:T(8,128)(2,1)}, bf16[256,512]{1,0:T(8,128)(2,1)}, bf16[128,512]{1,0:T(8,128)(2,1)}) custom-call(bf16[512,128]{1,0:T(8,128)(2,1)} %copy-done.6, bf16[512,128]{1,0:T(8,128)(2,1)} %copy-done.14, bf16[512,128]{1,0:T(8,128)(2,1)} %copy-done.12, bf16[512,128]{1,0:T(8,128)(2,1)} %copy-done.10, ...), custom_call_target="tpu_custom_call" | custom-call | flops 1500000000 | bytes 6000000 | tf_op jit(solution)/shard_map/weight_terms/pallas_call | solution.py:399
  139.7 6.2 %collective-permute-done.18 = bf16[256,512]{1,0:T(8,128)(2,1)S(1)} collective-permute-done((bf16[256,512]{1,0:T(8,128)(2,1)}, bf16[256,512]{1,0:T(8,128)(2,1)S(1)}, u32[]{:S(2)}, u32[]{:S(2)}) %collective-permute-start.18) | collective-permute-done | bytes 262176 | tf_op jit(solution)/shard_map/ppermute | solution.py:537
  147.2 13.8 %collective-permute-done.20.refs_4_ = bf16[256,512]{1,0:T(8,128)(2,1)S(1)} collective-permute-done((bf16[256,512]{1,0:T(8,128)(2,1)S(1)}, bf16[256,512]{1,0:T(8,128)(2,1)S(1)}, u32[]{:S(2)}, u32[]{:S(2)}) %collective-permute-start.20) | collective-permute-done | bytes 262176 | tf_op jit(solution)/shard_map/ppermute | solution.py:478
  160.9 3.8 %collective-permute-done.19.refs_3_ = bf16[256,512]{1,0:T(8,128)(2,1)} collective-permute-done((bf16[256,512]{1,0:T(8,128)(2,1)S(1)}, bf16[256,512]{1,0:T(8,128)(2,1)}, u32[]{:S(2)}, u32[]{:S(2)}) %collective-permute-start.19) | collective-permute-done | bytes 262176 | tf_op jit(solution)/shard_map/ppermute | solution.py:478
  165.5 2.9 %weight_grad_joined.1 = f32[256,1024]{1,0:T(8,128)} custom-call(f32[512,512]{1,0:T(8,128)} %get-tuple-element.83.refs_0_, f32[512,512]{1,0:T(8,128)} %get-tuple-element.84.refs_1_, bf16[256,1024]{1,0:T(8,128)(2,1)} %copy-done.5, bf16[256,512]{1,0:T(8,128)(2,1)} %collective-permute-done.19.refs_3_, bf16[256,512]{1,0:T(8,128)(2,1)} %copy-done.8), custom_call_target="tpu_custom_call" | custom-call | bytes 3000000 | tf_op jit(solution)/shard_map/weight_grad_joined/pallas_call | solution.py:456
  169.4 2.3 %query_grad_placed.1 = bf16[128,4096]{1,0:T(8,128)(2,1)} custom-call(bf16[4,128,1024]{2,1,0:T(8,128)(2,1)} %copy-done), custom_call_target="tpu_custom_call" | custom-call | bytes 5000000 | tf_op jit(solution)/shard_map/query_grad_placed/pallas_call | solution.py:426
  (74 shorter events, 22.0 us)
Async XLA Ops:
  5.0 42.8 %all-to-all-start = ((bf16[8,128,256]{2,1,0:T(8,128)(2,1)}), bf16[8,128,256]{2,1,0:T(8,128)(2,1)S(1)}, u32[]{:S(2)}, u32[]{:S(2)}) async-start(bf16[8,128,256]{2,1,0:T(8,128)(2,1)} %get-tuple-element.46), calls=%async_computation | async-start | bytes 1048576 | tf_op jit(solution)/shard_map/all_to_all | solution.py:484
  12.3 19.2 %collective-permute-start = (bf16[128,2048]{1,0:T(8,128)(2,1)}, bf16[128,2048]{1,0:T(8,128)(2,1)S(1)}, u32[]{:S(2)}, u32[]{:S(2)}) collective-permute-start(bf16[128,2048]{1,0:T(8,128)(2,1)} %get-tuple-element.51), channel_id=1, source_target_pairs={{0,1},{1,0},{2,3},{3,2},{4,5},{5,4},{6,7},{7,6},{8,9},{9,8},{10,11... | collective-permute-start | bytes 1572872 | tf_op jit(solution)/shard_map/ppermute | solution.py:478
  14.3 21.4 %collective-permute-start.1 = (bf16[128,2048]{1,0:T(8,128)(2,1)}, bf16[128,2048]{1,0:T(8,128)(2,1)S(1)}, u32[]{:S(2)}, u32[]{:S(2)}) collective-permute-start(bf16[128,2048]{1,0:T(8,128)(2,1)} %get-tuple-element.52), channel_id=1, source_target_pairs={{0,2},{1,3},{2,0},{3,1},{4,6},{5,7},{6,4},{7,5},{8,10},{9,11},{10,... | collective-permute-start | bytes 1572872 | tf_op jit(solution)/shard_map/ppermute | solution.py:478
  15.8 30.7 %collective-permute-start.2 = (bf16[128,2048]{1,0:T(8,128)(2,1)}, bf16[128,2048]{1,0:T(8,128)(2,1)S(1)}, u32[]{:S(2)}, u32[]{:S(2)}) collective-permute-start(bf16[128,2048]{1,0:T(8,128)(2,1)} %get-tuple-element.53), channel_id=1, source_target_pairs={{0,3},{1,2},{2,1},{3,0},{4,7},{5,6},{6,5},{7,4},{8,11},{9,10},{10,... | collective-permute-start | bytes 1572872 | tf_op jit(solution)/shard_map/ppermute | solution.py:478
  46.5 16.2 %collective-permute-start.3 = (bf16[128,2048]{1,0:T(8,128)(2,1)}, bf16[128,2048]{1,0:T(8,128)(2,1)S(1)}, u32[]{:S(2)}, u32[]{:S(2)}) collective-permute-start(bf16[128,2048]{1,0:T(8,128)(2,1)} %get-tuple-element.60), channel_id=1, source_target_pairs={{0,1},{1,0},{2,3},{3,2},{4,5},{5,4},{6,7},{7,6},{8,9},{9,8},{10,11... | collective-permute-start | bytes 1572872 | tf_op jit(solution)/shard_map/ppermute | solution.py:478
  47.3 15.4 %collective-permute-start.4 = (bf16[128,2048]{1,0:T(8,128)(2,1)}, bf16[128,2048]{1,0:T(8,128)(2,1)S(1)}, u32[]{:S(2)}, u32[]{:S(2)}) collective-permute-start(bf16[128,2048]{1,0:T(8,128)(2,1)} %get-tuple-element.61), channel_id=1, source_target_pairs={{0,2},{1,3},{2,0},{3,1},{4,6},{5,7},{6,4},{7,5},{8,10},{9,11},{10,... | collective-permute-start | bytes 1572872 | tf_op jit(solution)/shard_map/ppermute | solution.py:478
  62.7 19.1 %collective-permute-start.6 = (bf16[128,2048]{1,0:T(8,128)(2,1)}, bf16[128,2048]{1,0:T(8,128)(2,1)S(1)}, u32[]{:S(2)}, u32[]{:S(2)}) collective-permute-start(bf16[128,2048]{1,0:T(8,128)(2,1)} %get-tuple-element.67), channel_id=1, source_target_pairs={{0,3},{1,2},{2,1},{3,0},{4,7},{5,6},{6,5},{7,4},{8,11},{9,10},{10,... | collective-permute-start | bytes 1572872 | tf_op jit(solution)/shard_map/ppermute | solution.py:478
  64.9 15.6 %collective-permute-start.5 = (bf16[2,512,128]{2,1,0:T(8,128)(2,1)}, bf16[2,512,128]{2,1,0:T(8,128)(2,1)}, u32[]{:S(2)}, u32[]{:S(2)}) collective-permute-start(bf16[2,512,128]{2,1,0:T(8,128)(2,1)} %get-tuple-element.63), channel_id=1, source_target_pairs={{4,0},{5,1},{6,2},{7,3},{12,8},{13,9},{14,10},{15,11},{20,16},{21,... | collective-permute-start | bytes 786440 | tf_op jit(solution)/shard_map/ppermute | solution.py:510
  85.9 29.2 %collective-permute-start.11 = (bf16[1024,512]{1,0:T(8,128)(2,1)}, bf16[1024,512]{1,0:T(8,128)(2,1)}, u32[]{:S(2)}, u32[]{:S(2)}) collective-permute-start(bf16[1024,512]{1,0:T(8,128)(2,1)} %get-tuple-element.74), channel_id=1, source_target_pairs={{0,8},{8,0},{16,24},{24,16},{1,9},{9,1},{17,25},{25,17},{2,10},{10... | collective-permute-start | bytes 3145736 | tf_op jit(solution)/shard_map/ppermute | solution.py:481
  87.1 32.3 %copy-start.6 = (bf16[512,128]{1,0:T(8,128)(2,1)}, bf16[512,128]{1,0:T(8,128)(2,1)S(1)}, u32[]{:S(2)}) copy-start(bf16[512,128]{1,0:T(8,128)(2,1)S(1)} %get-tuple-element.88.refs_0_) | copy-start | bytes 393220
  87.1 14.6 %collective-permute-start.9 = (bf16[512,128]{1,0:T(8,128)(2,1)S(1)}, bf16[512,128]{1,0:T(8,128)(2,1)S(1)}, u32[]{:S(2)}, u32[]{:S(2)}) collective-permute-start(bf16[512,128]{1,0:T(8,128)(2,1)S(1)} %get-tuple-element.89.refs_0_), channel_id=1, source_target_pairs={{0,3},{1,2},{2,1},{3,0},{4,7},{5,6},{6,5},{7,4},{8,11},{9,10},{10,... | collective-permute-start | bytes 393224 | tf_op jit(solution)/shard_map/ppermute | solution.py:478
  97.3 6.5 %collective-permute-start.8 = (bf16[512,128]{1,0:T(8,128)(2,1)S(1)}, bf16[512,128]{1,0:T(8,128)(2,1)S(1)}, u32[]{:S(2)}, u32[]{:S(2)}) collective-permute-start(bf16[512,128]{1,0:T(8,128)(2,1)S(1)} %get-tuple-element.89.refs_0_), channel_id=1, source_target_pairs={{0,2},{1,3},{2,0},{3,1},{4,6},{5,7},{6,4},{7,5},{8,10},{9,11},{10,... | collective-permute-start | bytes 393224 | tf_op jit(solution)/shard_map/ppermute | solution.py:478
  97.3 7.0 %collective-permute-start.7 = (bf16[512,128]{1,0:T(8,128)(2,1)S(1)}, bf16[512,128]{1,0:T(8,128)(2,1)S(1)}, u32[]{:S(2)}, u32[]{:S(2)}) collective-permute-start(bf16[512,128]{1,0:T(8,128)(2,1)S(1)} %get-tuple-element.89.refs_0_), channel_id=1, source_target_pairs={{0,1},{1,0},{2,3},{3,2},{4,5},{5,4},{6,7},{7,6},{8,9},{9,8},{10,11... | collective-permute-start | bytes 393224 | tf_op jit(solution)/shard_map/ppermute | solution.py:478
  104.3 9.9 %collective-permute-start.10 = (bf16[512,512]{1,0:T(8,128)(2,1)S(1)}, bf16[512,512]{1,0:T(8,128)(2,1)S(1)}, u32[]{:S(2)}, u32[]{:S(2)}) collective-permute-start(bf16[512,512]{1,0:T(8,128)(2,1)S(1)} %pad_maximum_fusion), channel_id=1, source_target_pairs={{0,8},{8,0},{16,24},{24,16},{1,9},{9,1},{17,25},{25,17},{2,10},{10... | collective-permute-start | bytes 1572872 | tf_op jit(solution)/shard_map/ppermute | solution.py:481
  104.5 7.2 %collective-permute-start.15 = (bf16[512,128]{1,0:T(8,128)(2,1)S(1)}, bf16[512,128]{1,0:T(8,128)(2,1)S(1)}, u32[]{:S(2)}, u32[]{:S(2)}) collective-permute-start(bf16[512,128]{1,0:T(8,128)(2,1)S(1)} %get-tuple-element.88.refs_0_), channel_id=1, source_target_pairs={{0,3},{1,2},{2,1},{3,0},{4,7},{5,6},{6,5},{7,4},{8,11},{9,10},{10,... | collective-permute-start | bytes 393224 | tf_op jit(solution)/shard_map/ppermute | solution.py:478
  107.1 6.5 %collective-permute-start.14 = (bf16[512,128]{1,0:T(8,128)(2,1)S(1)}, bf16[512,128]{1,0:T(8,128)(2,1)S(1)}, u32[]{:S(2)}, u32[]{:S(2)}) collective-permute-start(bf16[512,128]{1,0:T(8,128)(2,1)S(1)} %get-tuple-element.88.refs_0_), channel_id=1, source_target_pairs={{0,2},{1,3},{2,0},{3,1},{4,6},{5,7},{6,4},{7,5},{8,10},{9,11},{10,... | collective-permute-start | bytes 393224 | tf_op jit(solution)/shard_map/ppermute | solution.py:478
  107.1 6.9 %collective-permute-start.13 = (bf16[512,128]{1,0:T(8,128)(2,1)S(1)}, bf16[512,128]{1,0:T(8,128)(2,1)S(1)}, u32[]{:S(2)}, u32[]{:S(2)}) collective-permute-start(bf16[512,128]{1,0:T(8,128)(2,1)S(1)} %get-tuple-element.88.refs_0_), channel_id=1, source_target_pairs={{0,1},{1,0},{2,3},{3,2},{4,5},{5,4},{6,7},{7,6},{8,9},{9,8},{10,11... | collective-permute-start | bytes 393224 | tf_op jit(solution)/shard_map/ppermute | solution.py:478
  114.1 6.9 %collective-permute-start.16 = (bf16[512,512]{1,0:T(8,128)(2,1)S(1)}, bf16[512,512]{1,0:T(8,128)(2,1)}, u32[]{:S(2)}, u32[]{:S(2)}) collective-permute-start(bf16[512,512]{1,0:T(8,128)(2,1)S(1)} %pad_maximum_fusion.1), channel_id=1, source_target_pairs={{0,8},{8,0},{16,24},{24,16},{1,9},{9,1},{17,25},{25,17},{2,10},{10... | collective-permute-start | bytes 1572872 | tf_op jit(solution)/shard_map/ppermute | solution.py:481
  119.4 9.0 %collective-permute-start.12 = (bf16[256,512]{1,0:T(8,128)(2,1)}, bf16[256,512]{1,0:T(8,128)(2,1)S(1)}, u32[]{:S(2)}, u32[]{:S(2)}) collective-permute-start(bf16[256,512]{1,0:T(8,128)(2,1)} %get-tuple-element.75), channel_id=1, source_target_pairs={{0,16},{8,24},{16,0},{24,8},{1,17},{9,25},{17,1},{25,9},{2,18},{10... | collective-permute-start | bytes 786440 | tf_op jit(solution)/shard_map/ppermute | solution.py:537
  128.4 40.1 %all-to-all-start.1 = ((bf16[4,128,1024]{2,1,0:T(8,128)(2,1)}), bf16[4,128,1024]{2,1,0:T(8,128)(2,1)S(1)}, u32[]{:S(2)}, u32[]{:S(2)}) async-start(bf16[4,128,1024]{2,1,0:T(8,128)(2,1)} %bitcast.7), calls=%async_computation.1 | async-start | bytes 2097152 | tf_op jit(solution)/shard_map/all_to_all | solution.py:484
  136.5 9.5 %collective-permute-start.18 = (bf16[256,512]{1,0:T(8,128)(2,1)}, bf16[256,512]{1,0:T(8,128)(2,1)S(1)}, u32[]{:S(2)}, u32[]{:S(2)}) collective-permute-start(bf16[256,512]{1,0:T(8,128)(2,1)} %get-tuple-element.86), channel_id=1, source_target_pairs={{0,16},{8,24},{16,0},{24,8},{1,17},{9,25},{17,1},{25,9},{2,18},{10... | collective-permute-start | bytes 786440 | tf_op jit(solution)/shard_map/ppermute | solution.py:537
  138.0 26.7 %collective-permute-start.17 = (bf16[256,1024]{1,0:T(8,128)(2,1)}, bf16[256,1024]{1,0:T(8,128)(2,1)S(1)}, u32[]{:S(2)}, u32[]{:S(2)}) collective-permute-start(bf16[256,1024]{1,0:T(8,128)(2,1)} %get-tuple-element.85), channel_id=1, source_target_pairs={{0,16},{8,24},{16,0},{24,8},{1,17},{9,25},{17,1},{25,9},{2,18},{10... | collective-permute-start | bytes 1572872 | tf_op jit(solution)/shard_map/ppermute | solution.py:537
  139.7 21.3 %collective-permute-start.20 = (bf16[256,512]{1,0:T(8,128)(2,1)S(1)}, bf16[256,512]{1,0:T(8,128)(2,1)S(1)}, u32[]{:S(2)}, u32[]{:S(2)}) collective-permute-start(bf16[256,512]{1,0:T(8,128)(2,1)S(1)} %add_convert_fusion), channel_id=1, source_target_pairs={{0,4},{1,5},{2,6},{3,7},{4,0},{5,1},{6,2},{7,3},{8,12},{9,13},{10,... | collective-permute-start | bytes 786440 | tf_op jit(solution)/shard_map/ppermute | solution.py:478
  147.1 17.6 %collective-permute-start.19 = (bf16[256,512]{1,0:T(8,128)(2,1)S(1)}, bf16[256,512]{1,0:T(8,128)(2,1)}, u32[]{:S(2)}, u32[]{:S(2)}) collective-permute-start(bf16[256,512]{1,0:T(8,128)(2,1)S(1)} %add_convert_fusion.1), channel_id=1, source_target_pairs={{0,4},{1,5},{2,6},{3,7},{4,0},{5,1},{6,2},{7,3},{8,12},{9,13},{10,... | collective-permute-start | bytes 786440 | tf_op jit(solution)/shard_map/ppermute | solution.py:478
  (19 other events, 179.2 us)

commit v4 on v3

v4 whole, which is shorter than its diff:
```python
import math

import jax
import jax.numpy as jnp
from jax import lax
from jax.experimental import pallas as pl
from jax.experimental.pallas import tpu as pltpu
from jax.sharding import PartitionSpec as P

D = 8192
QH = 32
KVH = 4
HD = 128
GROUP = QH // KVH
WIDE = GROUP * HD
TILE = 256
NEGATIVE = -1e30
BF16 = jnp.bfloat16
F32 = jnp.float32
VMEM_BYTES = 24 * 1024 * 1024
ALL_VMEM_BYTES = 62 * 1024 * 1024

NT = (((1,), (1,)), ((), ()))


def pack_kernel(rows, groups, halves, *refs):
    q_hbm, do_hbm, k_hbm, v_hbm, x_hbm, kv_out = refs[:6]
    piece_out = refs[6 : 5 + KVH]
    give_out, kv_s, piece_s, give_s, sems, out_sems = refs[5 + KVH :]
    head = lax.axis_index("seq") % KVH
    core = lax.axis_index("dp") % 2
    width = give_s.shape[1] // halves

    def of(index, block):
        return pl.ds(pl.multiple_of(index * block, block), block)

    loads = []

    def load(copies):
        made = []
        for source, target in copies:
            made.append(pltpu.make_async_copy(source, target, sems.at[len(loads)]))
            made[-1].start()
            loads.append(made[-1])
        return made

    small = load(
        (
            array.at[:, k * HD : (k + 1) * HD],
            kv_s.at[group * KVH + k, :, kind * HD : (kind + 1) * HD],
        )
        for k in range(KVH)
        for group in range(groups)
        for kind, array in enumerate((k_hbm, v_hbm))
    )
    large = [
        load(
            (
                array.at[:, of(head ^ k, WIDE)],
                piece_s.at[k - 1, :, kind * WIDE : (kind + 1) * WIDE],
            )
            for kind, array in enumerate((q_hbm, do_hbm))
        )
        for k in range(1, KVH)
    ]
    give = load(
        (
            x_hbm.at[:, of(2 * half + 1 - core, width)],
            give_s.at[:, half * width : (half + 1) * width],
        )
        for half in range(halves)
    )
    outs = []

    def pass_on(copies, source, target):
        for copy in copies:
            copy.wait()
        outs.append(pltpu.make_async_copy(source, target, out_sems.at[len(outs)]))
        outs[-1].start()

    pass_on(small, kv_s, kv_out)
    for k in range(1, KVH):
        pass_on(large[k - 1], piece_s.at[k - 1], piece_out[k - 1])
    pass_on(give, give_s, give_out)
    for copy in outs:
        copy.wait()


def packed(rows, groups, halves, queries, out_grad, key_states, value_states, layer_input):
    any_spec = pl.BlockSpec(memory_space=pltpu.HBM)
    cycle = KVH * groups
    outs = pl.pallas_call(
        lambda *refs: pack_kernel(rows, groups, halves, *refs),
        out_shape=[jax.ShapeDtypeStruct((cycle, rows, 2 * HD), BF16)]
        + [jax.ShapeDtypeStruct((rows, 2 * WIDE), BF16)] * (KVH - 1)
        + [jax.ShapeDtypeStruct((rows, D // 2), BF16)],
        in_specs=[any_spec] * 5,
        out_specs=[any_spec] * (KVH + 1),
        scratch_shapes=[
            pltpu.VMEM((cycle, rows, 2 * HD), BF16),
            pltpu.VMEM((KVH - 1, rows, 2 * WIDE), BF16),
            pltpu.VMEM((rows, D // 2), BF16),
            pltpu.SemaphoreType.DMA((2 * cycle + 2 * KVH + halves,)),
            pltpu.SemaphoreType.DMA((KVH + 1,)),
        ],
        compiler_params=pltpu.CompilerParams(vmem_limit_bytes=ALL_VMEM_BYTES),
        cost_estimate=pl.CostEstimate(flops=0, bytes_accessed=8 * 10**6, transcendentals=0),
        name="first_sends",
    )(queries, out_grad, key_states, value_states, layer_input)
    return outs[0], outs[1:KVH], outs[KVH]


def column_blocks(halves, groups, k):
    place = lax.axis_index("seq")
    group = place // KVH
    head = place % KVH
    half = lax.axis_index("dp") // 2
    core = lax.axis_index("dp") % 2
    blocks = []
    for apart in range(halves):
        for step in range(groups):
            mine = (((half ^ apart) * 2 + core) * groups + (group ^ step)) * KVH + (head ^ k)
            given = ((half ^ apart) * groups + (group ^ step)) * KVH + (head ^ k)
            blocks.append((mine, given))
    return blocks


def column_kernel(rows, halves, groups, slab, *refs):
    x_hbm, given_hbm = refs[:2]
    outs = refs[2 : 2 + KVH]
    x_s, sems, out_sems = refs[2 + KVH :]
    loads = []
    for k in range(KVH):
        for b, places in enumerate(column_blocks(halves, groups, k)):
            for which, source in enumerate((x_hbm, given_hbm)):
                loads.append(
                    pltpu.make_async_copy(
                        source.at[:, pl.ds(pl.multiple_of(places[which] * slab, slab), slab)],
                        x_s.at[k, which * rows : (which + 1) * rows, b * slab : (b + 1) * slab],
                        sems.at[len(loads)],
                    )
                )
    for load in loads:
        load.start()
    stores = []
    each = len(loads) // KVH
    for k in range(KVH):
        for load in loads[k * each : (k + 1) * each]:
            load.wait()
        stores.append(pltpu.make_async_copy(x_s.at[k], outs[k], out_sems.at[k]))
        stores[-1].start()
    for store in stores:
        store.wait()


def columns_for_group(rows, halves, groups, slab, layer_input, given):
    width = halves * groups * slab
    if slab % HD:
        return [
            jnp.concatenate(
                [
                    jnp.concatenate(
                        [
                            lax.dynamic_slice_in_dim(array, places[which] * slab, slab, 1)
                            for places in column_blocks(halves, groups, k)
                        ],
                        axis=1,
                    )
                    for which, array in enumerate((layer_input, given))
                ],
                axis=0,
            )
            for k in range(KVH)
        ]
    any_spec = pl.BlockSpec(memory_space=pltpu.HBM)
    return pl.pallas_call(
        lambda *refs: column_kernel(rows, halves, groups, slab, *refs),
        out_shape=[jax.ShapeDtypeStruct((2 * rows, width), BF16)] * KVH,
        in_specs=[any_spec] * 2,
        out_specs=[any_spec] * KVH,
        scratch_shapes=[
            pltpu.VMEM((KVH, 2 * rows, width), BF16),
            pltpu.SemaphoreType.DMA((2 * KVH * halves * groups,)),
            pltpu.SemaphoreType.DMA((KVH,)),
        ],
        compiler_params=pltpu.CompilerParams(vmem_limit_bytes=ALL_VMEM_BYTES),
        cost_estimate=pl.CostEstimate(flops=0, bytes_accessed=8 * 10**6, transcendentals=0),
        name="input_columns",
    )(layer_input, given)


def attention_kernel(rows, groups, *refs):
    span = KVH * rows
    q_hbm, do_hbm, kv_hbm = refs[:3]
    pieces = refs[3 : 3 + KVH - 1]
    at = 3 + KVH - 1
    dq_out = refs[at]
    at += 1
    own_out = refs[at]
    at += 1
    down_out = refs[at : at + groups - 1]
    at += groups - 1
    q_s, do_s, k_s, v_s, kt_s, dk_s, dv_s, down_s, sems = refs[at:]

    place = lax.axis_index("seq")
    group = place // KVH
    head = place % KVH

    def row_at(k, base=0):
        return pl.ds(pl.multiple_of(base + (head ^ k) * rows, rows), rows)

    def column_at(block):
        return pl.ds(pl.multiple_of(head * block, block), block)

    copies = [
        pltpu.make_async_copy(q_hbm.at[:, column_at(WIDE)], q_s.at[row_at(0)], sems.at[0]),
        pltpu.make_async_copy(do_hbm.at[:, column_at(WIDE)], do_s.at[row_at(0)], sems.at[1]),
    ]
    for kind, target in enumerate((k_s, v_s)):
        copies += [
            pltpu.make_async_copy(
                kv_hbm.at[source, :, kind * HD : (kind + 1) * HD],
                target.at[source * rows : (source + 1) * rows],
                sems.at[2 * KVH + 2 * source + kind],
            )
            for source in range(KVH * groups)
        ]
    for k in range(1, KVH):
        piece = pieces[k - 1]
        copies += [
            pltpu.make_async_copy(piece.at[:, :WIDE], q_s.at[row_at(k)], sems.at[2 * k]),
            pltpu.make_async_copy(piece.at[:, WIDE:], do_s.at[row_at(k)], sems.at[2 * k + 1]),
        ]
    for copy in copies:
        copy.start()
    for copy in copies:
        copy.wait()

    dk_s[...] = jnp.zeros_like(dk_s)
    dv_s[...] = jnp.zeros_like(dv_s)
    scale = 1.0 / math.sqrt(HD)
    fold = scale * math.log2(math.e)

    for which in range(groups):

        @pl.when(group == which)
        def _(which=which):
            for block in range((which + 1) * span // TILE):
                keys = slice(block * TILE, (block + 1) * TILE)
                kt_s[:, keys] = k_s[keys, :].T

            def one_head(h, carry):
                columns = pl.ds(pl.multiple_of(h * HD, HD), HD)
                for part in range(span // TILE):
                    q = q_s[part * TILE : (part + 1) * TILE, columns]
                    do = do_s[part * TILE : (part + 1) * TILE, columns]
                    length = which * span + (part + 1) * TILE
                    blocks = length // TILE
                    scores = []
                    grads = []
                    for b in range(blocks):
                        keys = slice(b * TILE, (b + 1) * TILE)
                        one = lax.dot_general(k_s[keys, :], q, NT, preferred_element_type=F32)
                        if b == blocks - 1:
                            key_place = lax.broadcasted_iota(jnp.int32, (TILE, TILE), 0)
                            query_place = lax.broadcasted_iota(jnp.int32, (TILE, TILE), 1)
                            one = jnp.where(key_place <= query_place, one, NEGATIVE)
                        scores.append(one)
                        grads.append(
                            lax.dot_general(v_s[keys, :], do, NT, preferred_element_type=F32)
                        )
                    top = scores[0].max(axis=0, keepdims=True)
                    for one in scores[1:]:
                        top = jnp.maximum(top, one.max(axis=0, keepdims=True))
                    expon = [jnp.exp2((one - top) * fold) for one in scores]
                    denom = sum(e.sum(axis=0, keepdims=True) for e in expon)
                    weighted = sum(
                        (e * gp).sum(axis=0, keepdims=True) for e, gp in zip(expon, grads)
                    )
                    inverse = 1.0 / denom
                    delta = weighted * inverse
                    probs = jnp.concatenate([(e * inverse).astype(BF16) for e in expon], axis=0)
                    grad_scores = jnp.concatenate(
                        [
                            (e * (inverse * scale) * (gp - delta)).astype(BF16)
                            for e, gp in zip(expon, grads)
                        ],
                        axis=0,
                    )
                    dv_s[:length, :] += jnp.dot(probs, do, preferred_element_type=F32)
                    dk_s[:length, :] += jnp.dot(grad_scores, q, preferred_element_type=F32)
                    dqt = jnp.dot(kt_s[:, :length], grad_scores, preferred_element_type=F32)
                    dq_out[part * TILE : (part + 1) * TILE, columns] = dqt.T.astype(BF16)
                return carry

            lax.fori_loop(0, GROUP, one_head, 0)
            base = which * span
            own_out[:, :HD] = dk_s[base : base + span, :]
            own_out[:, HD:] = dv_s[base : base + span, :]
            for step in range(1, which + 1):
                source = (which - step) * span
                down_s[step - 1, :, :HD] = dk_s[source : source + span, :].astype(BF16)
                down_s[step - 1, :, HD:] = dv_s[source : source + span, :].astype(BF16)
            for step in range(which + 1, groups):
                down_s[step - 1] = jnp.zeros((span, 2 * HD), BF16)

    outs = [
        pltpu.make_async_copy(down_s.at[step], down_out[step], sems.at[step])
        for step in range(groups - 1)
    ]
    for copy in outs:
        copy.start()
    for copy in outs:
        copy.wait()


def attention(rows, groups, queries, out_grad, keys_values, pieces):
    span = KVH * rows
    length = groups * span
    any_spec = pl.BlockSpec(memory_space=pltpu.HBM)
    n_in = 3 + len(pieces)
    out_shape = (
        [jax.ShapeDtypeStruct((span, WIDE), BF16)]
        + [jax.ShapeDtypeStruct((span, 2 * HD), F32)]
        + [jax.ShapeDtypeStruct((span, 2 * HD), BF16)] * (groups - 1)
    )
    out_specs = (
        [pl.BlockSpec(memory_space=pltpu.VMEM)] * 2
        + [any_spec] * (groups - 1)
    )
    outs = pl.pallas_call(
        lambda *refs: attention_kernel(rows, groups, *refs),
        out_shape=out_shape,
        in_specs=[any_spec] * n_in,
        out_specs=out_specs,
        scratch_shapes=[
            pltpu.VMEM((span, WIDE), BF16),
            pltpu.VMEM((span, WIDE), BF16),
            pltpu.VMEM((length, HD), BF16),
            pltpu.VMEM((length, HD), BF16),
            pltpu.VMEM((HD, length), BF16),
            pltpu.VMEM((length, HD), F32),
            pltpu.VMEM((length, HD), F32),
            pltpu.VMEM((max(groups - 1, 1), span, 2 * HD), BF16),
            pltpu.SemaphoreType.DMA((2 * KVH + 2 * KVH * groups,)),
        ],
        compiler_params=pltpu.CompilerParams(vmem_limit_bytes=ALL_VMEM_BYTES),
        cost_estimate=pl.CostEstimate(flops=10**10, bytes_accessed=5 * 10**7, transcendentals=0),
        name="attention",
    )(queries, out_grad, keys_values, *pieces)
    return outs[0], outs[1], outs[2:]


def weight_kernel(rows, halves, groups, slab, *refs):
    own = refs[:KVH]
    other = refs[KVH : 2 * KVH]
    x = refs[2 * KVH : 3 * KVH]
    keep, same = refs[3 * KVH : 3 * KVH + 2]
    at = 3 * KVH + 2
    away = (refs[at : at + groups - 1], refs[at + groups - 1 : at + 2 * groups - 2])
    mine_out = refs[at + 2 * groups - 2 : at + 2 * groups]
    g_s = refs[-1]
    width = KVH * HD
    head = lax.axis_index("seq") % KVH
    mine = pl.ds(pl.multiple_of(head * rows, rows), rows)
    for k in range(KVH):
        for kind in range(2):
            part = slice(kind * HD, (kind + 1) * HD)
            columns = pl.ds(pl.multiple_of((head ^ k) * HD, HD), HD)
            wide = pl.ds(pl.multiple_of(kind * width + (head ^ k) * HD, HD), HD)
            mine_out[kind][:, columns] = own[k][mine, part]
            for far in range(KVH):
                lines = pl.ds(pl.multiple_of((head ^ far) * rows, rows), rows)
                first = 2 * far * rows
                g_s[first : first + rows, wide] = own[k][lines, part]
                g_s[first + rows : first + 2 * rows, wide] = other[k][lines, part]
    for apart in range(halves - 1, -1, -1):
        for step in range(groups - 1, -1, -1):
            block = (apart * groups + step) * slab
            left = jnp.concatenate([x[k][:, block : block + slab].T for k in range(KVH)], axis=1)
            product = jnp.dot(left, g_s[...], preferred_element_type=F32)
            lines = slice((apart - 1) * slab, apart * slab)
            if apart == 0:
                keep[step * slab : (step + 1) * slab, :] = product
            elif step == 0:
                same[lines, :] = product.astype(BF16)
            else:
                for kind in range(2):
                    away[kind][step - 1][lines, :] = product[
                        :, kind * width : (kind + 1) * width
                    ].astype(BF16)


def weight_terms(rows, halves, groups, slab, own, other, inputs):
    span = KVH * rows
    channels = KVH * HD
    vmem = pl.BlockSpec(memory_space=pltpu.VMEM)
    others = max(halves - 1, 1) * slab
    outs = pl.pallas_call(
        lambda *refs: weight_kernel(rows, halves, groups, slab, *refs),
        out_shape=[
            jax.ShapeDtypeStruct((groups * slab, 2 * channels), F32),
            jax.ShapeDtypeStruct((others, 2 * channels), BF16),
        ]
        + [jax.ShapeDtypeStruct((others, channels), BF16)] * (2 * (groups - 1))
        + [jax.ShapeDtypeStruct((rows, channels), BF16)] * 2,
        in_specs=[vmem] * (3 * KVH),
        out_specs=[vmem] * (2 * groups + 2),
        scratch_shapes=[pltpu.VMEM((2 * span, 2 * channels), BF16)],
        compiler_params=pltpu.CompilerParams(vmem_limit_bytes=VMEM_BYTES),
        cost_estimate=pl.CostEstimate(flops=3 * 10**9, bytes_accessed=6 * 10**6, transcendentals=0),
        name="weight_terms",
    )(*own, *other, *inputs)
    at = groups - 1
    away = outs[2 : 2 + 2 * at]
    return outs[0], outs[1], (away[:at], away[at:]), outs[2 + 2 * at :]


def place_kernel(pieces, out):
    for head in range(KVH):
        out[:, head * WIDE : (head + 1) * WIDE] = pieces[head]


def placed(rows, pieces):
    vmem = pl.BlockSpec(memory_space=pltpu.VMEM)
    return pl.pallas_call(
        place_kernel,
        out_shape=jax.ShapeDtypeStruct((rows, QH * HD), BF16),
        in_specs=[vmem],
        out_specs=vmem,
        compiler_params=pltpu.CompilerParams(vmem_limit_bytes=VMEM_BYTES),
        cost_estimate=pl.CostEstimate(flops=0, bytes_accessed=5 * 10**6, transcendentals=0),
        name="query_grad_placed",
    )(pieces)


def add_kernel(kind, step, keep, *refs):
    out = refs[-1]
    slab, width = out.shape
    total = keep[step * slab : (step + 1) * slab, kind * width : (kind + 1) * width]
    for ref in refs[:-1]:
        total = total + ref[...].astype(F32)
    out[...] = total.astype(BF16)


def added(keep, parts, kind, step):
    vmem = pl.BlockSpec(memory_space=pltpu.VMEM)
    return pl.pallas_call(
        lambda *refs: add_kernel(kind, step, *refs),
        out_shape=jax.ShapeDtypeStruct(parts[0].shape, BF16),
        in_specs=[vmem] * (1 + len(parts)),
        out_specs=vmem,
        compiler_params=pltpu.CompilerParams(vmem_limit_bytes=VMEM_BYTES),
        cost_estimate=pl.CostEstimate(flops=0, bytes_accessed=10**6, transcendentals=0),
        name="sequences_added",
    )(keep, *parts)


def join_kernel(wide, *refs):
    keep = refs[0]
    both = refs[1 : 1 + wide]
    out = refs[-1]
    rest = refs[1 + wide : -1]
    count = len(rest) // 2
    slab, width = out.shape[0], out.shape[1] // 2
    for kind in range(2):
        at = slice(kind * width, (kind + 1) * width)
        total = keep[:slab, at]
        for ref in both:
            total = total + ref[:, at].astype(F32)
        for ref in rest[kind * count : (kind + 1) * count]:
            total = total + ref[...].astype(F32)
        out[:, at] = total


def joined(slab, keep, both, rest):
    vmem = pl.BlockSpec(memory_space=pltpu.VMEM)
    return pl.pallas_call(
        lambda *refs: join_kernel(len(both), *refs),
        out_shape=jax.ShapeDtypeStruct((slab, keep.shape[1]), F32),
        in_specs=[vmem] * (1 + len(both) + len(rest)),
        out_specs=vmem,
        compiler_params=pltpu.CompilerParams(vmem_limit_bytes=VMEM_BYTES),
        cost_estimate=pl.CostEstimate(flops=0, bytes_accessed=3 * 10**6, transcendentals=0),
        name="weight_grad_joined",
    )(keep, *both, *rest)


def local(layer_input, queries, key_states, value_states, out_grad):
    rows = layer_input.shape[0]
    cycle = lax.axis_size("seq")
    replicas = lax.axis_size("dp")
    groups = cycle // KVH
    halves = replicas // 2
    slab = D // (replicas * cycle)
    after = lax.optimization_barrier
    within = [[i + k for k in range(KVH)] for i in range(0, cycle, KVH)]

    def swap(array, k):
        return lax.ppermute(array, "seq", [(i, i ^ k) for i in range(cycle)])

    def across_cores(array):
        return lax.ppermute(array, "dp", [(i, i ^ 1) for i in range(replicas)])

    def exchange(array, parts=None):
        return lax.all_to_all(
            array, "seq", split_axis=0, concat_axis=0, tiled=True, axis_index_groups=parts
        )

    keys_values, sends, give = packed(
        rows, groups, halves, queries, out_grad, key_states, value_states, layer_input
    )
    keys_values = exchange(keys_values)
    pieces = [None] * KVH
    for k in range(KVH - 1, 0, -1):
        pieces[k] = swap(sends[k - 1], k)
    pieces = pieces[1:]

    columns = columns_for_group(rows, halves, groups, slab, layer_input, across_cores(give))
    columns, pieces = after((columns, pieces))
    inputs = [columns[0], None] + [swap(columns[k], k) for k in range(2, KVH)]

    grads, own, down = attention(rows, groups, queries, out_grad, keys_values, pieces)
    columns, inputs[2:], down = after((columns, inputs[2:], down))
    inputs[1] = swap(columns[1], 1)

    received = [
        lax.ppermute(
            down[step - 1], "seq", [(i + step * KVH, i) for i in range(cycle - step * KVH)]
        )
        for step in range(1, groups)
    ]
    received, inputs[1] = after((received, inputs[1]))
    total = own
    for part in received:
        total = total + part.astype(F32)
    total = total.astype(BF16)
    gathered = [total] + [swap(total, k) for k in range(1, KVH)]
    others = [across_cores(piece) for piece in gathered]
    keep, same, away, narrow = weight_terms(
        rows, halves, groups, slab, gathered, others, inputs
    )

    def over_sequences(array):
        return [
            lax.ppermute(
                array[(apart - 1) * slab : apart * slab],
                "dp",
                [(i, i ^ (2 * apart)) for i in range(replicas)],
            )
            for apart in range(1, halves)
        ]

    parts = [[over_sequences(array) for array in away[kind]] for kind in range(2)]
    rest = [[], []]
    for kind in (1, 0):
        totals = [
            added(keep, parts[kind][step - 1], kind, step) for step in range(1, groups)
        ]
        rest[kind] = [swap(total, (step + 1) * KVH) for step, total in enumerate(totals)]
    weight_grad = joined(slab, keep, over_sequences(same), rest[0] + rest[1])

    returned = exchange(grads.reshape(KVH, rows, WIDE), within)
    query_grad = placed(rows, returned)
    return (query_grad, narrow[0], narrow[1], weight_grad)


def solution(mesh):
    spec = P(("dp", "seq"), None)
    return jax.shard_map(
        local, mesh=mesh, in_specs=(spec,) * 5, out_specs=(spec,) * 4, check_vma=False
    )
```

time: 172 us -> 154 us (0.90)
  Pallas kernels: 35.4 us -> 27.7 us
  starting transfers between devices: 38.3 us -> 32.8 us
  waiting for transfers between devices: 89.2 us -> 84.8 us
  other arithmetic: 3.49 us -> 0.06 us
  local copies, waits for them, and re-layouts: 4.53 us -> 6.73 us
    pallas_call x4 -> x5, Pallas kernels: 16.2 us -> 10.5 us  [the longest x1 3.25 us: packed(): pl.pallas_call(lambda *refs: pack_kernel(rows, groups, halves, *refs), ou...]
    ppermute x14 -> x11, starting transfers between devices: 21.9 us -> 16.5 us  [swap(): return lax.ppermute(array, 'seq', [(i, i ^ k) for i in range(cycle)])]
    ppermute x3, waiting for transfers between devices: 13.6 us -> 8.75 us  [over_sequences(): lax.ppermute(array[(apart - 1) * slab:apart * slab], 'dp', [(i, i ^ 2 * a...]
    ppermute x1, waiting for transfers between devices: 14.3 us -> 10.3 us  [local(): lax.ppermute(down[step - 1], 'seq', [(i + step * KVH, i) for i in range(c...]
    ppermute x14 -> x11, waiting for transfers between devices: 61.3 us -> 64.4 us  [swap(): return lax.ppermute(array, 'seq', [(i, i ^ k) for i in range(cycle)])]
    convert_element_type x2 -> x0, other arithmetic: 2.23 us -> none  [local(): rest.append(swap(total.astype(BF16), step * KVH))]
    unnamed x40 -> x20, local copies, waits for them, and re-layouts: 4.53 us -> 6.73 us
  transfers between devices with their start and end apart: 23 -> 22, of which waited for: 15 -> 14; matrix products, arithmetic and copies ran while one was open for 2% -> 0% of each run, Pallas kernels for 15% -> 15%
where the time goes in v4:
time: 154 us; the launch traced here: 153 us
  waiting for transfers between devices  84.8 us (55%)
  starting transfers between devices  32.8 us (21%)
  Pallas kernels  27.7 us (18%)
  local copies, waits for them, and re-layouts  6.73 us (4%)
    ppermute x11, waiting for transfers between devices, swap(): return lax.ppermute(array, 'seq', [(i, i ^ k) for i in range(cycle)])  64.4 us
    ppermute x11, starting transfers between devices, swap(): return lax.ppermute(array, 'seq', [(i, i ^ k) for i in range(cycle)])  16.5 us
    pallas_call x1, Pallas kernels, attention(): pl.pallas_call(lambda *refs: attention_kernel(rows, groups, *refs), out_s...  14 us
    all_to_all x2, starting transfers between devices, exchange(): lax.all_to_all(array, 'seq', split_axis=0, concat_axis=0, tiled=True, axi...  10.4 us
    ppermute x1, waiting for transfers between devices, local(): lax.ppermute(down[step - 1], 'seq', [(i + step * KVH, i) for i in range(c...  10.3 us
    ppermute x3, waiting for transfers between devices, over_sequences(): lax.ppermute(array[(apart - 1) * slab:apart * slab], 'dp', [(i, i ^ 2 * a...  8.75 us
    unnamed x20, local copies, waits for them, and re-layouts  6.73 us
    ppermute x3, starting transfers between devices, over_sequences(): lax.ppermute(array[(apart - 1) * slab:apart * slab], 'dp', [(i, i ^ 2 * a...  3.62 us
  transfers between devices with their start and end apart: 22, of which 14 were waited for; matrix products, arithmetic and copies ran while one was open for 0% of the time, Pallas kernels for 15%

profile of v4, /device:TPU:0, one launch (start us, length us, event | category | flops | bytes accessed | tf_op | source)
XLA Modules:
  0.0 152.9 jit_solution(16859000201238614178)
XLA Ops:
  0.6 3.2 %first_sends.1 = (bf16[8,128,256]{2,1,0:T(8,128)(2,1)}, bf16[128,2048]{1,0:T(8,128)(2,1)}, bf16[128,2048]{1,0:T(8,128)(2,1)}, bf16[128,2048]{1,0:T(8,128)(2,1)}, bf16[128,4096]{1,0:T(8,128)(2,1)}) custom-call(bf16[128,4096]{1,0:T(8,128)(2,1)} %refs_0_.5, bf16[128,4096]{1,0:T(8,128)(2,1)} %refs_1_.3, bf16[128,512]{1,0:T(8,128)(2,1)} %refs_2_.1, ...), custom_call_target="tpu_custom_call" | custom-call | bytes 8000000 | tf_op jit(solution)/shard_map/first_sends/pallas_call | solution.py:92
  4.4 6.8 %all-to-all-start = ((bf16[8,128,256]{2,1,0:T(8,128)(2,1)}), bf16[8,128,256]{2,1,0:T(8,128)(2,1)S(1)}, u32[]{:S(2)}, u32[]{:S(2)}) async-start(bf16[8,128,256]{2,1,0:T(8,128)(2,1)} %get-tuple-element.35), calls=%async_computation | async-start | bytes 1048576 | tf_op jit(solution)/shard_map/all_to_all | solution.py:506
  11.2 2.0 %collective-permute-start.1 = (bf16[128,2048]{1,0:T(8,128)(2,1)}, bf16[128,2048]{1,0:T(8,128)(2,1)}, u32[]{:S(2)}, u32[]{:S(2)}) collective-permute-start(bf16[128,2048]{1,0:T(8,128)(2,1)} %get-tuple-element.41), channel_id=1, source_target_pairs={{0,1},{1,0},{2,3},{3,2},{4,5},{5,4},{6,7},{7,6},{8,9},{9,8},{10,11... | collective-permute-start | bytes 1572872 | tf_op jit(solution)/shard_map/ppermute | solution.py:500
  15.7 2.7 %input_columns.1 = (bf16[256,1024]{1,0:T(8,128)(2,1)}, bf16[256,1024]{1,0:T(8,128)(2,1)}, bf16[256,1024]{1,0:T(8,128)(2,1)}, bf16[256,1024]{1,0:T(8,128)(2,1)}) custom-call(bf16[128,8192]{1,0:T(8,128)(2,1)} %refs_0_.4, bf16[128,4096]{1,0:T(8,128)(2,1)} %copy-done.7), custom_call_target="tpu_custom_call" | custom-call | bytes 8000000 | tf_op jit(solution)/shard_map/input_columns/pallas_call | solution.py:176
  18.5 12.7 %collective-permute-done.1.refs_3_ = bf16[128,2048]{1,0:T(8,128)(2,1)} collective-permute-done((bf16[128,2048]{1,0:T(8,128)(2,1)}, bf16[128,2048]{1,0:T(8,128)(2,1)}, u32[]{:S(2)}, u32[]{:S(2)}) %collective-permute-start.1) | collective-permute-done | bytes 524320 | tf_op jit(solution)/shard_map/ppermute | solution.py:500
  31.2 3.5 %collective-permute-done.2.refs_4_ = bf16[128,2048]{1,0:T(8,128)(2,1)} collective-permute-done((bf16[128,2048]{1,0:T(8,128)(2,1)}, bf16[128,2048]{1,0:T(8,128)(2,1)}, u32[]{:S(2)}, u32[]{:S(2)}) %collective-permute-start.2) | collective-permute-done | bytes 524320 | tf_op jit(solution)/shard_map/ppermute | solution.py:500
  34.7 11.4 %collective-permute-done.3.refs_5_ = bf16[128,2048]{1,0:T(8,128)(2,1)} collective-permute-done((bf16[128,2048]{1,0:T(8,128)(2,1)}, bf16[128,2048]{1,0:T(8,128)(2,1)}, u32[]{:S(2)}, u32[]{:S(2)}) %collective-permute-start.3) | collective-permute-done | bytes 524320 | tf_op jit(solution)/shard_map/ppermute | solution.py:500
  49.0 14.0 %attention.1 = (bf16[512,1024]{1,0:T(8,128)(2,1)}, f32[512,256]{1,0:T(8,128)}, bf16[512,256]{1,0:T(8,128)(2,1)}) custom-call(bf16[128,4096]{1,0:T(8,128)(2,1)} %refs_0_.5, bf16[128,4096]{1,0:T(8,128)(2,1)} %refs_1_.3, bf16[8,128,256]{2,1,0:T(8,128)(2,1)} %copy-done.8, bf16[128,2048]{1,0:T(8,128)(2,1)} %collective-permute-done.1.refs_3_, ...), custom_call_target="tpu_custom_call" | custom-call | flops 10000000000 | bytes 50000000 | tf_op jit(solution)/shard_map/attention/pallas_call | solution.py:331
  63.0 7.8 %collective-permute-done.5.refs_11_ = bf16[256,1024]{1,0:T(8,128)(2,1)S(1)} collective-permute-done((bf16[256,1024]{1,0:T(8,128)(2,1)}, bf16[256,1024]{1,0:T(8,128)(2,1)S(1)}, u32[]{:S(2)}, u32[]{:S(2)}) %collective-permute-start.5) | collective-permute-done | bytes 524320 | tf_op jit(solution)/shard_map/ppermute | solution.py:500
  74.3 3.5 %all-to-all-start.1 = ((bf16[4,128,1024]{2,1,0:T(8,128)(2,1)}), bf16[4,128,1024]{2,1,0:T(8,128)(2,1)S(1)}, u32[]{:S(2)}, u32[]{:S(2)}) async-start(bf16[4,128,1024]{2,1,0:T(8,128)(2,1)} %bitcast.1), calls=%async_computation.1 | async-start | bytes 2097152 | tf_op jit(solution)/shard_map/all_to_all | solution.py:506
  77.9 10.3 %collective-permute-done.6 = bf16[512,256]{1,0:T(8,128)(2,1)S(1)} collective-permute-done((bf16[512,256]{1,0:T(8,128)(2,1)}, bf16[512,256]{1,0:T(8,128)(2,1)S(1)}, u32[]{:S(2)}, u32[]{:S(2)}) %collective-permute-start.6) | collective-permute-done | bytes 262176 | tf_op jit(solution)/shard_map/ppermute | solution.py:528
  88.1 3.1 %collective-permute-done.7.refs_9_ = bf16[256,1024]{1,0:T(8,128)(2,1)S(1)} collective-permute-done((bf16[256,1024]{1,0:T(8,128)(2,1)}, bf16[256,1024]{1,0:T(8,128)(2,1)S(1)}, u32[]{:S(2)}, u32[]{:S(2)}) %collective-permute-start.7) | collective-permute-done | bytes 524320 | tf_op jit(solution)/shard_map/ppermute | solution.py:500
  91.3 5.4 %collective-permute-start.10 = (bf16[512,256]{1,0:T(8,128)(2,1)S(1)}, bf16[512,256]{1,0:T(8,128)(2,1)S(1)}, u32[]{:S(2)}, u32[]{:S(2)}) collective-permute-start(bf16[512,256]{1,0:T(8,128)(2,1)S(1)} %add_convert_fusion.refs_0_), channel_id=1, source_target_pairs={{0,3},{1,2},{2,1},{3,0},{4,7},{5,6},{6,5},{7,4},{8,11},{9,10},{10,... | collective-permute-start | bytes 786440 | tf_op jit(solution)/shard_map/ppermute | solution.py:500
  97.4 7.1 %collective-permute-done.10.refs_3_ = bf16[512,256]{1,0:T(8,128)(2,1)S(1)} collective-permute-done((bf16[512,256]{1,0:T(8,128)(2,1)S(1)}, bf16[512,256]{1,0:T(8,128)(2,1)S(1)}, u32[]{:S(2)}, u32[]{:S(2)}) %collective-permute-start.10) | collective-permute-done | bytes 262176 | tf_op jit(solution)/shard_map/ppermute | solution.py:500
  104.5 2.3 %collective-permute-done.9.refs_2_ = bf16[512,256]{1,0:T(8,128)(2,1)S(1)} collective-permute-done((bf16[512,256]{1,0:T(8,128)(2,1)S(1)}, bf16[512,256]{1,0:T(8,128)(2,1)S(1)}, u32[]{:S(2)}, u32[]{:S(2)}) %collective-permute-start.9) | collective-permute-done | bytes 262176 | tf_op jit(solution)/shard_map/ppermute | solution.py:500
  112.9 3.0 %weight_terms.1 = (f32[512,1024]{1,0:T(8,128)S(1)}, bf16[256,1024]{1,0:T(8,128)(2,1)}, bf16[256,512]{1,0:T(8,128)(2,1)S(1)}, bf16[256,512]{1,0:T(8,128)(2,1)S(1)...) custom-call(bf16[512,256]{1,0:T(8,128)(2,1)S(1)} %add_convert_fusion.refs_0_, ...), custom_call_target="tpu_custom_call" | custom-call | flops 3000000000 | bytes 6000000 | tf_op jit(solution)/shard_map/weight_terms/pallas_call | solution.py:399
  115.9 1.6 %collective-permute-start.16 = (bf16[256,512]{1,0:T(8,128)(2,1)S(1)}, bf16[256,512]{1,0:T(8,128)(2,1)S(1)}, u32[]{:S(2)}, u32[]{:S(2)}) collective-permute-start(bf16[256,512]{1,0:T(8,128)(2,1)S(1)} %get-tuple-element.64), channel_id=1, source_target_pairs={{0,16},{8,24},{16,0},{24,8},{1,17},{9,25},{17,1},{25,9},{2,18},{10... | collective-permute-start | bytes 786440 | tf_op jit(solution)/shard_map/ppermute | solution.py:546
  119.5 5.6 %collective-permute-done.16.refs_1_ = bf16[256,512]{1,0:T(8,128)(2,1)S(1)} collective-permute-done((bf16[256,512]{1,0:T(8,128)(2,1)S(1)}, bf16[256,512]{1,0:T(8,128)(2,1)S(1)}, u32[]{:S(2)}, u32[]{:S(2)}) %collective-permute-start.16) | collective-permute-done | bytes 262176 | tf_op jit(solution)/shard_map/ppermute | solution.py:546
  125.9 1.7 %collective-permute-start.17 = (bf16[256,512]{1,0:T(8,128)(2,1)}, bf16[256,512]{1,0:T(8,128)(2,1)S(1)}, u32[]{:S(2)}, u32[]{:S(2)}) collective-permute-start(bf16[256,512]{1,0:T(8,128)(2,1)} %sequences_added.2), channel_id=1, source_target_pairs={{0,4},{1,5},{2,6},{3,7},{4,0},{5,1},{6,2},{7,3},{8,12},{9,13},{10,... | collective-permute-start | bytes 786440 | tf_op jit(solution)/shard_map/ppermute | solution.py:500
  127.6 3.2 %collective-permute-done.18.refs_1_ = bf16[256,512]{1,0:T(8,128)(2,1)S(1)} collective-permute-done((bf16[256,512]{1,0:T(8,128)(2,1)S(1)}, bf16[256,512]{1,0:T(8,128)(2,1)S(1)}, u32[]{:S(2)}, u32[]{:S(2)}) %collective-permute-start.18) | collective-permute-done | bytes 262176 | tf_op jit(solution)/shard_map/ppermute | solution.py:546
  131.5 1.7 %collective-permute-start.19 = (bf16[256,512]{1,0:T(8,128)(2,1)}, bf16[256,512]{1,0:T(8,128)(2,1)}, u32[]{:S(2)}, u32[]{:S(2)}) collective-permute-start(bf16[256,512]{1,0:T(8,128)(2,1)} %sequences_added.3), channel_id=1, source_target_pairs={{0,4},{1,5},{2,6},{3,7},{4,0},{5,1},{6,2},{7,3},{8,12},{9,13},{10,... | collective-permute-start | bytes 786440 | tf_op jit(solution)/shard_map/ppermute | solution.py:500
  134.3 11.0 %collective-permute-done.17.refs_2_ = bf16[256,512]{1,0:T(8,128)(2,1)S(1)} collective-permute-done((bf16[256,512]{1,0:T(8,128)(2,1)}, bf16[256,512]{1,0:T(8,128)(2,1)S(1)}, u32[]{:S(2)}, u32[]{:S(2)}) %collective-permute-start.17) | collective-permute-done | bytes 262176 | tf_op jit(solution)/shard_map/ppermute | solution.py:500
  145.3 5.4 %collective-permute-done.19.refs_3_ = bf16[256,512]{1,0:T(8,128)(2,1)} collective-permute-done((bf16[256,512]{1,0:T(8,128)(2,1)}, bf16[256,512]{1,0:T(8,128)(2,1)}, u32[]{:S(2)}, u32[]{:S(2)}) %collective-permute-start.19) | collective-permute-done | bytes 262176 | tf_op jit(solution)/shard_map/ppermute | solution.py:500
  150.7 2.2 %weight_grad_joined.1 = f32[256,1024]{1,0:T(8,128)} custom-call(f32[512,1024]{1,0:T(8,128)S(1)} %get-tuple-element.62.refs_0_, bf16[256,1024]{1,0:T(8,128)(2,1)} %collective-permute-done.15.refs_1_, bf16[256,512]{1,0:T(8,128)(2,1)S(1)} %collective-permute-done.17.refs_2_, bf16[256,512]{1,0:T(8,128)(2,1)} %collective-permute-done.19.refs_3_), custom_call_target="tpu_custom_call" | custom-call | bytes 3000000 | tf_op jit(solution)/shard_map/weight_grad_joined/pallas_call | solution.py:478
  (49 shorter events, 20.7 us)
Async XLA Ops:
  3.9 10.9 %collective-permute-start = (bf16[128,4096]{1,0:T(8,128)(2,1)}, bf16[128,4096]{1,0:T(8,128)(2,1)S(1)}, u32[]{:S(2)}, u32[]{:S(2)}) collective-permute-start(bf16[128,4096]{1,0:T(8,128)(2,1)} %get-tuple-element.36), channel_id=1, source_target_pairs={{0,8},{8,0},{16,24},{24,16},{1,9},{9,1},{17,25},{25,17},{2,10},{10... | collective-permute-start | bytes 3145736 | tf_op jit(solution)/shard_map/ppermute | solution.py:503
  4.4 43.8 %all-to-all-start = ((bf16[8,128,256]{2,1,0:T(8,128)(2,1)}), bf16[8,128,256]{2,1,0:T(8,128)(2,1)S(1)}, u32[]{:S(2)}, u32[]{:S(2)}) async-start(bf16[8,128,256]{2,1,0:T(8,128)(2,1)} %get-tuple-element.35), calls=%async_computation | async-start | bytes 1048576 | tf_op jit(solution)/shard_map/all_to_all | solution.py:506
  11.2 20.0 %collective-permute-start.1 = (bf16[128,2048]{1,0:T(8,128)(2,1)}, bf16[128,2048]{1,0:T(8,128)(2,1)}, u32[]{:S(2)}, u32[]{:S(2)}) collective-permute-start(bf16[128,2048]{1,0:T(8,128)(2,1)} %get-tuple-element.41), channel_id=1, source_target_pairs={{0,1},{1,0},{2,3},{3,2},{4,5},{5,4},{6,7},{7,6},{8,9},{9,8},{10,11... | collective-permute-start | bytes 1572872 | tf_op jit(solution)/shard_map/ppermute | solution.py:500
  13.3 21.5 %collective-permute-start.2 = (bf16[128,2048]{1,0:T(8,128)(2,1)}, bf16[128,2048]{1,0:T(8,128)(2,1)}, u32[]{:S(2)}, u32[]{:S(2)}) collective-permute-start(bf16[128,2048]{1,0:T(8,128)(2,1)} %get-tuple-element.42), channel_id=1, source_target_pairs={{0,2},{1,3},{2,0},{3,1},{4,6},{5,7},{6,4},{7,5},{8,10},{9,11},{10,... | collective-permute-start | bytes 1572872 | tf_op jit(solution)/shard_map/ppermute | solution.py:500
  14.7 31.4 %collective-permute-start.3 = (bf16[128,2048]{1,0:T(8,128)(2,1)}, bf16[128,2048]{1,0:T(8,128)(2,1)}, u32[]{:S(2)}, u32[]{:S(2)}) collective-permute-start(bf16[128,2048]{1,0:T(8,128)(2,1)} %get-tuple-element.43), channel_id=1, source_target_pairs={{0,3},{1,2},{2,1},{3,0},{4,7},{5,6},{6,5},{7,4},{8,11},{9,10},{10,... | collective-permute-start | bytes 1572872 | tf_op jit(solution)/shard_map/ppermute | solution.py:500
  46.1 16.9 %collective-permute-start.4 = (bf16[256,1024]{1,0:T(8,128)(2,1)}, bf16[256,1024]{1,0:T(8,128)(2,1)S(1)}, u32[]{:S(2)}, u32[]{:S(2)}) collective-permute-start(bf16[256,1024]{1,0:T(8,128)(2,1)} %get-tuple-element.51), channel_id=1, source_target_pairs={{0,2},{1,3},{2,0},{3,1},{4,6},{5,7},{6,4},{7,5},{8,10},{9,11},{10,... | collective-permute-start | bytes 1572872 | tf_op jit(solution)/shard_map/ppermute | solution.py:500
  46.7 24.0 %collective-permute-start.5 = (bf16[256,1024]{1,0:T(8,128)(2,1)}, bf16[256,1024]{1,0:T(8,128)(2,1)S(1)}, u32[]{:S(2)}, u32[]{:S(2)}) collective-permute-start(bf16[256,1024]{1,0:T(8,128)(2,1)} %get-tuple-element.52), channel_id=1, source_target_pairs={{0,3},{1,2},{2,1},{3,0},{4,7},{5,6},{6,5},{7,4},{8,11},{9,10},{10,... | collective-permute-start | bytes 1572872 | tf_op jit(solution)/shard_map/ppermute | solution.py:500
  63.0 28.3 %copy-start.9 = (f32[512,256]{1,0:T(8,128)S(1)}, f32[512,256]{1,0:T(8,128)}, u32[]{:S(2)}) copy-start(f32[512,256]{1,0:T(8,128)} %get-tuple-element.48) | copy-start | bytes 1572868
  63.0 45.3 %copy-start.1 = (bf16[256,1024]{1,0:T(8,128)(2,1)}, bf16[256,1024]{1,0:T(8,128)(2,1)S(1)}, u32[]{:S(2)}) copy-start(bf16[256,1024]{1,0:T(8,128)(2,1)S(1)} %collective-permute-done.4.refs_10_) | copy-start | bytes 1572868
  71.6 19.7 %collective-permute-start.7 = (bf16[256,1024]{1,0:T(8,128)(2,1)}, bf16[256,1024]{1,0:T(8,128)(2,1)S(1)}, u32[]{:S(2)}, u32[]{:S(2)}) collective-permute-start(bf16[256,1024]{1,0:T(8,128)(2,1)} %get-tuple-element.55), channel_id=1, source_target_pairs={{0,1},{1,0},{2,3},{3,2},{4,5},{5,4},{6,7},{7,6},{8,9},{9,8},{10,11... | collective-permute-start | bytes 1572872 | tf_op jit(solution)/shard_map/ppermute | solution.py:500
  73.0 15.1 %collective-permute-start.6 = (bf16[512,256]{1,0:T(8,128)(2,1)}, bf16[512,256]{1,0:T(8,128)(2,1)S(1)}, u32[]{:S(2)}, u32[]{:S(2)}) collective-permute-start(bf16[512,256]{1,0:T(8,128)(2,1)} %get-tuple-element.54), channel_id=1, source_target_pairs={{4,0},{5,1},{6,2},{7,3},{12,8},{13,9},{14,10},{15,11},{20,16},{21,... | collective-permute-start | bytes 786440 | tf_op jit(solution)/shard_map/ppermute | solution.py:528
  74.3 58.9 %all-to-all-start.1 = ((bf16[4,128,1024]{2,1,0:T(8,128)(2,1)}), bf16[4,128,1024]{2,1,0:T(8,128)(2,1)S(1)}, u32[]{:S(2)}, u32[]{:S(2)}) async-start(bf16[4,128,1024]{2,1,0:T(8,128)(2,1)} %bitcast.1), calls=%async_computation.1 | async-start | bytes 2097152 | tf_op jit(solution)/shard_map/all_to_all | solution.py:506
  91.3 13.2 %collective-permute-start.10 = (bf16[512,256]{1,0:T(8,128)(2,1)S(1)}, bf16[512,256]{1,0:T(8,128)(2,1)S(1)}, u32[]{:S(2)}, u32[]{:S(2)}) collective-permute-start(bf16[512,256]{1,0:T(8,128)(2,1)S(1)} %add_convert_fusion.refs_0_), channel_id=1, source_target_pairs={{0,3},{1,2},{2,1},{3,0},{4,7},{5,6},{6,5},{7,4},{8,11},{9,10},{10,... | collective-permute-start | bytes 786440 | tf_op jit(solution)/shard_map/ppermute | solution.py:500
  96.7 10.1 %collective-permute-start.9 = (bf16[512,256]{1,0:T(8,128)(2,1)S(1)}, bf16[512,256]{1,0:T(8,128)(2,1)S(1)}, u32[]{:S(2)}, u32[]{:S(2)}) collective-permute-start(bf16[512,256]{1,0:T(8,128)(2,1)S(1)} %add_convert_fusion.refs_0_), channel_id=1, source_target_pairs={{0,2},{1,3},{2,0},{3,1},{4,6},{5,7},{6,4},{7,5},{8,10},{9,11},{10,... | collective-permute-start | bytes 786440 | tf_op jit(solution)/shard_map/ppermute | solution.py:500
  96.7 10.1 %collective-permute-start.8 = (bf16[512,256]{1,0:T(8,128)(2,1)S(1)}, bf16[512,256]{1,0:T(8,128)(2,1)S(1)}, u32[]{:S(2)}, u32[]{:S(2)}) collective-permute-start(bf16[512,256]{1,0:T(8,128)(2,1)S(1)} %add_convert_fusion.refs_0_), channel_id=1, source_target_pairs={{0,1},{1,0},{2,3},{3,2},{4,5},{5,4},{6,7},{7,6},{8,9},{9,8},{10,11... | collective-permute-start | bytes 786440 | tf_op jit(solution)/shard_map/ppermute | solution.py:500
  97.4 10.0 %collective-permute-start.11 = (bf16[512,256]{1,0:T(8,128)(2,1)S(1)}, bf16[512,256]{1,0:T(8,128)(2,1)S(1)}, u32[]{:S(2)}, u32[]{:S(2)}) collective-permute-start(bf16[512,256]{1,0:T(8,128)(2,1)S(1)} %add_convert_fusion.refs_0_), channel_id=1, source_target_pairs={{0,8},{8,0},{16,24},{24,16},{1,9},{9,1},{17,25},{25,17},{2,10},{10... | collective-permute-start | bytes 786440 | tf_op jit(solution)/shard_map/ppermute | solution.py:503
  104.5 2.8 %collective-permute-start.14 = (bf16[512,256]{1,0:T(8,128)(2,1)S(1)}, bf16[512,256]{1,0:T(8,128)(2,1)S(1)}, u32[]{:S(2)}, u32[]{:S(2)}) collective-permute-start(bf16[512,256]{1,0:T(8,128)(2,1)S(1)} %collective-permute-done.10.refs_3_), channel_id=1, source_target_pairs={{0,8},{8,0},{16,24},{24,16},{1,9},{9,1},{17,25},{25,17},{2,10},{10... | collective-permute-start | bytes 786440 | tf_op jit(solution)/shard_map/ppermute | solution.py:503
  106.8 1.5 %collective-permute-start.13 = (bf16[512,256]{1,0:T(8,128)(2,1)S(1)}, bf16[512,256]{1,0:T(8,128)(2,1)S(1)}, u32[]{:S(2)}, u32[]{:S(2)}) collective-permute-start(bf16[512,256]{1,0:T(8,128)(2,1)S(1)} %collective-permute-done.9.refs_2_), channel_id=1, source_target_pairs={{0,8},{8,0},{16,24},{24,16},{1,9},{9,1},{17,25},{25,17},{2,10},{10... | collective-permute-start | bytes 786440 | tf_op jit(solution)/shard_map/ppermute | solution.py:503
  106.8 1.9 %collective-permute-start.12 = (bf16[512,256]{1,0:T(8,128)(2,1)S(1)}, bf16[512,256]{1,0:T(8,128)(2,1)S(1)}, u32[]{:S(2)}, u32[]{:S(2)}) collective-permute-start(bf16[512,256]{1,0:T(8,128)(2,1)S(1)} %collective-permute-done.8.refs_1_), channel_id=1, source_target_pairs={{0,8},{8,0},{16,24},{24,16},{1,9},{9,1},{17,25},{25,17},{2,10},{10... | collective-permute-start | bytes 786440 | tf_op jit(solution)/shard_map/ppermute | solution.py:503
  115.9 9.2 %collective-permute-start.16 = (bf16[256,512]{1,0:T(8,128)(2,1)S(1)}, bf16[256,512]{1,0:T(8,128)(2,1)S(1)}, u32[]{:S(2)}, u32[]{:S(2)}) collective-permute-start(bf16[256,512]{1,0:T(8,128)(2,1)S(1)} %get-tuple-element.64), channel_id=1, source_target_pairs={{0,16},{8,24},{16,0},{24,8},{1,17},{9,25},{17,1},{25,9},{2,18},{10... | collective-permute-start | bytes 786440 | tf_op jit(solution)/shard_map/ppermute | solution.py:546
  117.5 13.2 %collective-permute-start.18 = (bf16[256,512]{1,0:T(8,128)(2,1)S(1)}, bf16[256,512]{1,0:T(8,128)(2,1)S(1)}, u32[]{:S(2)}, u32[]{:S(2)}) collective-permute-start(bf16[256,512]{1,0:T(8,128)(2,1)S(1)} %get-tuple-element.65), channel_id=1, source_target_pairs={{0,16},{8,24},{16,0},{24,8},{1,17},{9,25},{17,1},{25,9},{2,18},{10... | collective-permute-start | bytes 786440 | tf_op jit(solution)/shard_map/ppermute | solution.py:546
  118.0 32.7 %collective-permute-start.15 = (bf16[256,1024]{1,0:T(8,128)(2,1)}, bf16[256,1024]{1,0:T(8,128)(2,1)}, u32[]{:S(2)}, u32[]{:S(2)}) collective-permute-start(bf16[256,1024]{1,0:T(8,128)(2,1)} %get-tuple-element.63), channel_id=1, source_target_pairs={{0,16},{8,24},{16,0},{24,8},{1,17},{9,25},{17,1},{25,9},{2,18},{10... | collective-permute-start | bytes 1572872 | tf_op jit(solution)/shard_map/ppermute | solution.py:546
  125.9 19.4 %collective-permute-start.17 = (bf16[256,512]{1,0:T(8,128)(2,1)}, bf16[256,512]{1,0:T(8,128)(2,1)S(1)}, u32[]{:S(2)}, u32[]{:S(2)}) collective-permute-start(bf16[256,512]{1,0:T(8,128)(2,1)} %sequences_added.2), channel_id=1, source_target_pairs={{0,4},{1,5},{2,6},{3,7},{4,0},{5,1},{6,2},{7,3},{8,12},{9,13},{10,... | collective-permute-start | bytes 786440 | tf_op jit(solution)/shard_map/ppermute | solution.py:500
  131.5 19.2 %collective-permute-start.19 = (bf16[256,512]{1,0:T(8,128)(2,1)}, bf16[256,512]{1,0:T(8,128)(2,1)}, u32[]{:S(2)}, u32[]{:S(2)}) collective-permute-start(bf16[256,512]{1,0:T(8,128)(2,1)} %sequences_added.3), channel_id=1, source_target_pairs={{0,4},{1,5},{2,6},{3,7},{4,0},{5,1},{6,2},{7,3},{8,12},{9,13},{10,... | collective-permute-start | bytes 786440 | tf_op jit(solution)/shard_map/ppermute | solution.py:500
  (8 other events, 23.8 us)

commit v5 on v4

--- a/solution.py
+++ b/solution.py
@@ -14,6 +14,7 @@
 GROUP = QH // KVH
 WIDE = GROUP * HD
 TILE = 256
+PART = 4 * HD
 NEGATIVE = -1e30
 BF16 = jnp.bfloat16
 F32 = jnp.float32
@@ -194,13 +195,13 @@
     q_hbm, do_hbm, kv_hbm = refs[:3]
     pieces = refs[3 : 3 + KVH - 1]
     at = 3 + KVH - 1
-    dq_out = refs[at]
-    at += 1
+    dq_out = refs[at : at + KVH]
+    at += KVH
     own_out = refs[at]
     at += 1
     down_out = refs[at : at + groups - 1]
     at += groups - 1
-    q_s, do_s, k_s, v_s, kt_s, dk_s, dv_s, down_s, sems = refs[at:]
+    q_s, do_s, dq_s, k_s, v_s, kt_s, dk_s, dv_s, down_s, sems, q_sems, dq_sems = refs[at:]
 
     place = lax.axis_index("seq")
     group = place // KVH
@@ -212,27 +213,50 @@
     def column_at(block):
         return pl.ds(pl.multiple_of(head * block, block), block)
 
-    copies = [
-        pltpu.make_async_copy(q_hbm.at[:, column_at(WIDE)], q_s.at[row_at(0)], sems.at[0]),
-        pltpu.make_async_copy(do_hbm.at[:, column_at(WIDE)], do_s.at[row_at(0)], sems.at[1]),
-    ]
+    def loads(chunk):
+        first = chunk * PART
+        made = []
+        for k in range(KVH):
+            for kind, target in enumerate((q_s, do_s)):
+                if k:
+                    source = pieces[k - 1].at[:, pl.ds(pl.multiple_of(kind * WIDE + first, PART), PART)]
+                else:
+                    source = (q_hbm, do_hbm)[kind].at[
+                        :, pl.ds(pl.multiple_of(head * WIDE + first, PART), PART)
+                    ]
+                made.append(
+                    pltpu.make_async_copy(
+                        source,
+                        target.at[row_at(k), pl.ds(pl.multiple_of(first, PART), PART)],
+                        q_sems.at[chunk, 2 * k + kind],
+                    )
+                )
+        return made
+
+    def stores(chunk):
+        columns = pl.ds(pl.multiple_of(chunk * PART, PART), PART)
+        return [
+            pltpu.make_async_copy(
+                dq_s.at[row_at(k), columns], dq_out[k].at[:, columns], dq_sems.at[chunk, k]
+            )
+            for k in range(KVH)
+        ]
+
+    copies = []
     for kind, target in enumerate((k_s, v_s)):
         copies += [
             pltpu.make_async_copy(
                 kv_hbm.at[source, :, kind * HD : (kind + 1) * HD],
                 target.at[source * rows : (source + 1) * rows],
-                sems.at[2 * KVH + 2 * source + kind],
+                sems.at[2 * source + kind],
             )
             for source in range(KVH * groups)
         ]
-    for k in range(1, KVH):
-        piece = pieces[k - 1]
-        copies += [
-            pltpu.make_async_copy(piece.at[:, :WIDE], q_s.at[row_at(k)], sems.at[2 * k]),
-            pltpu.make_async_copy(piece.at[:, WIDE:], do_s.at[row_at(k)], sems.at[2 * k + 1]),
-        ]
-    for copy in copies:
+    for copy in copies + loads(0):
         copy.start()
+    for chunk in range(1, WIDE // PART):
+        for copy in loads(chunk):
+            copy.start()
     for copy in copies:
         copy.wait()
 
@@ -290,10 +314,19 @@
                     dv_s[:length, :] += jnp.dot(probs, do, preferred_element_type=F32)
                     dk_s[:length, :] += jnp.dot(grad_scores, q, preferred_element_type=F32)
                     dqt = jnp.dot(kt_s[:, :length], grad_scores, preferred_element_type=F32)
-                    dq_out[part * TILE : (part + 1) * TILE, columns] = dqt.T.astype(BF16)
+                    dq_s[part * TILE : (part + 1) * TILE, columns] = dqt.T.astype(BF16)
                 return carry
 
-            lax.fori_loop(0, GROUP, one_head, 0)
+            def one_chunk(chunk, carry):
+                for copy in loads(chunk):
+                    copy.wait()
+                for h in range(PART // HD):
+                    one_head(chunk * (PART // HD) + h, 0)
+                for copy in stores(chunk):
+                    copy.start()
+                return carry
+
+            lax.fori_loop(0, WIDE // PART, one_chunk, 0)
             base = which * span
             own_out[:, :HD] = dk_s[base : base + span, :]
             own_out[:, HD:] = dv_s[base : base + span, :]
@@ -310,6 +343,8 @@
     ]
     for copy in outs:
         copy.start()
+    for chunk in range(WIDE // PART):
+        outs += stores(chunk)
     for copy in outs:
         copy.wait()
 
@@ -320,12 +355,13 @@
     any_spec = pl.BlockSpec(memory_space=pltpu.HBM)
     n_in = 3 + len(pieces)
     out_shape = (
-        [jax.ShapeDtypeStruct((span, WIDE), BF16)]
+        [jax.ShapeDtypeStruct((rows, WIDE), BF16)] * KVH
         + [jax.ShapeDtypeStruct((span, 2 * HD), F32)]
         + [jax.ShapeDtypeStruct((span, 2 * HD), BF16)] * (groups - 1)
     )
     out_specs = (
-        [pl.BlockSpec(memory_space=pltpu.VMEM)] * 2
+        [any_spec] * KVH
+        + [pl.BlockSpec(memory_space=pltpu.VMEM)]
         + [any_spec] * (groups - 1)
     )
     outs = pl.pallas_call(
@@ -336,27 +372,34 @@
         scratch_shapes=[
             pltpu.VMEM((span, WIDE), BF16),
             pltpu.VMEM((span, WIDE), BF16),
+            pltpu.VMEM((span, WIDE), BF16),
             pltpu.VMEM((length, HD), BF16),
             pltpu.VMEM((length, HD), BF16),
             pltpu.VMEM((HD, length), BF16),
             pltpu.VMEM((length, HD), F32),
             pltpu.VMEM((length, HD), F32),
             pltpu.VMEM((max(groups - 1, 1), span, 2 * HD), BF16),
-            pltpu.SemaphoreType.DMA((2 * KVH + 2 * KVH * groups,)),
+            pltpu.SemaphoreType.DMA((2 * KVH * groups,)),
+            pltpu.SemaphoreType.DMA((WIDE // PART, 2 * KVH)),
+            pltpu.SemaphoreType.DMA((WIDE // PART, KVH)),
         ],
         compiler_params=pltpu.CompilerParams(vmem_limit_bytes=ALL_VMEM_BYTES),
         cost_estimate=pl.CostEstimate(flops=10**10, bytes_accessed=5 * 10**7, transcendentals=0),
         name="attention",
     )(queries, out_grad, keys_values, *pieces)
-    return outs[0], outs[1], outs[2:]
-
-
-def weight_kernel(rows, halves, groups, slab, *refs):
+    return outs[:KVH], outs[KVH], outs[KVH + 1 :]
+
+
+def products(x, g_s, block, slab):
+    left = jnp.concatenate([x[k][:, block : block + slab].T for k in range(KVH)], axis=1)
+    return jnp.dot(left, g_s[...], preferred_element_type=F32)
+
+
+def away_kernel(rows, halves, groups, slab, *refs):
     own = refs[:KVH]
     other = refs[KVH : 2 * KVH]
     x = refs[2 * KVH : 3 * KVH]
-    keep, same = refs[3 * KVH : 3 * KVH + 2]
-    at = 3 * KVH + 2
+    at = 3 * KVH
     away = (refs[at : at + groups - 1], refs[at + groups - 1 : at + 2 * groups - 2])
     mine_out = refs[at + 2 * groups - 2 : at + 2 * groups]
     g_s = refs[-1]
@@ -374,51 +417,68 @@
                 first = 2 * far * rows
                 g_s[first : first + rows, wide] = own[k][lines, part]
                 g_s[first + rows : first + 2 * rows, wide] = other[k][lines, part]
-    for apart in range(halves - 1, -1, -1):
-        for step in range(groups - 1, -1, -1):
-            block = (apart * groups + step) * slab
-            left = jnp.concatenate([x[k][:, block : block + slab].T for k in range(KVH)], axis=1)
-            product = jnp.dot(left, g_s[...], preferred_element_type=F32)
+    for apart in range(1, halves):
+        for step in range(1, groups):
+            product = products(x, g_s, (apart * groups + step) * slab, slab)
             lines = slice((apart - 1) * slab, apart * slab)
-            if apart == 0:
-                keep[step * slab : (step + 1) * slab, :] = product
-            elif step == 0:
-                same[lines, :] = product.astype(BF16)
-            else:
-                for kind in range(2):
-                    away[kind][step - 1][lines, :] = product[
-                        :, kind * width : (kind + 1) * width
-                    ].astype(BF16)
-
-
-def weight_terms(rows, halves, groups, slab, own, other, inputs):
+            for kind in range(2):
+                away[kind][step - 1][lines, :] = product[
+                    :, kind * width : (kind + 1) * width
+                ].astype(BF16)
+
+
+def away_terms(rows, halves, groups, slab, own, other, inputs):
     span = KVH * rows
     channels = KVH * HD
     vmem = pl.BlockSpec(memory_space=pltpu.VMEM)
     others = max(halves - 1, 1) * slab
     outs = pl.pallas_call(
-        lambda *refs: weight_kernel(rows, halves, groups, slab, *refs),
-        out_shape=[
-            jax.ShapeDtypeStruct((groups * slab, 2 * channels), F32),
-            jax.ShapeDtypeStruct((others, 2 * channels), BF16),
-        ]
-        + [jax.ShapeDtypeStruct((others, channels), BF16)] * (2 * (groups - 1))
-        + [jax.ShapeDtypeStruct((rows, channels), BF16)] * 2,
+        lambda *refs: away_kernel(rows, halves, groups, slab, *refs),
+        out_shape=[jax.ShapeDtypeStruct((others, channels), BF16)] * (2 * (groups - 1))
+        + [jax.ShapeDtypeStruct((rows, channels), BF16)] * 2
+        + [jax.ShapeDtypeStruct((2 * span, 2 * channels), BF16)],
         in_specs=[vmem] * (3 * KVH),
-        out_specs=[vmem] * (2 * groups + 2),
-        scratch_shapes=[pltpu.VMEM((2 * span, 2 * channels), BF16)],
+        out_specs=[vmem] * (2 * groups + 1),
         compiler_params=pltpu.CompilerParams(vmem_limit_bytes=VMEM_BYTES),
-        cost_estimate=pl.CostEstimate(flops=3 * 10**9, bytes_accessed=6 * 10**6, transcendentals=0),
-        name="weight_terms",
+        cost_estimate=pl.CostEstimate(flops=10**9, bytes_accessed=6 * 10**6, transcendentals=0),
+        name="weight_terms_away",
     )(*own, *other, *inputs)
     at = groups - 1
-    away = outs[2 : 2 + 2 * at]
-    return outs[0], outs[1], (away[:at], away[at:]), outs[2 + 2 * at :]
-
-
-def place_kernel(pieces, out):
-    for head in range(KVH):
-        out[:, head * WIDE : (head + 1) * WIDE] = pieces[head]
+    return (outs[:at], outs[at : 2 * at]), outs[2 * at : 2 * at + 2], outs[-1]
+
+
+def near_kernel(halves, groups, slab, *refs):
+    x = refs[:KVH]
+    g_s, keep, same = refs[KVH:]
+    for step in range(groups - 1, -1, -1):
+        keep[step * slab : (step + 1) * slab, :] = products(x, g_s, step * slab, slab)
+    for apart in range(1, halves):
+        product = products(x, g_s, apart * groups * slab, slab)
+        same[(apart - 1) * slab : apart * slab, :] = product.astype(BF16)
+
+
+def near_terms(halves, groups, slab, inputs, joined_grads):
+    channels = joined_grads.shape[1]
+    vmem = pl.BlockSpec(memory_space=pltpu.VMEM)
+    return pl.pallas_call(
+        lambda *refs: near_kernel(halves, groups, slab, *refs),
+        out_shape=[
+            jax.ShapeDtypeStruct((groups * slab, channels), F32),
+            jax.ShapeDtypeStruct((max(halves - 1, 1) * slab, channels), BF16),
+        ],
+        in_specs=[vmem] * (KVH + 1),
+        out_specs=[vmem] * 2,
+        compiler_params=pltpu.CompilerParams(vmem_limit_bytes=VMEM_BYTES),
+        cost_estimate=pl.CostEstimate(flops=2 * 10**9, bytes_accessed=6 * 10**6, transcendentals=0),
+        name="weight_terms_near",
+    )(*inputs, joined_grads)
+
+
+def place_kernel(*refs):
+    out = refs[KVH]
+    head = lax.axis_index("seq") % KVH
+    for k in range(KVH):
+        out[:, pl.ds(pl.multiple_of((head ^ k) * WIDE, WIDE), WIDE)] = refs[k][...]
 
 
 def placed(rows, pieces):
@@ -426,12 +486,12 @@
     return pl.pallas_call(
         place_kernel,
         out_shape=jax.ShapeDtypeStruct((rows, QH * HD), BF16),
-        in_specs=[vmem],
+        in_specs=[vmem] * KVH,
         out_specs=vmem,
         compiler_params=pltpu.CompilerParams(vmem_limit_bytes=VMEM_BYTES),
         cost_estimate=pl.CostEstimate(flops=0, bytes_accessed=5 * 10**6, transcendentals=0),
         name="query_grad_placed",
-    )(pieces)
+    )(*pieces)
 
 
 def add_kernel(kind, step, keep, *refs):
@@ -537,9 +597,10 @@
     total = total.astype(BF16)
     gathered = [total] + [swap(total, k) for k in range(1, KVH)]
     others = [across_cores(piece) for piece in gathered]
-    keep, same, away, narrow = weight_terms(
+    away, narrow, joined_grads = away_terms(
         rows, halves, groups, slab, gathered, others, inputs
     )
+    keep, same = near_terms(halves, groups, slab, inputs, joined_grads)
 
     def over_sequences(array):
         return [
@@ -552,15 +613,18 @@
         ]
 
     parts = [[over_sequences(array) for array in away[kind]] for kind in range(2)]
-    rest = [[], []]
+    returned = [grads[0]] + [swap(grads[k], k) for k in range(1, KVH)]
+
+    totals = [None, None]
+    rest = [None, None]
     for kind in (1, 0):
-        totals = [
+        if not kind:
+            parts[0], _ = after((parts[0], returned))
+        totals[kind] = [
             added(keep, parts[kind][step - 1], kind, step) for step in range(1, groups)
         ]
-        rest[kind] = [swap(total, (step + 1) * KVH) for step, total in enumerate(totals)]
+        rest[kind] = [swap(total, (step + 1) * KVH) for step, total in enumerate(totals[kind])]
     weight_grad = joined(slab, keep, over_sequences(same), rest[0] + rest[1])
-
-    returned = exchange(grads.reshape(KVH, rows, WIDE), within)
     query_grad = placed(rows, returned)
     return (query_grad, narrow[0], narrow[1], weight_grad)
 

time: 154 us -> 146 us (0.948)
  waiting for transfers between devices: 84.8 us -> 92.4 us
  starting transfers between devices: 32.8 us -> 26.4 us
  local copies, waits for them, and re-layouts: 6.73 us -> 0.98 us
  Pallas kernels: 27.7 us -> 23.8 us
    ppermute x11 -> x14, waiting for transfers between devices: 64.4 us -> 74.3 us  [swap(): return lax.ppermute(array, 'seq', [(i, i ^ k) for i in range(cycle)])]
    unnamed x20 -> x8, local copies, waits for them, and re-layouts: 6.73 us -> 0.98 us
    ppermute x3, waiting for transfers between devices: 8.75 us -> 4.32 us  [over_sequences(): lax.ppermute(array[(apart - 1) * slab:apart * slab], 'dp', [(i, i ^ 2 * a...]
    all_to_all x2 -> x1, starting transfers between devices: 10.4 us -> 6.82 us  [exchange(): lax.all_to_all(array, 'seq', split_axis=0, concat_axis=0, tiled=True, axi...]
    ppermute x1, waiting for transfers between devices: 10.3 us -> 13.7 us  [local(): lax.ppermute(down[step - 1], 'seq', [(i + step * KVH, i) for i in range(c...]
    ppermute x11 -> x14, starting transfers between devices: 16.5 us -> 14.2 us  [swap(): return lax.ppermute(array, 'seq', [(i, i ^ k) for i in range(cycle)])]
    pallas_call x1, Pallas kernels: 14 us -> 11.9 us  [attention(): pl.pallas_call(lambda *refs: attention_kernel(rows, groups, *refs), out_s...]
    pallas_call x1 -> x2, Pallas kernels: 3.01 us -> 3.65 us  [the longest x1 1.83 us: near_terms(): pl.pallas_call(lambda *refs: near_kernel(halves, groups, slab, *refs), ou...]
  transfers between devices with their start and end apart: 22 -> 24, of which waited for: 14 -> 13; matrix products, arithmetic and copies ran while one was open for 0% -> 0% of each run, Pallas kernels for 15% -> 13%
where the time goes in v5:
time: 146 us; the launch traced here: 145 us
  waiting for transfers between devices  92.4 us (63%)
  starting transfers between devices  26.4 us (18%)
  Pallas kernels  23.8 us (16%)
    ppermute x14, waiting for transfers between devices, swap(): return lax.ppermute(array, 'seq', [(i, i ^ k) for i in range(cycle)])  74.3 us
    ppermute x14, starting transfers between devices, swap(): return lax.ppermute(array, 'seq', [(i, i ^ k) for i in range(cycle)])  14.2 us
    ppermute x1, waiting for transfers between devices, local(): lax.ppermute(down[step - 1], 'seq', [(i + step * KVH, i) for i in range(c...  13.7 us
    pallas_call x1, Pallas kernels, attention(): pl.pallas_call(lambda *refs: attention_kernel(rows, groups, *refs), out_s...  11.9 us
    all_to_all x1, starting transfers between devices, exchange(): lax.all_to_all(array, 'seq', split_axis=0, concat_axis=0, tiled=True, axi...  6.82 us
    ppermute x3, waiting for transfers between devices, over_sequences(): lax.ppermute(array[(apart - 1) * slab:apart * slab], 'dp', [(i, i ^ 2 * a...  4.32 us
    ppermute x3, starting transfers between devices, over_sequences(): lax.ppermute(array[(apart - 1) * slab:apart * slab], 'dp', [(i, i ^ 2 * a...  3.61 us
    pallas_call x1, Pallas kernels, packed(): pl.pallas_call(lambda *refs: pack_kernel(rows, groups, halves, *refs), ou...  3.25 us
  transfers between devices with their start and end apart: 24, of which 13 were waited for; matrix products, arithmetic and copies ran while one was open for 0% of the time, Pallas kernels for 13%

profile of v5, /device:TPU:0, one launch (start us, length us, event | category | flops | bytes accessed | tf_op | source)
XLA Modules:
  0.0 145.5 jit_solution(12123375220734575839)
XLA Ops:
  0.6 3.2 %first_sends.1 = (bf16[8,128,256]{2,1,0:T(8,128)(2,1)}, bf16[128,2048]{1,0:T(8,128)(2,1)}, bf16[128,2048]{1,0:T(8,128)(2,1)}, bf16[128,2048]{1,0:T(8,128)(2,1)}, bf16[128,4096]{1,0:T(8,128)(2,1)}) custom-call(bf16[128,4096]{1,0:T(8,128)(2,1)} %refs_0_.5, bf16[128,4096]{1,0:T(8,128)(2,1)} %refs_1_.3, bf16[128,512]{1,0:T(8,128)(2,1)} %refs_2_.1, ...), custom_call_target="tpu_custom_call" | custom-call | bytes 8000000 | tf_op jit(solution)/shard_map/first_sends/pallas_call | solution.py:93
  4.4 6.8 %all-to-all-start = ((bf16[8,128,256]{2,1,0:T(8,128)(2,1)}), bf16[8,128,256]{2,1,0:T(8,128)(2,1)}, u32[]{:S(2)}, u32[]{:S(2)}) async-start(bf16[8,128,256]{2,1,0:T(8,128)(2,1)} %get-tuple-element.40), calls=%async_computation | async-start | bytes 1048576 | tf_op jit(solution)/shard_map/all_to_all | solution.py:566
  11.2 2.0 %collective-permute-start.1 = (bf16[128,2048]{1,0:T(8,128)(2,1)}, bf16[128,2048]{1,0:T(8,128)(2,1)S(1)}, u32[]{:S(2)}, u32[]{:S(2)}) collective-permute-start(bf16[128,2048]{1,0:T(8,128)(2,1)} %get-tuple-element.46), channel_id=1, source_target_pairs={{0,1},{1,0},{2,3},{3,2},{4,5},{5,4},{6,7},{7,6},{8,9},{9,8},{10,11... | collective-permute-start | bytes 1572872 | tf_op jit(solution)/shard_map/ppermute | solution.py:560
  15.7 2.7 %input_columns.1 = (bf16[256,1024]{1,0:T(8,128)(2,1)}, bf16[256,1024]{1,0:T(8,128)(2,1)}, bf16[256,1024]{1,0:T(8,128)(2,1)}, bf16[256,1024]{1,0:T(8,128)(2,1)}) custom-call(bf16[128,8192]{1,0:T(8,128)(2,1)} %refs_0_.4, bf16[128,4096]{1,0:T(8,128)(2,1)} %copy-done.2), custom_call_target="tpu_custom_call" | custom-call | bytes 8000000 | tf_op jit(solution)/shard_map/input_columns/pallas_call | solution.py:177
  18.4 12.6 %collective-permute-done.1.refs_3_ = bf16[128,2048]{1,0:T(8,128)(2,1)S(1)} collective-permute-done((bf16[128,2048]{1,0:T(8,128)(2,1)}, bf16[128,2048]{1,0:T(8,128)(2,1)S(1)}, u32[]{:S(2)}, u32[]{:S(2)}) %collective-permute-start.1) | collective-permute-done | bytes 524320 | tf_op jit(solution)/shard_map/ppermute | solution.py:560
  31.1 3.6 %collective-permute-done.2.refs_4_ = bf16[128,2048]{1,0:T(8,128)(2,1)} collective-permute-done((bf16[128,2048]{1,0:T(8,128)(2,1)}, bf16[128,2048]{1,0:T(8,128)(2,1)}, u32[]{:S(2)}, u32[]{:S(2)}) %collective-permute-start.2) | collective-permute-done | bytes 524320 | tf_op jit(solution)/shard_map/ppermute | solution.py:560
  34.7 11.4 %collective-permute-done.3.refs_5_ = bf16[128,2048]{1,0:T(8,128)(2,1)} collective-permute-done((bf16[128,2048]{1,0:T(8,128)(2,1)}, bf16[128,2048]{1,0:T(8,128)(2,1)}, u32[]{:S(2)}, u32[]{:S(2)}) %collective-permute-start.3) | collective-permute-done | bytes 524320 | tf_op jit(solution)/shard_map/ppermute | solution.py:560
  48.2 11.9 %attention.1 = (bf16[128,1024]{1,0:T(8,128)(2,1)}, bf16[128,1024]{1,0:T(8,128)(2,1)}, bf16[128,1024]{1,0:T(8,128)(2,1)}, bf16[128,1024]{1,0:T(8,128)(2,1)}, f32[...) custom-call(bf16[128,4096]{1,0:T(8,128)(2,1)} %refs_0_.5, bf16[128,4096]{1,0:T(8,128)(2,1)} %refs_1_.3, ...), custom_call_target="tpu_custom_call" | custom-call | flops 10000000000 | bytes 50000000 | tf_op jit(solution)/shard_map/attention/pallas_call | solution.py:367
  61.2 9.6 %collective-permute-done.8.refs_11_.refs_3_ = bf16[256,1024]{1,0:T(8,128)(2,1)S(1)} collective-permute-done((bf16[256,1024]{1,0:T(8,128)(2,1)}, bf16[256,1024]{1,0:T(8,128)(2,1)S(1)}, u32[]{:S(2)}, u32[]{:S(2)}) %collective-permute-start.8) | collective-permute-done | bytes 524320 | tf_op jit(solution)/shard_map/ppermute | solution.py:560
  70.8 1.5 %collective-permute-start.10 = (bf16[256,1024]{1,0:T(8,128)(2,1)}, bf16[256,1024]{1,0:T(8,128)(2,1)S(1)}, u32[]{:S(2)}, u32[]{:S(2)}) collective-permute-start(bf16[256,1024]{1,0:T(8,128)(2,1)} %get-tuple-element.63), channel_id=1, source_target_pairs={{0,1},{1,0},{2,3},{3,2},{4,5},{5,4},{6,7},{7,6},{8,9},{9,8},{10,11... | collective-permute-start | bytes 1572872 | tf_op jit(solution)/shard_map/ppermute | solution.py:560
  73.5 13.7 %collective-permute-done.9 = bf16[512,256]{1,0:T(8,128)(2,1)S(1)} collective-permute-done((bf16[512,256]{1,0:T(8,128)(2,1)}, bf16[512,256]{1,0:T(8,128)(2,1)S(1)}, u32[]{:S(2)}, u32[]{:S(2)}) %collective-permute-start.9) | collective-permute-done | bytes 262176 | tf_op jit(solution)/shard_map/ppermute | solution.py:588
  88.4 2.0 %collective-permute-start.12 = (bf16[512,256]{1,0:T(8,128)(2,1)S(1)}, bf16[512,256]{1,0:T(8,128)(2,1)S(1)}, u32[]{:S(2)}, u32[]{:S(2)}) collective-permute-start(bf16[512,256]{1,0:T(8,128)(2,1)S(1)} %add_convert_fusion.refs_0_), channel_id=1, source_target_pairs={{0,2},{1,3},{2,0},{3,1},{4,6},{5,7},{6,4},{7,5},{8,10},{9,11},{10,... | collective-permute-start | bytes 786440 | tf_op jit(solution)/shard_map/ppermute | solution.py:560
  90.5 1.5 %collective-permute-start.11 = (bf16[512,256]{1,0:T(8,128)(2,1)S(1)}, bf16[512,256]{1,0:T(8,128)(2,1)S(1)}, u32[]{:S(2)}, u32[]{:S(2)}) collective-permute-start(bf16[512,256]{1,0:T(8,128)(2,1)S(1)} %add_convert_fusion.refs_0_), channel_id=1, source_target_pairs={{0,1},{1,0},{2,3},{3,2},{4,5},{5,4},{6,7},{7,6},{8,9},{9,8},{10,11... | collective-permute-start | bytes 786440 | tf_op jit(solution)/shard_map/ppermute | solution.py:560
  91.9 6.6 %collective-permute-done.13.refs_3_ = bf16[512,256]{1,0:T(8,128)(2,1)S(1)} collective-permute-done((bf16[512,256]{1,0:T(8,128)(2,1)S(1)}, bf16[512,256]{1,0:T(8,128)(2,1)S(1)}, u32[]{:S(2)}, u32[]{:S(2)}) %collective-permute-start.13) | collective-permute-done | bytes 262176 | tf_op jit(solution)/shard_map/ppermute | solution.py:560
  98.6 3.3 %collective-permute-done.12.refs_2_ = bf16[512,256]{1,0:T(8,128)(2,1)S(1)} collective-permute-done((bf16[512,256]{1,0:T(8,128)(2,1)S(1)}, bf16[512,256]{1,0:T(8,128)(2,1)S(1)}, u32[]{:S(2)}, u32[]{:S(2)}) %collective-permute-start.12) | collective-permute-done | bytes 262176 | tf_op jit(solution)/shard_map/ppermute | solution.py:560
  104.3 2.4 %collective-permute-start.6 = (bf16[128,1024]{1,0:T(8,128)(2,1)}, bf16[128,1024]{1,0:T(8,128)(2,1)S(1)}, u32[]{:S(2)}, u32[]{:S(2)}) collective-permute-start(bf16[128,1024]{1,0:T(8,128)(2,1)} %get-tuple-element.55), channel_id=1, source_target_pairs={{0,3},{1,2},{2,1},{3,0},{4,7},{5,6},{6,5},{7,4},{8,11},{9,10},{10,... | collective-permute-start | bytes 786440 | tf_op jit(solution)/shard_map/ppermute | solution.py:560
  106.7 1.8 %weight_terms_away.1 = (bf16[256,512]{1,0:T(8,128)(2,1)S(1)}, bf16[256,512]{1,0:T(8,128)(2,1)S(1)}, bf16[128,512]{1,0:T(8,128)(2,1)}, bf16[128,512]{1,0:T(8,128)(2,1)}, bf16[1024,1024]{1,0:T(8,128)(2,1)S(1)}) custom-call(bf16[512,256]{1,0:T(8,128)(2,1)S(1)} %add_convert_fusion.refs_0_, bf16[512,256]{1,0:T(8,128)(2,1)S(1)} %collective-permute-done.11.refs_1_, ...), custom_call_target="tpu_custom_call" | custom-call | flops 1000000000 | bytes 6000000 | tf_op jit(solution)/shard_map/weight_terms_away/pallas_call | solution.py:435
  108.5 1.5 %collective-permute-start.19 = (bf16[256,512]{1,0:T(8,128)(2,1)S(1)}, bf16[256,512]{1,0:T(8,128)(2,1)S(1)}, u32[]{:S(2)}, u32[]{:S(2)}) collective-permute-start(bf16[256,512]{1,0:T(8,128)(2,1)S(1)} %get-tuple-element.73), channel_id=1, source_target_pairs={{0,16},{8,24},{16,0},{24,8},{1,17},{9,25},{17,1},{25,9},{2,18},{10... | collective-permute-start | bytes 786440 | tf_op jit(solution)/shard_map/ppermute | solution.py:607
  110.5 1.8 %weight_terms_near.1 = (f32[512,1024]{1,0:T(8,128)S(1)}, bf16[256,1024]{1,0:T(8,128)(2,1)S(1)}) custom-call(bf16[256,1024]{1,0:T(8,128)(2,1)S(1)} %copy-done, bf16[256,1024]{1,0:T(8,128)(2,1)S(1)} %collective-permute-done.10.refs_9_.refs_1_, bf16[256,1024]{1,0:T(8,128)(2,1)S(1)} %collective-permute-done.7.refs_10_.refs_2_, ...), custom_call_target="tpu_custom_call" | custom-call | flops 2000000000 | bytes 6000000 | tf_op jit(solution)/shard_map/weight_terms_near/pallas_call | solution.py:463
  112.4 1.6 %collective-permute-start.18 = (bf16[256,1024]{1,0:T(8,128)(2,1)S(1)}, bf16[256,1024]{1,0:T(8,128)(2,1)S(1)}, u32[]{:S(2)}, u32[]{:S(2)}) collective-permute-start(bf16[256,1024]{1,0:T(8,128)(2,1)S(1)} %get-tuple-element.72), channel_id=1, source_target_pairs={{0,16},{8,24},{16,0},{24,8},{1,17},{9,25},{17,1},{25,9},{2,18},{10... | collective-permute-start | bytes 1572872 | tf_op jit(solution)/shard_map/ppermute | solution.py:607
  113.9 4.9 %collective-permute-done.6.refs_3_ = bf16[128,1024]{1,0:T(8,128)(2,1)S(1)} collective-permute-done((bf16[128,1024]{1,0:T(8,128)(2,1)}, bf16[128,1024]{1,0:T(8,128)(2,1)S(1)}, u32[]{:S(2)}, u32[]{:S(2)}) %collective-permute-start.6) | collective-permute-done | bytes 262176 | tf_op jit(solution)/shard_map/ppermute | solution.py:560
  119.0 4.3 %collective-permute-done.21.refs_1_ = bf16[256,512]{1,0:T(8,128)(2,1)S(1)} collective-permute-done((bf16[256,512]{1,0:T(8,128)(2,1)S(1)}, bf16[256,512]{1,0:T(8,128)(2,1)S(1)}, u32[]{:S(2)}, u32[]{:S(2)}) %collective-permute-start.21) | collective-permute-done | bytes 262176 | tf_op jit(solution)/shard_map/ppermute | solution.py:607
  124.5 14.3 %collective-permute-done.20.refs_2_ = bf16[256,512]{1,0:T(8,128)(2,1)S(1)} collective-permute-done((bf16[256,512]{1,0:T(8,128)(2,1)S(1)}, bf16[256,512]{1,0:T(8,128)(2,1)S(1)}, u32[]{:S(2)}, u32[]{:S(2)}) %collective-permute-start.20) | collective-permute-done | bytes 262176 | tf_op jit(solution)/shard_map/ppermute | solution.py:560
  138.9 5.5 %collective-permute-done.22.refs_3_ = bf16[256,512]{1,0:T(8,128)(2,1)S(1)} collective-permute-done((bf16[256,512]{1,0:T(8,128)(2,1)S(1)}, bf16[256,512]{1,0:T(8,128)(2,1)S(1)}, u32[]{:S(2)}, u32[]{:S(2)}) %collective-permute-start.22) | collective-permute-done | bytes 262176 | tf_op jit(solution)/shard_map/ppermute | solution.py:560
  (42 shorter events, 14.0 us)
Async XLA Ops:
  3.9 10.9 %collective-permute-start = (bf16[128,4096]{1,0:T(8,128)(2,1)}, bf16[128,4096]{1,0:T(8,128)(2,1)S(1)}, u32[]{:S(2)}, u32[]{:S(2)}) collective-permute-start(bf16[128,4096]{1,0:T(8,128)(2,1)} %get-tuple-element.41), channel_id=1, source_target_pairs={{0,8},{8,0},{16,24},{24,16},{1,9},{9,1},{17,25},{25,17},{2,10},{10... | collective-permute-start | bytes 3145736 | tf_op jit(solution)/shard_map/ppermute | solution.py:563
  4.4 43.8 %all-to-all-start = ((bf16[8,128,256]{2,1,0:T(8,128)(2,1)}), bf16[8,128,256]{2,1,0:T(8,128)(2,1)}, u32[]{:S(2)}, u32[]{:S(2)}) async-start(bf16[8,128,256]{2,1,0:T(8,128)(2,1)} %get-tuple-element.40), calls=%async_computation | async-start | bytes 1048576 | tf_op jit(solution)/shard_map/all_to_all | solution.py:566
  11.2 19.9 %collective-permute-start.1 = (bf16[128,2048]{1,0:T(8,128)(2,1)}, bf16[128,2048]{1,0:T(8,128)(2,1)S(1)}, u32[]{:S(2)}, u32[]{:S(2)}) collective-permute-start(bf16[128,2048]{1,0:T(8,128)(2,1)} %get-tuple-element.46), channel_id=1, source_target_pairs={{0,1},{1,0},{2,3},{3,2},{4,5},{5,4},{6,7},{7,6},{8,9},{9,8},{10,11... | collective-permute-start | bytes 1572872 | tf_op jit(solution)/shard_map/ppermute | solution.py:560
  13.3 21.5 %collective-permute-start.2 = (bf16[128,2048]{1,0:T(8,128)(2,1)}, bf16[128,2048]{1,0:T(8,128)(2,1)}, u32[]{:S(2)}, u32[]{:S(2)}) collective-permute-start(bf16[128,2048]{1,0:T(8,128)(2,1)} %get-tuple-element.47), channel_id=1, source_target_pairs={{0,2},{1,3},{2,0},{3,1},{4,6},{5,7},{6,4},{7,5},{8,10},{9,11},{10,... | collective-permute-start | bytes 1572872 | tf_op jit(solution)/shard_map/ppermute | solution.py:560
  14.7 31.4 %collective-permute-start.3 = (bf16[128,2048]{1,0:T(8,128)(2,1)}, bf16[128,2048]{1,0:T(8,128)(2,1)}, u32[]{:S(2)}, u32[]{:S(2)}) collective-permute-start(bf16[128,2048]{1,0:T(8,128)(2,1)} %get-tuple-element.48), channel_id=1, source_target_pairs={{0,3},{1,2},{2,1},{3,0},{4,7},{5,6},{6,5},{7,4},{8,11},{9,10},{10,... | collective-permute-start | bytes 1572872 | tf_op jit(solution)/shard_map/ppermute | solution.py:560
  46.1 15.1 %collective-permute-start.7 = (bf16[256,1024]{1,0:T(8,128)(2,1)}, bf16[256,1024]{1,0:T(8,128)(2,1)S(1)}, u32[]{:S(2)}, u32[]{:S(2)}) collective-permute-start(bf16[256,1024]{1,0:T(8,128)(2,1)} %get-tuple-element.59), channel_id=1, source_target_pairs={{0,2},{1,3},{2,0},{3,1},{4,6},{5,7},{6,4},{7,5},{8,10},{9,11},{10,... | collective-permute-start | bytes 1572872 | tf_op jit(solution)/shard_map/ppermute | solution.py:560
  46.7 24.0 %collective-permute-start.8 = (bf16[256,1024]{1,0:T(8,128)(2,1)}, bf16[256,1024]{1,0:T(8,128)(2,1)S(1)}, u32[]{:S(2)}, u32[]{:S(2)}) collective-permute-start(bf16[256,1024]{1,0:T(8,128)(2,1)} %get-tuple-element.60), channel_id=1, source_target_pairs={{0,3},{1,2},{2,1},{3,0},{4,7},{5,6},{6,5},{7,4},{8,11},{9,10},{10,... | collective-permute-start | bytes 1572872 | tf_op jit(solution)/shard_map/ppermute | solution.py:560
  70.8 16.5 %collective-permute-start.10 = (bf16[256,1024]{1,0:T(8,128)(2,1)}, bf16[256,1024]{1,0:T(8,128)(2,1)S(1)}, u32[]{:S(2)}, u32[]{:S(2)}) collective-permute-start(bf16[256,1024]{1,0:T(8,128)(2,1)} %get-tuple-element.63), channel_id=1, source_target_pairs={{0,1},{1,0},{2,3},{3,2},{4,5},{5,4},{6,7},{7,6},{8,9},{9,8},{10,11... | collective-permute-start | bytes 1572872 | tf_op jit(solution)/shard_map/ppermute | solution.py:560
  72.3 15.0 %collective-permute-start.9 = (bf16[512,256]{1,0:T(8,128)(2,1)}, bf16[512,256]{1,0:T(8,128)(2,1)S(1)}, u32[]{:S(2)}, u32[]{:S(2)}) collective-permute-start(bf16[512,256]{1,0:T(8,128)(2,1)} %get-tuple-element.62), channel_id=1, source_target_pairs={{4,0},{5,1},{6,2},{7,3},{12,8},{13,9},{14,10},{15,11},{20,16},{21,... | collective-permute-start | bytes 786440 | tf_op jit(solution)/shard_map/ppermute | solution.py:588
  88.4 10.2 %collective-permute-start.13 = (bf16[512,256]{1,0:T(8,128)(2,1)S(1)}, bf16[512,256]{1,0:T(8,128)(2,1)S(1)}, u32[]{:S(2)}, u32[]{:S(2)}) collective-permute-start(bf16[512,256]{1,0:T(8,128)(2,1)S(1)} %add_convert_fusion.refs_0_), channel_id=1, source_target_pairs={{0,3},{1,2},{2,1},{3,0},{4,7},{5,6},{6,5},{7,4},{8,11},{9,10},{10,... | collective-permute-start | bytes 786440 | tf_op jit(solution)/shard_map/ppermute | solution.py:560
  88.4 13.4 %collective-permute-start.12 = (bf16[512,256]{1,0:T(8,128)(2,1)S(1)}, bf16[512,256]{1,0:T(8,128)(2,1)S(1)}, u32[]{:S(2)}, u32[]{:S(2)}) collective-permute-start(bf16[512,256]{1,0:T(8,128)(2,1)S(1)} %add_convert_fusion.refs_0_), channel_id=1, source_target_pairs={{0,2},{1,3},{2,0},{3,1},{4,6},{5,7},{6,4},{7,5},{8,10},{9,11},{10,... | collective-permute-start | bytes 786440 | tf_op jit(solution)/shard_map/ppermute | solution.py:560
  90.5 12.7 %collective-permute-start.11 = (bf16[512,256]{1,0:T(8,128)(2,1)S(1)}, bf16[512,256]{1,0:T(8,128)(2,1)S(1)}, u32[]{:S(2)}, u32[]{:S(2)}) collective-permute-start(bf16[512,256]{1,0:T(8,128)(2,1)S(1)} %add_convert_fusion.refs_0_), channel_id=1, source_target_pairs={{0,1},{1,0},{2,3},{3,2},{4,5},{5,4},{6,7},{7,6},{8,9},{9,8},{10,11... | collective-permute-start | bytes 786440 | tf_op jit(solution)/shard_map/ppermute | solution.py:560
  91.9 12.3 %collective-permute-start.14 = (bf16[512,256]{1,0:T(8,128)(2,1)S(1)}, bf16[512,256]{1,0:T(8,128)(2,1)S(1)}, u32[]{:S(2)}, u32[]{:S(2)}) collective-permute-start(bf16[512,256]{1,0:T(8,128)(2,1)S(1)} %add_convert_fusion.refs_0_), channel_id=1, source_target_pairs={{0,8},{8,0},{16,24},{24,16},{1,9},{9,1},{17,25},{25,17},{2,10},{10... | collective-permute-start | bytes 786440 | tf_op jit(solution)/shard_map/ppermute | solution.py:563
  98.5 5.7 %collective-permute-start.17 = (bf16[512,256]{1,0:T(8,128)(2,1)S(1)}, bf16[512,256]{1,0:T(8,128)(2,1)S(1)}, u32[]{:S(2)}, u32[]{:S(2)}) collective-permute-start(bf16[512,256]{1,0:T(8,128)(2,1)S(1)} %collective-permute-done.13.refs_3_), channel_id=1, source_target_pairs={{0,8},{8,0},{16,24},{24,16},{1,9},{9,1},{17,25},{25,17},{2,10},{10... | collective-permute-start | bytes 786440 | tf_op jit(solution)/shard_map/ppermute | solution.py:563
  101.8 4.8 %collective-permute-start.16 = (bf16[512,256]{1,0:T(8,128)(2,1)S(1)}, bf16[512,256]{1,0:T(8,128)(2,1)S(1)}, u32[]{:S(2)}, u32[]{:S(2)}) collective-permute-start(bf16[512,256]{1,0:T(8,128)(2,1)S(1)} %collective-permute-done.12.refs_2_), channel_id=1, source_target_pairs={{0,8},{8,0},{16,24},{24,16},{1,9},{9,1},{17,25},{25,17},{2,10},{10... | collective-permute-start | bytes 786440 | tf_op jit(solution)/shard_map/ppermute | solution.py:563
  103.1 3.5 %collective-permute-start.15 = (bf16[512,256]{1,0:T(8,128)(2,1)S(1)}, bf16[512,256]{1,0:T(8,128)(2,1)S(1)}, u32[]{:S(2)}, u32[]{:S(2)}) collective-permute-start(bf16[512,256]{1,0:T(8,128)(2,1)S(1)} %collective-permute-done.11.refs_1_), channel_id=1, source_target_pairs={{0,8},{8,0},{16,24},{24,16},{1,9},{9,1},{17,25},{25,17},{2,10},{10... | collective-permute-start | bytes 786440 | tf_op jit(solution)/shard_map/ppermute | solution.py:563
  103.1 9.2 %collective-permute-start.4 = (bf16[128,1024]{1,0:T(8,128)(2,1)}, bf16[128,1024]{1,0:T(8,128)(2,1)S(1)}, u32[]{:S(2)}, u32[]{:S(2)}) collective-permute-start(bf16[128,1024]{1,0:T(8,128)(2,1)} %get-tuple-element.53), channel_id=1, source_target_pairs={{0,1},{1,0},{2,3},{3,2},{4,5},{5,4},{6,7},{7,6},{8,9},{9,8},{10,11... | collective-permute-start | bytes 786440 | tf_op jit(solution)/shard_map/ppermute | solution.py:560
  104.3 9.7 %collective-permute-start.5 = (bf16[128,1024]{1,0:T(8,128)(2,1)}, bf16[128,1024]{1,0:T(8,128)(2,1)S(1)}, u32[]{:S(2)}, u32[]{:S(2)}) collective-permute-start(bf16[128,1024]{1,0:T(8,128)(2,1)} %get-tuple-element.54), channel_id=1, source_target_pairs={{0,2},{1,3},{2,0},{3,1},{4,6},{5,7},{6,4},{7,5},{8,10},{9,11},{10,... | collective-permute-start | bytes 786440 | tf_op jit(solution)/shard_map/ppermute | solution.py:560
  104.3 14.6 %collective-permute-start.6 = (bf16[128,1024]{1,0:T(8,128)(2,1)}, bf16[128,1024]{1,0:T(8,128)(2,1)S(1)}, u32[]{:S(2)}, u32[]{:S(2)}) collective-permute-start(bf16[128,1024]{1,0:T(8,128)(2,1)} %get-tuple-element.55), channel_id=1, source_target_pairs={{0,3},{1,2},{2,1},{3,0},{4,7},{5,6},{6,5},{7,4},{8,11},{9,10},{10,... | collective-permute-start | bytes 786440 | tf_op jit(solution)/shard_map/ppermute | solution.py:560
  108.5 10.4 %collective-permute-start.19 = (bf16[256,512]{1,0:T(8,128)(2,1)S(1)}, bf16[256,512]{1,0:T(8,128)(2,1)S(1)}, u32[]{:S(2)}, u32[]{:S(2)}) collective-permute-start(bf16[256,512]{1,0:T(8,128)(2,1)S(1)} %get-tuple-element.73), channel_id=1, source_target_pairs={{0,16},{8,24},{16,0},{24,8},{1,17},{9,25},{17,1},{25,9},{2,18},{10... | collective-permute-start | bytes 786440 | tf_op jit(solution)/shard_map/ppermute | solution.py:607
  110.0 13.3 %collective-permute-start.21 = (bf16[256,512]{1,0:T(8,128)(2,1)S(1)}, bf16[256,512]{1,0:T(8,128)(2,1)S(1)}, u32[]{:S(2)}, u32[]{:S(2)}) collective-permute-start(bf16[256,512]{1,0:T(8,128)(2,1)S(1)} %get-tuple-element.75), channel_id=1, source_target_pairs={{0,16},{8,24},{16,0},{24,8},{1,17},{9,25},{17,1},{25,9},{2,18},{10... | collective-permute-start | bytes 786440 | tf_op jit(solution)/shard_map/ppermute | solution.py:607
  112.4 32.0 %collective-permute-start.18 = (bf16[256,1024]{1,0:T(8,128)(2,1)S(1)}, bf16[256,1024]{1,0:T(8,128)(2,1)S(1)}, u32[]{:S(2)}, u32[]{:S(2)}) collective-permute-start(bf16[256,1024]{1,0:T(8,128)(2,1)S(1)} %get-tuple-element.72), channel_id=1, source_target_pairs={{0,16},{8,24},{16,0},{24,8},{1,17},{9,25},{17,1},{25,9},{2,18},{10... | collective-permute-start | bytes 1572872 | tf_op jit(solution)/shard_map/ppermute | solution.py:607
  118.9 19.9 %collective-permute-start.20 = (bf16[256,512]{1,0:T(8,128)(2,1)S(1)}, bf16[256,512]{1,0:T(8,128)(2,1)S(1)}, u32[]{:S(2)}, u32[]{:S(2)}) collective-permute-start(bf16[256,512]{1,0:T(8,128)(2,1)S(1)} %sequences_added.2), channel_id=1, source_target_pairs={{0,4},{1,5},{2,6},{3,7},{4,0},{5,1},{6,2},{7,3},{8,12},{9,13},{10,... | collective-permute-start | bytes 786440 | tf_op jit(solution)/shard_map/ppermute | solution.py:560
  123.4 21.0 %collective-permute-start.22 = (bf16[256,512]{1,0:T(8,128)(2,1)S(1)}, bf16[256,512]{1,0:T(8,128)(2,1)S(1)}, u32[]{:S(2)}, u32[]{:S(2)}) collective-permute-start(bf16[256,512]{1,0:T(8,128)(2,1)S(1)} %sequences_added.3), channel_id=1, source_target_pairs={{0,4},{1,5},{2,6},{3,7},{4,0},{5,1},{6,2},{7,3},{8,12},{9,13},{10,... | collective-permute-start | bytes 786440 | tf_op jit(solution)/shard_map/ppermute | solution.py:560
  (4 other events, 81.1 us)

commit v6 on v5

--- a/solution.py
+++ b/solution.py
@@ -578,11 +578,10 @@
 
     columns = columns_for_group(rows, halves, groups, slab, layer_input, across_cores(give))
     columns, pieces = after((columns, pieces))
-    inputs = [columns[0], None] + [swap(columns[k], k) for k in range(2, KVH)]
+    inputs = [columns[0]] + [swap(columns[k], k) for k in range(1, KVH)]
 
     grads, own, down = attention(rows, groups, queries, out_grad, keys_values, pieces)
-    columns, inputs[2:], down = after((columns, inputs[2:], down))
-    inputs[1] = swap(columns[1], 1)
+    inputs[1:], down = after((inputs[1:], down))
 
     received = [
         lax.ppermute(
@@ -590,7 +589,8 @@
         )
         for step in range(1, groups)
     ]
-    received, inputs[1] = after((received, inputs[1]))
+    returned = [grads[0], swap(grads[1], 1), swap(grads[2], 2), None]
+    received, returned[:3] = after((received, returned[:3]))
     total = own
     for part in received:
         total = total + part.astype(F32)
@@ -613,13 +613,13 @@
         ]
 
     parts = [[over_sequences(array) for array in away[kind]] for kind in range(2)]
-    returned = [grads[0]] + [swap(grads[k], k) for k in range(1, KVH)]
+    returned[3] = swap(grads[3], 3)
 
     totals = [None, None]
     rest = [None, None]
     for kind in (1, 0):
         if not kind:
-            parts[0], _ = after((parts[0], returned))
+            parts[0], _ = after((parts[0], returned[3]))
         totals[kind] = [
             added(keep, parts[kind][step - 1], kind, step) for step in range(1, groups)
         ]

time: 146 us -> 140 us (0.959)
  waiting for transfers between devices: 92.4 us -> 86.1 us
  Pallas kernels: 23.8 us -> 25.9 us
  starting transfers between devices: 26.4 us -> 24.3 us
    ppermute x14, waiting for transfers between devices: 74.3 us -> 67.1 us  [swap(): return lax.ppermute(array, 'seq', [(i, i ^ k) for i in range(cycle)])]
    ppermute x1, waiting for transfers between devices: 13.7 us -> 9.6 us  [local(): lax.ppermute(down[step - 1], 'seq', [(i + step * KVH, i) for i in range(c...]
    ppermute x3, waiting for transfers between devices: 4.32 us -> 8.15 us  [over_sequences(): lax.ppermute(array[(apart - 1) * slab:apart * slab], 'dp', [(i, i ^ 2 * a...]
    ppermute x14, starting transfers between devices: 14.2 us -> 11.9 us  [swap(): return lax.ppermute(array, 'seq', [(i, i ^ k) for i in range(cycle)])]
  transfers between devices with their start and end apart: 24 -> 24, of which waited for: 13 -> 14; matrix products, arithmetic and copies ran while one was open for 0% -> 0% of each run, Pallas kernels for 13% -> 15%
where the time goes in v6:
time: 140 us; the launch traced here: 139 us
  waiting for transfers between devices  86.1 us (62%)
  Pallas kernels  25.9 us (18%)
  starting transfers between devices  24.3 us (17%)
    ppermute x14, waiting for transfers between devices, swap(): return lax.ppermute(array, 'seq', [(i, i ^ k) for i in range(cycle)])  67.1 us
    pallas_call x1, Pallas kernels, attention(): pl.pallas_call(lambda *refs: attention_kernel(rows, groups, *refs), out_s...  11.9 us
    ppermute x14, starting transfers between devices, swap(): return lax.ppermute(array, 'seq', [(i, i ^ k) for i in range(cycle)])  11.9 us
    ppermute x1, waiting for transfers between devices, local(): lax.ppermute(down[step - 1], 'seq', [(i + step * KVH, i) for i in range(c...  9.6 us
    ppermute x3, waiting for transfers between devices, over_sequences(): lax.ppermute(array[(apart - 1) * slab:apart * slab], 'dp', [(i, i ^ 2 * a...  8.15 us
    all_to_all x1, starting transfers between devices, exchange(): lax.all_to_all(array, 'seq', split_axis=0, concat_axis=0, tiled=True, axi...  6.82 us
    ppermute x3, starting transfers between devices, over_sequences(): lax.ppermute(array[(apart - 1) * slab:apart * slab], 'dp', [(i, i ^ 2 * a...  3.61 us
    pallas_call x1, Pallas kernels, packed(): pl.pallas_call(lambda *refs: pack_kernel(rows, groups, halves, *refs), ou...  3.25 us
  transfers between devices with their start and end apart: 24, of which 14 were waited for; matrix products, arithmetic and copies ran while one was open for 0% of the time, Pallas kernels for 15%

profile of v6, /device:TPU:0, one launch (start us, length us, event | category | flops | bytes accessed | tf_op | source)
XLA Modules:
  0.0 139.0 jit_solution(6415274430461445545)
XLA Ops:
  0.6 3.2 %first_sends.1 = (bf16[8,128,256]{2,1,0:T(8,128)(2,1)}, bf16[128,2048]{1,0:T(8,128)(2,1)}, bf16[128,2048]{1,0:T(8,128)(2,1)}, bf16[128,2048]{1,0:T(8,128)(2,1)}, bf16[128,4096]{1,0:T(8,128)(2,1)}) custom-call(bf16[128,4096]{1,0:T(8,128)(2,1)} %refs_0_.5, bf16[128,4096]{1,0:T(8,128)(2,1)} %refs_1_.3, bf16[128,512]{1,0:T(8,128)(2,1)} %refs_2_.1, ...), custom_call_target="tpu_custom_call" | custom-call | bytes 8000000 | tf_op jit(solution)/shard_map/first_sends/pallas_call | solution.py:93
  4.4 6.8 %all-to-all-start = ((bf16[8,128,256]{2,1,0:T(8,128)(2,1)}), bf16[8,128,256]{2,1,0:T(8,128)(2,1)}, u32[]{:S(2)}, u32[]{:S(2)}) async-start(bf16[8,128,256]{2,1,0:T(8,128)(2,1)} %get-tuple-element.53), calls=%async_computation | async-start | bytes 1048576 | tf_op jit(solution)/shard_map/all_to_all | solution.py:566
  11.2 2.0 %collective-permute-start.1 = (bf16[128,2048]{1,0:T(8,128)(2,1)}, bf16[128,2048]{1,0:T(8,128)(2,1)S(1)}, u32[]{:S(2)}, u32[]{:S(2)}) collective-permute-start(bf16[128,2048]{1,0:T(8,128)(2,1)} %get-tuple-element.47), channel_id=1, source_target_pairs={{0,1},{1,0},{2,3},{3,2},{4,5},{5,4},{6,7},{7,6},{8,9},{9,8},{10,11... | collective-permute-start | bytes 1572872 | tf_op jit(solution)/shard_map/ppermute | solution.py:560
  15.7 2.7 %input_columns.1 = (bf16[256,1024]{1,0:T(8,128)(2,1)}, bf16[256,1024]{1,0:T(8,128)(2,1)}, bf16[256,1024]{1,0:T(8,128)(2,1)}, bf16[256,1024]{1,0:T(8,128)(2,1)}) custom-call(bf16[128,8192]{1,0:T(8,128)(2,1)} %refs_0_.4, bf16[128,4096]{1,0:T(8,128)(2,1)} %copy-done.2), custom_call_target="tpu_custom_call" | custom-call | bytes 8000000 | tf_op jit(solution)/shard_map/input_columns/pallas_call | solution.py:177
  18.4 12.6 %collective-permute-done.1.refs_3_ = bf16[128,2048]{1,0:T(8,128)(2,1)S(1)} collective-permute-done((bf16[128,2048]{1,0:T(8,128)(2,1)}, bf16[128,2048]{1,0:T(8,128)(2,1)S(1)}, u32[]{:S(2)}, u32[]{:S(2)}) %collective-permute-start.1) | collective-permute-done | bytes 524320 | tf_op jit(solution)/shard_map/ppermute | solution.py:560
  31.1 3.6 %collective-permute-done.2.refs_4_ = bf16[128,2048]{1,0:T(8,128)(2,1)} collective-permute-done((bf16[128,2048]{1,0:T(8,128)(2,1)}, bf16[128,2048]{1,0:T(8,128)(2,1)}, u32[]{:S(2)}, u32[]{:S(2)}) %collective-permute-start.2) | collective-permute-done | bytes 524320 | tf_op jit(solution)/shard_map/ppermute | solution.py:560
  34.7 11.4 %collective-permute-done.3.refs_5_ = bf16[128,2048]{1,0:T(8,128)(2,1)} collective-permute-done((bf16[128,2048]{1,0:T(8,128)(2,1)}, bf16[128,2048]{1,0:T(8,128)(2,1)}, u32[]{:S(2)}, u32[]{:S(2)}) %collective-permute-start.3) | collective-permute-done | bytes 524320 | tf_op jit(solution)/shard_map/ppermute | solution.py:560
  47.0 2.6 %collective-permute-start.6 = (bf16[256,1024]{1,0:T(8,128)(2,1)}, bf16[256,1024]{1,0:T(8,128)(2,1)}, u32[]{:S(2)}, u32[]{:S(2)}) collective-permute-start(bf16[256,1024]{1,0:T(8,128)(2,1)} %get-tuple-element.52), channel_id=1, source_target_pairs={{0,3},{1,2},{2,1},{3,0},{4,7},{5,6},{6,5},{7,4},{8,11},{9,10},{10,... | collective-permute-start | bytes 1572872 | tf_op jit(solution)/shard_map/ppermute | solution.py:560
  49.6 11.9 %attention.1 = (bf16[128,1024]{1,0:T(8,128)(2,1)}, bf16[128,1024]{1,0:T(8,128)(2,1)}, bf16[128,1024]{1,0:T(8,128)(2,1)}, bf16[128,1024]{1,0:T(8,128)(2,1)}, f32[...) custom-call(bf16[128,4096]{1,0:T(8,128)(2,1)} %refs_0_.5, bf16[128,4096]{1,0:T(8,128)(2,1)} %refs_1_.3, ...), custom_call_target="tpu_custom_call" | custom-call | flops 10000000000 | bytes 50000000 | tf_op jit(solution)/shard_map/attention/pallas_call | solution.py:367
  62.5 11.5 %collective-permute-done.6.refs_11_.refs_3_ = bf16[256,1024]{1,0:T(8,128)(2,1)} collective-permute-done((bf16[256,1024]{1,0:T(8,128)(2,1)}, bf16[256,1024]{1,0:T(8,128)(2,1)}, u32[]{:S(2)}, u32[]{:S(2)}) %collective-permute-start.6) | collective-permute-done | bytes 524320 | tf_op jit(solution)/shard_map/ppermute | solution.py:560
  75.3 2.2 %collective-permute-done.8.refs_1_ = bf16[128,1024]{1,0:T(8,128)(2,1)S(1)} collective-permute-done((bf16[128,1024]{1,0:T(8,128)(2,1)}, bf16[128,1024]{1,0:T(8,128)(2,1)S(1)}, u32[]{:S(2)}, u32[]{:S(2)}) %collective-permute-start.8) | collective-permute-done | bytes 262176 | tf_op jit(solution)/shard_map/ppermute | solution.py:560
  77.6 9.6 %collective-permute-done.7 = bf16[512,256]{1,0:T(8,128)(2,1)S(1)} collective-permute-done((bf16[512,256]{1,0:T(8,128)(2,1)}, bf16[512,256]{1,0:T(8,128)(2,1)S(1)}, u32[]{:S(2)}, u32[]{:S(2)}) %collective-permute-start.7) | collective-permute-done | bytes 262176 | tf_op jit(solution)/shard_map/ppermute | solution.py:587
  88.4 1.9 %collective-permute-start.12 = (bf16[512,256]{1,0:T(8,128)(2,1)S(1)}, bf16[512,256]{1,0:T(8,128)(2,1)S(1)}, u32[]{:S(2)}, u32[]{:S(2)}) collective-permute-start(bf16[512,256]{1,0:T(8,128)(2,1)S(1)} %add_convert_fusion.refs_0_), channel_id=1, source_target_pairs={{0,2},{1,3},{2,0},{3,1},{4,6},{5,7},{6,4},{7,5},{8,10},{9,11},{10,... | collective-permute-start | bytes 786440 | tf_op jit(solution)/shard_map/ppermute | solution.py:560
  90.3 1.5 %collective-permute-start.11 = (bf16[512,256]{1,0:T(8,128)(2,1)S(1)}, bf16[512,256]{1,0:T(8,128)(2,1)S(1)}, u32[]{:S(2)}, u32[]{:S(2)}) collective-permute-start(bf16[512,256]{1,0:T(8,128)(2,1)S(1)} %add_convert_fusion.refs_0_), channel_id=1, source_target_pairs={{0,1},{1,0},{2,3},{3,2},{4,5},{5,4},{6,7},{7,6},{8,9},{9,8},{10,11... | collective-permute-start | bytes 786440 | tf_op jit(solution)/shard_map/ppermute | solution.py:560
  91.9 5.6 %collective-permute-done.13.refs_3_ = bf16[512,256]{1,0:T(8,128)(2,1)S(1)} collective-permute-done((bf16[512,256]{1,0:T(8,128)(2,1)S(1)}, bf16[512,256]{1,0:T(8,128)(2,1)S(1)}, u32[]{:S(2)}, u32[]{:S(2)}) %collective-permute-start.13) | collective-permute-done | bytes 262176 | tf_op jit(solution)/shard_map/ppermute | solution.py:560
  98.0 2.1 %collective-permute-done.11.refs_1_ = bf16[512,256]{1,0:T(8,128)(2,1)S(1)} collective-permute-done((bf16[512,256]{1,0:T(8,128)(2,1)S(1)}, bf16[512,256]{1,0:T(8,128)(2,1)S(1)}, u32[]{:S(2)}, u32[]{:S(2)}) %collective-permute-start.11) | collective-permute-done | bytes 262176 | tf_op jit(solution)/shard_map/ppermute | solution.py:560
  101.7 2.9 %weight_terms_away.1 = (bf16[256,512]{1,0:T(8,128)(2,1)S(1)}, bf16[256,512]{1,0:T(8,128)(2,1)S(1)}, bf16[128,512]{1,0:T(8,128)(2,1)}, bf16[128,512]{1,0:T(8,128)(2,1)}, bf16[1024,1024]{1,0:T(8,128)(2,1)S(1)}) custom-call(bf16[512,256]{1,0:T(8,128)(2,1)S(1)} %add_convert_fusion.refs_0_, bf16[512,256]{1,0:T(8,128)(2,1)S(1)} %collective-permute-done.11.refs_1_, ...), custom_call_target="tpu_custom_call" | custom-call | flops 1000000000 | bytes 6000000 | tf_op jit(solution)/shard_map/weight_terms_away/pallas_call | solution.py:435
  104.5 1.5 %collective-permute-start.19 = (bf16[256,512]{1,0:T(8,128)(2,1)S(1)}, bf16[256,512]{1,0:T(8,128)(2,1)S(1)}, u32[]{:S(2)}, u32[]{:S(2)}) collective-permute-start(bf16[256,512]{1,0:T(8,128)(2,1)S(1)} %get-tuple-element.77), channel_id=1, source_target_pairs={{0,16},{8,24},{16,0},{24,8},{1,17},{9,25},{17,1},{25,9},{2,18},{10... | collective-permute-start | bytes 786440 | tf_op jit(solution)/shard_map/ppermute | solution.py:607
  106.5 2.9 %weight_terms_near.1 = (f32[512,1024]{1,0:T(8,128)S(1)}, bf16[256,1024]{1,0:T(8,128)(2,1)S(1)}) custom-call(bf16[256,1024]{1,0:T(8,128)(2,1)S(1)} %copy-done, bf16[256,1024]{1,0:T(8,128)(2,1)S(1)} %collective-permute-done.4.refs_9_.refs_1_, bf16[256,1024]{1,0:T(8,128)(2,1)S(1)} %collective-permute-done.5.refs_10_.refs_2_, ...), custom_call_target="tpu_custom_call" | custom-call | flops 2000000000 | bytes 6000000 | tf_op jit(solution)/shard_map/weight_terms_near/pallas_call | solution.py:463
  109.4 1.6 %collective-permute-start.18 = (bf16[256,1024]{1,0:T(8,128)(2,1)S(1)}, bf16[256,1024]{1,0:T(8,128)(2,1)S(1)}, u32[]{:S(2)}, u32[]{:S(2)}) collective-permute-start(bf16[256,1024]{1,0:T(8,128)(2,1)S(1)} %get-tuple-element.76), channel_id=1, source_target_pairs={{0,16},{8,24},{16,0},{24,8},{1,17},{9,25},{17,1},{25,9},{2,18},{10... | collective-permute-start | bytes 1572872 | tf_op jit(solution)/shard_map/ppermute | solution.py:607
  111.0 2.7 %collective-permute-done.19.refs_1_ = bf16[256,512]{1,0:T(8,128)(2,1)S(1)} collective-permute-done((bf16[256,512]{1,0:T(8,128)(2,1)S(1)}, bf16[256,512]{1,0:T(8,128)(2,1)S(1)}, u32[]{:S(2)}, u32[]{:S(2)}) %collective-permute-start.19) | collective-permute-done | bytes 262176 | tf_op jit(solution)/shard_map/ppermute | solution.py:607
  113.8 5.5 %collective-permute-done.21.refs_1_ = bf16[256,512]{1,0:T(8,128)(2,1)S(1)} collective-permute-done((bf16[256,512]{1,0:T(8,128)(2,1)S(1)}, bf16[256,512]{1,0:T(8,128)(2,1)S(1)}, u32[]{:S(2)}, u32[]{:S(2)}) %collective-permute-start.21) | collective-permute-done | bytes 262176 | tf_op jit(solution)/shard_map/ppermute | solution.py:607
  120.5 11.9 %collective-permute-done.20.refs_2_ = bf16[256,512]{1,0:T(8,128)(2,1)S(1)} collective-permute-done((bf16[256,512]{1,0:T(8,128)(2,1)S(1)}, bf16[256,512]{1,0:T(8,128)(2,1)S(1)}, u32[]{:S(2)}, u32[]{:S(2)}) %collective-permute-start.20) | collective-permute-done | bytes 262176 | tf_op jit(solution)/shard_map/ppermute | solution.py:560
  132.4 5.5 %collective-permute-done.22.refs_3_ = bf16[256,512]{1,0:T(8,128)(2,1)S(1)} collective-permute-done((bf16[256,512]{1,0:T(8,128)(2,1)S(1)}, bf16[256,512]{1,0:T(8,128)(2,1)S(1)}, u32[]{:S(2)}, u32[]{:S(2)}) %collective-permute-start.22) | collective-permute-done | bytes 262176 | tf_op jit(solution)/shard_map/ppermute | solution.py:560
  (42 shorter events, 12.3 us)
Async XLA Ops:
  3.9 10.9 %collective-permute-start = (bf16[128,4096]{1,0:T(8,128)(2,1)}, bf16[128,4096]{1,0:T(8,128)(2,1)S(1)}, u32[]{:S(2)}, u32[]{:S(2)}) collective-permute-start(bf16[128,4096]{1,0:T(8,128)(2,1)} %get-tuple-element.42), channel_id=1, source_target_pairs={{0,8},{8,0},{16,24},{24,16},{1,9},{9,1},{17,25},{25,17},{2,10},{10... | collective-permute-start | bytes 3145736 | tf_op jit(solution)/shard_map/ppermute | solution.py:563
  4.4 45.2 %all-to-all-start = ((bf16[8,128,256]{2,1,0:T(8,128)(2,1)}), bf16[8,128,256]{2,1,0:T(8,128)(2,1)}, u32[]{:S(2)}, u32[]{:S(2)}) async-start(bf16[8,128,256]{2,1,0:T(8,128)(2,1)} %get-tuple-element.53), calls=%async_computation | async-start | bytes 1048576 | tf_op jit(solution)/shard_map/all_to_all | solution.py:566
  11.2 19.9 %collective-permute-start.1 = (bf16[128,2048]{1,0:T(8,128)(2,1)}, bf16[128,2048]{1,0:T(8,128)(2,1)S(1)}, u32[]{:S(2)}, u32[]{:S(2)}) collective-permute-start(bf16[128,2048]{1,0:T(8,128)(2,1)} %get-tuple-element.47), channel_id=1, source_target_pairs={{0,1},{1,0},{2,3},{3,2},{4,5},{5,4},{6,7},{7,6},{8,9},{9,8},{10,11... | collective-permute-start | bytes 1572872 | tf_op jit(solution)/shard_map/ppermute | solution.py:560
  13.3 21.5 %collective-permute-start.2 = (bf16[128,2048]{1,0:T(8,128)(2,1)}, bf16[128,2048]{1,0:T(8,128)(2,1)}, u32[]{:S(2)}, u32[]{:S(2)}) collective-permute-start(bf16[128,2048]{1,0:T(8,128)(2,1)} %get-tuple-element.48), channel_id=1, source_target_pairs={{0,2},{1,3},{2,0},{3,1},{4,6},{5,7},{6,4},{7,5},{8,10},{9,11},{10,... | collective-permute-start | bytes 1572872 | tf_op jit(solution)/shard_map/ppermute | solution.py:560
  14.7 31.4 %collective-permute-start.3 = (bf16[128,2048]{1,0:T(8,128)(2,1)}, bf16[128,2048]{1,0:T(8,128)(2,1)}, u32[]{:S(2)}, u32[]{:S(2)}) collective-permute-start(bf16[128,2048]{1,0:T(8,128)(2,1)} %get-tuple-element.49), channel_id=1, source_target_pairs={{0,3},{1,2},{2,1},{3,0},{4,7},{5,6},{6,5},{7,4},{8,11},{9,10},{10,... | collective-permute-start | bytes 1572872 | tf_op jit(solution)/shard_map/ppermute | solution.py:560
  46.1 16.4 %collective-permute-start.4 = (bf16[256,1024]{1,0:T(8,128)(2,1)}, bf16[256,1024]{1,0:T(8,128)(2,1)S(1)}, u32[]{:S(2)}, u32[]{:S(2)}) collective-permute-start(bf16[256,1024]{1,0:T(8,128)(2,1)} %get-tuple-element.50), channel_id=1, source_target_pairs={{0,1},{1,0},{2,3},{3,2},{4,5},{5,4},{6,7},{7,6},{8,9},{9,8},{10,11... | collective-permute-start | bytes 1572872 | tf_op jit(solution)/shard_map/ppermute | solution.py:560
  46.7 15.8 %collective-permute-start.5 = (bf16[256,1024]{1,0:T(8,128)(2,1)}, bf16[256,1024]{1,0:T(8,128)(2,1)S(1)}, u32[]{:S(2)}, u32[]{:S(2)}) collective-permute-start(bf16[256,1024]{1,0:T(8,128)(2,1)} %get-tuple-element.51), channel_id=1, source_target_pairs={{0,2},{1,3},{2,0},{3,1},{4,6},{5,7},{6,4},{7,5},{8,10},{9,11},{10,... | collective-permute-start | bytes 1572872 | tf_op jit(solution)/shard_map/ppermute | solution.py:560
  47.0 27.0 %collective-permute-start.6 = (bf16[256,1024]{1,0:T(8,128)(2,1)}, bf16[256,1024]{1,0:T(8,128)(2,1)}, u32[]{:S(2)}, u32[]{:S(2)}) collective-permute-start(bf16[256,1024]{1,0:T(8,128)(2,1)} %get-tuple-element.52), channel_id=1, source_target_pairs={{0,3},{1,2},{2,1},{3,0},{4,7},{5,6},{6,5},{7,4},{8,11},{9,10},{10,... | collective-permute-start | bytes 1572872 | tf_op jit(solution)/shard_map/ppermute | solution.py:560
  61.6 16.0 %collective-permute-start.8 = (bf16[128,1024]{1,0:T(8,128)(2,1)}, bf16[128,1024]{1,0:T(8,128)(2,1)S(1)}, u32[]{:S(2)}, u32[]{:S(2)}) collective-permute-start(bf16[128,1024]{1,0:T(8,128)(2,1)} %get-tuple-element.60), channel_id=1, source_target_pairs={{0,1},{1,0},{2,3},{3,2},{4,5},{5,4},{6,7},{7,6},{8,9},{9,8},{10,11... | collective-permute-start | bytes 786440 | tf_op jit(solution)/shard_map/ppermute | solution.py:560
  62.2 15.4 %collective-permute-start.9 = (bf16[128,1024]{1,0:T(8,128)(2,1)}, bf16[128,1024]{1,0:T(8,128)(2,1)S(1)}, u32[]{:S(2)}, u32[]{:S(2)}) collective-permute-start(bf16[128,1024]{1,0:T(8,128)(2,1)} %get-tuple-element.61), channel_id=1, source_target_pairs={{0,2},{1,3},{2,0},{3,1},{4,6},{5,7},{6,4},{7,5},{8,10},{9,11},{10,... | collective-permute-start | bytes 786440 | tf_op jit(solution)/shard_map/ppermute | solution.py:560
  74.1 13.2 %collective-permute-start.7 = (bf16[512,256]{1,0:T(8,128)(2,1)}, bf16[512,256]{1,0:T(8,128)(2,1)S(1)}, u32[]{:S(2)}, u32[]{:S(2)}) collective-permute-start(bf16[512,256]{1,0:T(8,128)(2,1)} %get-tuple-element.58), channel_id=1, source_target_pairs={{4,0},{5,1},{6,2},{7,3},{12,8},{13,9},{14,10},{15,11},{20,16},{21,... | collective-permute-start | bytes 786440 | tf_op jit(solution)/shard_map/ppermute | solution.py:587
  88.3 9.1 %collective-permute-start.13 = (bf16[512,256]{1,0:T(8,128)(2,1)S(1)}, bf16[512,256]{1,0:T(8,128)(2,1)S(1)}, u32[]{:S(2)}, u32[]{:S(2)}) collective-permute-start(bf16[512,256]{1,0:T(8,128)(2,1)S(1)} %add_convert_fusion.refs_0_), channel_id=1, source_target_pairs={{0,3},{1,2},{2,1},{3,0},{4,7},{5,6},{6,5},{7,4},{8,11},{9,10},{10,... | collective-permute-start | bytes 786440 | tf_op jit(solution)/shard_map/ppermute | solution.py:560
  88.4 9.5 %collective-permute-start.12 = (bf16[512,256]{1,0:T(8,128)(2,1)S(1)}, bf16[512,256]{1,0:T(8,128)(2,1)S(1)}, u32[]{:S(2)}, u32[]{:S(2)}) collective-permute-start(bf16[512,256]{1,0:T(8,128)(2,1)S(1)} %add_convert_fusion.refs_0_), channel_id=1, source_target_pairs={{0,2},{1,3},{2,0},{3,1},{4,6},{5,7},{6,4},{7,5},{8,10},{9,11},{10,... | collective-permute-start | bytes 786440 | tf_op jit(solution)/shard_map/ppermute | solution.py:560
  90.3 9.8 %collective-permute-start.11 = (bf16[512,256]{1,0:T(8,128)(2,1)S(1)}, bf16[512,256]{1,0:T(8,128)(2,1)S(1)}, u32[]{:S(2)}, u32[]{:S(2)}) collective-permute-start(bf16[512,256]{1,0:T(8,128)(2,1)S(1)} %add_convert_fusion.refs_0_), channel_id=1, source_target_pairs={{0,1},{1,0},{2,3},{3,2},{4,5},{5,4},{6,7},{7,6},{8,9},{9,8},{10,11... | collective-permute-start | bytes 786440 | tf_op jit(solution)/shard_map/ppermute | solution.py:560
  91.9 8.5 %collective-permute-start.14 = (bf16[512,256]{1,0:T(8,128)(2,1)S(1)}, bf16[512,256]{1,0:T(8,128)(2,1)S(1)}, u32[]{:S(2)}, u32[]{:S(2)}) collective-permute-start(bf16[512,256]{1,0:T(8,128)(2,1)S(1)} %add_convert_fusion.refs_0_), channel_id=1, source_target_pairs={{0,8},{8,0},{16,24},{24,16},{1,9},{9,1},{17,25},{25,17},{2,10},{10... | collective-permute-start | bytes 786440 | tf_op jit(solution)/shard_map/ppermute | solution.py:563
  97.5 3.0 %collective-permute-start.17 = (bf16[512,256]{1,0:T(8,128)(2,1)S(1)}, bf16[512,256]{1,0:T(8,128)(2,1)S(1)}, u32[]{:S(2)}, u32[]{:S(2)}) collective-permute-start(bf16[512,256]{1,0:T(8,128)(2,1)S(1)} %collective-permute-done.13.refs_3_), channel_id=1, source_target_pairs={{0,8},{8,0},{16,24},{24,16},{1,9},{9,1},{17,25},{25,17},{2,10},{10... | collective-permute-start | bytes 786440 | tf_op jit(solution)/shard_map/ppermute | solution.py:563
  97.9 2.5 %collective-permute-start.16 = (bf16[512,256]{1,0:T(8,128)(2,1)S(1)}, bf16[512,256]{1,0:T(8,128)(2,1)S(1)}, u32[]{:S(2)}, u32[]{:S(2)}) collective-permute-start(bf16[512,256]{1,0:T(8,128)(2,1)S(1)} %collective-permute-done.12.refs_2_), channel_id=1, source_target_pairs={{0,8},{8,0},{16,24},{24,16},{1,9},{9,1},{17,25},{25,17},{2,10},{10... | collective-permute-start | bytes 786440 | tf_op jit(solution)/shard_map/ppermute | solution.py:563
  100.1 1.5 %collective-permute-start.15 = (bf16[512,256]{1,0:T(8,128)(2,1)S(1)}, bf16[512,256]{1,0:T(8,128)(2,1)S(1)}, u32[]{:S(2)}, u32[]{:S(2)}) collective-permute-start(bf16[512,256]{1,0:T(8,128)(2,1)S(1)} %collective-permute-done.11.refs_1_), channel_id=1, source_target_pairs={{0,8},{8,0},{16,24},{24,16},{1,9},{9,1},{17,25},{25,17},{2,10},{10... | collective-permute-start | bytes 786440 | tf_op jit(solution)/shard_map/ppermute | solution.py:563
  100.1 10.9 %collective-permute-start.10 = (bf16[128,1024]{1,0:T(8,128)(2,1)}, bf16[128,1024]{1,0:T(8,128)(2,1)S(1)}, u32[]{:S(2)}, u32[]{:S(2)}) collective-permute-start(bf16[128,1024]{1,0:T(8,128)(2,1)} %get-tuple-element.65), channel_id=1, source_target_pairs={{0,3},{1,2},{2,1},{3,0},{4,7},{5,6},{6,5},{7,4},{8,11},{9,10},{10,... | collective-permute-start | bytes 786440 | tf_op jit(solution)/shard_map/ppermute | solution.py:560
  104.5 9.2 %collective-permute-start.19 = (bf16[256,512]{1,0:T(8,128)(2,1)S(1)}, bf16[256,512]{1,0:T(8,128)(2,1)S(1)}, u32[]{:S(2)}, u32[]{:S(2)}) collective-permute-start(bf16[256,512]{1,0:T(8,128)(2,1)S(1)} %get-tuple-element.77), channel_id=1, source_target_pairs={{0,16},{8,24},{16,0},{24,8},{1,17},{9,25},{17,1},{25,9},{2,18},{10... | collective-permute-start | bytes 786440 | tf_op jit(solution)/shard_map/ppermute | solution.py:607
  106.0 13.3 %collective-permute-start.21 = (bf16[256,512]{1,0:T(8,128)(2,1)S(1)}, bf16[256,512]{1,0:T(8,128)(2,1)S(1)}, u32[]{:S(2)}, u32[]{:S(2)}) collective-permute-start(bf16[256,512]{1,0:T(8,128)(2,1)S(1)} %get-tuple-element.79), channel_id=1, source_target_pairs={{0,16},{8,24},{16,0},{24,8},{1,17},{9,25},{17,1},{25,9},{2,18},{10... | collective-permute-start | bytes 786440 | tf_op jit(solution)/shard_map/ppermute | solution.py:607
  109.4 28.5 %collective-permute-start.18 = (bf16[256,1024]{1,0:T(8,128)(2,1)S(1)}, bf16[256,1024]{1,0:T(8,128)(2,1)S(1)}, u32[]{:S(2)}, u32[]{:S(2)}) collective-permute-start(bf16[256,1024]{1,0:T(8,128)(2,1)S(1)} %get-tuple-element.76), channel_id=1, source_target_pairs={{0,16},{8,24},{16,0},{24,8},{1,17},{9,25},{17,1},{25,9},{2,18},{10... | collective-permute-start | bytes 1572872 | tf_op jit(solution)/shard_map/ppermute | solution.py:607
  113.7 18.7 %collective-permute-start.20 = (bf16[256,512]{1,0:T(8,128)(2,1)S(1)}, bf16[256,512]{1,0:T(8,128)(2,1)S(1)}, u32[]{:S(2)}, u32[]{:S(2)}) collective-permute-start(bf16[256,512]{1,0:T(8,128)(2,1)S(1)} %sequences_added.2), channel_id=1, source_target_pairs={{0,4},{1,5},{2,6},{3,7},{4,0},{5,1},{6,2},{7,3},{8,12},{9,13},{10,... | collective-permute-start | bytes 786440 | tf_op jit(solution)/shard_map/ppermute | solution.py:560
  119.3 18.6 %collective-permute-start.22 = (bf16[256,512]{1,0:T(8,128)(2,1)S(1)}, bf16[256,512]{1,0:T(8,128)(2,1)S(1)}, u32[]{:S(2)}, u32[]{:S(2)}) collective-permute-start(bf16[256,512]{1,0:T(8,128)(2,1)S(1)} %sequences_added.3), channel_id=1, source_target_pairs={{0,4},{1,5},{2,6},{3,7},{4,0},{5,1},{6,2},{7,3},{8,12},{9,13},{10,... | collective-permute-start | bytes 786440 | tf_op jit(solution)/shard_map/ppermute | solution.py:560
  (4 other events, 77.3 us)

commit v7 on v6

--- a/solution.py
+++ b/solution.py
@@ -20,6 +20,7 @@
 F32 = jnp.float32
 VMEM_BYTES = 24 * 1024 * 1024
 ALL_VMEM_BYTES = 62 * 1024 * 1024
+ATTENTION_VMEM_BYTES = 40 * 1024 * 1024
 
 NT = (((1,), (1,)), ((), ()))
 
@@ -383,7 +384,7 @@
             pltpu.SemaphoreType.DMA((WIDE // PART, 2 * KVH)),
             pltpu.SemaphoreType.DMA((WIDE // PART, KVH)),
         ],
-        compiler_params=pltpu.CompilerParams(vmem_limit_bytes=ALL_VMEM_BYTES),
+        compiler_params=pltpu.CompilerParams(vmem_limit_bytes=ATTENTION_VMEM_BYTES),
         cost_estimate=pl.CostEstimate(flops=10**10, bytes_accessed=5 * 10**7, transcendentals=0),
         name="attention",
     )(queries, out_grad, keys_values, *pieces)

time: 140 us -> 138 us (0.986)
  Pallas kernels: 25.9 us -> 24.3 us
    ppermute x14, waiting for transfers between devices: 67.1 us -> 68.8 us  [swap(): return lax.ppermute(array, 'seq', [(i, i ^ k) for i in range(cycle)])]
    pallas_call x1, Pallas kernels: 11.9 us -> 10.3 us  [attention(): pl.pallas_call(lambda *refs: attention_kernel(rows, groups, *refs), out_s...]
  transfers between devices with their start and end apart: 24 -> 24, of which waited for: 14 -> 16; matrix products, arithmetic and copies ran while one was open for 0% -> 0% of each run, Pallas kernels for 15% -> 15%
where the time goes in v7:
time: 138 us; the launch traced here: 137 us
  waiting for transfers between devices  86 us (62%)
  starting transfers between devices  24.9 us (18%)
  Pallas kernels  24.3 us (18%)
    ppermute x14, waiting for transfers between devices, swap(): return lax.ppermute(array, 'seq', [(i, i ^ k) for i in range(cycle)])  68.8 us
    ppermute x14, starting transfers between devices, swap(): return lax.ppermute(array, 'seq', [(i, i ^ k) for i in range(cycle)])  12.4 us
    pallas_call x1, Pallas kernels, attention(): pl.pallas_call(lambda *refs: attention_kernel(rows, groups, *refs), out_s...  10.3 us
    ppermute x1, waiting for transfers between devices, local(): lax.ppermute(down[step - 1], 'seq', [(i + step * KVH, i) for i in range(c...  8.38 us
    ppermute x3, waiting for transfers between devices, over_sequences(): lax.ppermute(array[(apart - 1) * slab:apart * slab], 'dp', [(i, i ^ 2 * a...  8.13 us
    all_to_all x1, starting transfers between devices, exchange(): lax.all_to_all(array, 'seq', split_axis=0, concat_axis=0, tiled=True, axi...  6.97 us
    ppermute x3, starting transfers between devices, over_sequences(): lax.ppermute(array[(apart - 1) * slab:apart * slab], 'dp', [(i, i ^ 2 * a...  3.63 us
    pallas_call x1, Pallas kernels, packed(): pl.pallas_call(lambda *refs: pack_kernel(rows, groups, halves, *refs), ou...  3.25 us
  transfers between devices with their start and end apart: 24, of which 16 were waited for; matrix products, arithmetic and copies ran while one was open for 0% of the time, Pallas kernels for 15%

profile of v7, /device:TPU:0, one launch (start us, length us, event | category | flops | bytes accessed | tf_op | source)
XLA Modules:
  0.0 137.2 jit_solution(5072281168600943530)
XLA Ops:
  0.6 3.2 %first_sends.1 = (bf16[8,128,256]{2,1,0:T(8,128)(2,1)}, bf16[128,2048]{1,0:T(8,128)(2,1)}, bf16[128,2048]{1,0:T(8,128)(2,1)}, bf16[128,2048]{1,0:T(8,128)(2,1)}, bf16[128,4096]{1,0:T(8,128)(2,1)}) custom-call(bf16[128,4096]{1,0:T(8,128)(2,1)} %refs_0_.5, bf16[128,4096]{1,0:T(8,128)(2,1)} %refs_1_.3, bf16[128,512]{1,0:T(8,128)(2,1)} %refs_2_.1, ...), custom_call_target="tpu_custom_call" | custom-call | bytes 8000000 | tf_op jit(solution)/shard_map/first_sends/pallas_call | solution.py:94
  4.4 7.0 %all-to-all-start = ((bf16[8,128,256]{2,1,0:T(8,128)(2,1)}), bf16[8,128,256]{2,1,0:T(8,128)(2,1)S(1)}, u32[]{:S(2)}, u32[]{:S(2)}) async-start(bf16[8,128,256]{2,1,0:T(8,128)(2,1)} %get-tuple-element.53), calls=%async_computation | async-start | bytes 1048576 | tf_op jit(solution)/shard_map/all_to_all | solution.py:567
  11.4 2.0 %collective-permute-start.1 = (bf16[128,2048]{1,0:T(8,128)(2,1)}, bf16[128,2048]{1,0:T(8,128)(2,1)}, u32[]{:S(2)}, u32[]{:S(2)}) collective-permute-start(bf16[128,2048]{1,0:T(8,128)(2,1)} %get-tuple-element.47), channel_id=1, source_target_pairs={{0,1},{1,0},{2,3},{3,2},{4,5},{5,4},{6,7},{7,6},{8,9},{9,8},{10,11... | collective-permute-start | bytes 1572872 | tf_op jit(solution)/shard_map/ppermute | solution.py:561
  13.4 1.5 %collective-permute-start.2 = (bf16[128,2048]{1,0:T(8,128)(2,1)}, bf16[128,2048]{1,0:T(8,128)(2,1)}, u32[]{:S(2)}, u32[]{:S(2)}) collective-permute-start(bf16[128,2048]{1,0:T(8,128)(2,1)} %get-tuple-element.48), channel_id=1, source_target_pairs={{0,2},{1,3},{2,0},{3,1},{4,6},{5,7},{6,4},{7,5},{8,10},{9,11},{10,... | collective-permute-start | bytes 1572872 | tf_op jit(solution)/shard_map/ppermute | solution.py:561
  14.9 2.7 %input_columns.1 = (bf16[256,1024]{1,0:T(8,128)(2,1)}, bf16[256,1024]{1,0:T(8,128)(2,1)}, bf16[256,1024]{1,0:T(8,128)(2,1)}, bf16[256,1024]{1,0:T(8,128)(2,1)}) custom-call(bf16[128,8192]{1,0:T(8,128)(2,1)} %refs_0_.4, bf16[128,4096]{1,0:T(8,128)(2,1)} %collective-permute-done.refs_1_), custom_call_target="tpu_custom_call" | custom-call | bytes 8000000 | tf_op jit(solution)/shard_map/input_columns/pallas_call | solution.py:178
  17.6 13.7 %collective-permute-done.1.refs_3_ = bf16[128,2048]{1,0:T(8,128)(2,1)} collective-permute-done((bf16[128,2048]{1,0:T(8,128)(2,1)}, bf16[128,2048]{1,0:T(8,128)(2,1)}, u32[]{:S(2)}, u32[]{:S(2)}) %collective-permute-start.1) | collective-permute-done | bytes 524320 | tf_op jit(solution)/shard_map/ppermute | solution.py:561
  31.3 3.5 %collective-permute-done.2.refs_4_ = bf16[128,2048]{1,0:T(8,128)(2,1)} collective-permute-done((bf16[128,2048]{1,0:T(8,128)(2,1)}, bf16[128,2048]{1,0:T(8,128)(2,1)}, u32[]{:S(2)}, u32[]{:S(2)}) %collective-permute-start.2) | collective-permute-done | bytes 524320 | tf_op jit(solution)/shard_map/ppermute | solution.py:561
  34.9 11.4 %collective-permute-done.3.refs_5_ = bf16[128,2048]{1,0:T(8,128)(2,1)} collective-permute-done((bf16[128,2048]{1,0:T(8,128)(2,1)}, bf16[128,2048]{1,0:T(8,128)(2,1)}, u32[]{:S(2)}, u32[]{:S(2)}) %collective-permute-start.3) | collective-permute-done | bytes 524320 | tf_op jit(solution)/shard_map/ppermute | solution.py:561
  47.2 2.6 %collective-permute-start.6 = (bf16[256,1024]{1,0:T(8,128)(2,1)}, bf16[256,1024]{1,0:T(8,128)(2,1)}, u32[]{:S(2)}, u32[]{:S(2)}) collective-permute-start(bf16[256,1024]{1,0:T(8,128)(2,1)} %get-tuple-element.52), channel_id=1, source_target_pairs={{0,3},{1,2},{2,1},{3,0},{4,7},{5,6},{6,5},{7,4},{8,11},{9,10},{10,... | collective-permute-start | bytes 1572872 | tf_op jit(solution)/shard_map/ppermute | solution.py:561
  51.0 10.3 %attention.1 = (bf16[128,1024]{1,0:T(8,128)(2,1)S(1)}, bf16[128,1024]{1,0:T(8,128)(2,1)S(1)}, bf16[128,1024]{1,0:T(8,128)(2,1)S(1)}, bf16[128,1024]{1,0:T(8,128)...) custom-call(bf16[128,4096]{1,0:T(8,128)(2,1)S(1)} %copy-done, bf16[128,4096]{1,0:T(8,128)(2,1)S(1)} %copy-done.1, ...), custom_call_target="tpu_custom_call" | custom-call | flops 10000000000 | bytes 50000000 | tf_op jit(solution)/shard_map/attention/pallas_call | solution.py:368
  62.3 11.9 %collective-permute-done.6.refs_11_.refs_3_ = bf16[256,1024]{1,0:T(8,128)(2,1)} collective-permute-done((bf16[256,1024]{1,0:T(8,128)(2,1)}, bf16[256,1024]{1,0:T(8,128)(2,1)}, u32[]{:S(2)}, u32[]{:S(2)}) %collective-permute-start.6) | collective-permute-done | bytes 524320 | tf_op jit(solution)/shard_map/ppermute | solution.py:561
  75.5 2.1 %collective-permute-done.8.refs_1_ = bf16[128,1024]{1,0:T(8,128)(2,1)S(1)} collective-permute-done((bf16[128,1024]{1,0:T(8,128)(2,1)S(1)}, bf16[128,1024]{1,0:T(8,128)(2,1)S(1)}, u32[]{:S(2)}, u32[]{:S(2)}) %collective-permute-start.8) | collective-permute-done | bytes 262176 | tf_op jit(solution)/shard_map/ppermute | solution.py:561
  78.7 8.4 %collective-permute-done.7 = bf16[512,256]{1,0:T(8,128)(2,1)S(1)} collective-permute-done((bf16[512,256]{1,0:T(8,128)(2,1)S(1)}, bf16[512,256]{1,0:T(8,128)(2,1)S(1)}, u32[]{:S(2)}, u32[]{:S(2)}) %collective-permute-start.7) | collective-permute-done | bytes 262176 | tf_op jit(solution)/shard_map/ppermute | solution.py:588
  87.3 2.4 %collective-permute-start.12 = (bf16[512,256]{1,0:T(8,128)(2,1)S(1)}, bf16[512,256]{1,0:T(8,128)(2,1)S(1)}, u32[]{:S(2)}, u32[]{:S(2)}) collective-permute-start(bf16[512,256]{1,0:T(8,128)(2,1)S(1)} %add_convert_fusion.refs_0_), channel_id=1, source_target_pairs={{0,2},{1,3},{2,0},{3,1},{4,6},{5,7},{6,4},{7,5},{8,10},{9,11},{10,... | collective-permute-start | bytes 786440 | tf_op jit(solution)/shard_map/ppermute | solution.py:561
  90.7 4.5 %collective-permute-done.13.refs_3_ = bf16[512,256]{1,0:T(8,128)(2,1)S(1)} collective-permute-done((bf16[512,256]{1,0:T(8,128)(2,1)S(1)}, bf16[512,256]{1,0:T(8,128)(2,1)S(1)}, u32[]{:S(2)}, u32[]{:S(2)}) %collective-permute-start.13) | collective-permute-done | bytes 262176 | tf_op jit(solution)/shard_map/ppermute | solution.py:561
  95.2 2.3 %collective-permute-done.12.refs_2_ = bf16[512,256]{1,0:T(8,128)(2,1)S(1)} collective-permute-done((bf16[512,256]{1,0:T(8,128)(2,1)S(1)}, bf16[512,256]{1,0:T(8,128)(2,1)S(1)}, u32[]{:S(2)}, u32[]{:S(2)}) %collective-permute-start.12) | collective-permute-done | bytes 262176 | tf_op jit(solution)/shard_map/ppermute | solution.py:561
  99.5 2.9 %weight_terms_away.1 = (bf16[256,512]{1,0:T(8,128)(2,1)S(1)}, bf16[256,512]{1,0:T(8,128)(2,1)S(1)}, bf16[128,512]{1,0:T(8,128)(2,1)}, bf16[128,512]{1,0:T(8,128)(2,1)}, bf16[1024,1024]{1,0:T(8,128)(2,1)S(1)}) custom-call(bf16[512,256]{1,0:T(8,128)(2,1)S(1)} %add_convert_fusion.refs_0_, bf16[512,256]{1,0:T(8,128)(2,1)S(1)} %collective-permute-done.11.refs_1_, ...), custom_call_target="tpu_custom_call" | custom-call | flops 1000000000 | bytes 6000000 | tf_op jit(solution)/shard_map/weight_terms_away/pallas_call | solution.py:436
  102.3 1.5 %collective-permute-start.19 = (bf16[256,512]{1,0:T(8,128)(2,1)S(1)}, bf16[256,512]{1,0:T(8,128)(2,1)S(1)}, u32[]{:S(2)}, u32[]{:S(2)}) collective-permute-start(bf16[256,512]{1,0:T(8,128)(2,1)S(1)} %get-tuple-element.77), channel_id=1, source_target_pairs={{0,16},{8,24},{16,0},{24,8},{1,17},{9,25},{17,1},{25,9},{2,18},{10... | collective-permute-start | bytes 786440 | tf_op jit(solution)/shard_map/ppermute | solution.py:608
  104.3 2.9 %weight_terms_near.1 = (f32[512,1024]{1,0:T(8,128)S(1)}, bf16[256,1024]{1,0:T(8,128)(2,1)S(1)}) custom-call(bf16[256,1024]{1,0:T(8,128)(2,1)S(1)} %copy-done.2, bf16[256,1024]{1,0:T(8,128)(2,1)S(1)} %collective-permute-done.4.refs_9_.refs_1_, bf16[256,1024]{1,0:T(8,128)(2,1)S(1)} %collective-permute-done.5.refs_10_.refs_2_, ...), custom_call_target="tpu_custom_call" | custom-call | flops 2000000000 | bytes 6000000 | tf_op jit(solution)/shard_map/weight_terms_near/pallas_call | solution.py:464
  107.2 1.6 %collective-permute-start.18 = (bf16[256,1024]{1,0:T(8,128)(2,1)S(1)}, bf16[256,1024]{1,0:T(8,128)(2,1)S(1)}, u32[]{:S(2)}, u32[]{:S(2)}) collective-permute-start(bf16[256,1024]{1,0:T(8,128)(2,1)S(1)} %get-tuple-element.76), channel_id=1, source_target_pairs={{0,16},{8,24},{16,0},{24,8},{1,17},{9,25},{17,1},{25,9},{2,18},{10... | collective-permute-start | bytes 1572872 | tf_op jit(solution)/shard_map/ppermute | solution.py:608
  108.8 2.6 %collective-permute-done.19.refs_1_ = bf16[256,512]{1,0:T(8,128)(2,1)S(1)} collective-permute-done((bf16[256,512]{1,0:T(8,128)(2,1)S(1)}, bf16[256,512]{1,0:T(8,128)(2,1)S(1)}, u32[]{:S(2)}, u32[]{:S(2)}) %collective-permute-start.19) | collective-permute-done | bytes 262176 | tf_op jit(solution)/shard_map/ppermute | solution.py:608
  111.6 5.5 %collective-permute-done.21.refs_1_ = bf16[256,512]{1,0:T(8,128)(2,1)S(1)} collective-permute-done((bf16[256,512]{1,0:T(8,128)(2,1)S(1)}, bf16[256,512]{1,0:T(8,128)(2,1)S(1)}, u32[]{:S(2)}, u32[]{:S(2)}) %collective-permute-start.21) | collective-permute-done | bytes 262176 | tf_op jit(solution)/shard_map/ppermute | solution.py:608
  118.3 12.9 %collective-permute-done.20.refs_2_ = bf16[256,512]{1,0:T(8,128)(2,1)S(1)} collective-permute-done((bf16[256,512]{1,0:T(8,128)(2,1)S(1)}, bf16[256,512]{1,0:T(8,128)(2,1)S(1)}, u32[]{:S(2)}, u32[]{:S(2)}) %collective-permute-start.20) | collective-permute-done | bytes 262176 | tf_op jit(solution)/shard_map/ppermute | solution.py:561
  131.1 4.9 %collective-permute-done.22.refs_3_ = bf16[256,512]{1,0:T(8,128)(2,1)S(1)} collective-permute-done((bf16[256,512]{1,0:T(8,128)(2,1)S(1)}, bf16[256,512]{1,0:T(8,128)(2,1)S(1)}, u32[]{:S(2)}, u32[]{:S(2)}) %collective-permute-start.22) | collective-permute-done | bytes 262176 | tf_op jit(solution)/shard_map/ppermute | solution.py:561
  (40 shorter events, 12.1 us)
Async XLA Ops:
  3.9 11.0 %collective-permute-start = (bf16[128,4096]{1,0:T(8,128)(2,1)}, bf16[128,4096]{1,0:T(8,128)(2,1)}, u32[]{:S(2)}, u32[]{:S(2)}) collective-permute-start(bf16[128,4096]{1,0:T(8,128)(2,1)} %get-tuple-element.42), channel_id=1, source_target_pairs={{0,8},{8,0},{16,24},{24,16},{1,9},{9,1},{17,25},{25,17},{2,10},{10... | collective-permute-start | bytes 3145736 | tf_op jit(solution)/shard_map/ppermute | solution.py:564
  4.4 45.4 %all-to-all-start = ((bf16[8,128,256]{2,1,0:T(8,128)(2,1)}), bf16[8,128,256]{2,1,0:T(8,128)(2,1)S(1)}, u32[]{:S(2)}, u32[]{:S(2)}) async-start(bf16[8,128,256]{2,1,0:T(8,128)(2,1)} %get-tuple-element.53), calls=%async_computation | async-start | bytes 1048576 | tf_op jit(solution)/shard_map/all_to_all | solution.py:567
  11.4 19.9 %collective-permute-start.1 = (bf16[128,2048]{1,0:T(8,128)(2,1)}, bf16[128,2048]{1,0:T(8,128)(2,1)}, u32[]{:S(2)}, u32[]{:S(2)}) collective-permute-start(bf16[128,2048]{1,0:T(8,128)(2,1)} %get-tuple-element.47), channel_id=1, source_target_pairs={{0,1},{1,0},{2,3},{3,2},{4,5},{5,4},{6,7},{7,6},{8,9},{9,8},{10,11... | collective-permute-start | bytes 1572872 | tf_op jit(solution)/shard_map/ppermute | solution.py:561
  13.4 21.5 %collective-permute-start.2 = (bf16[128,2048]{1,0:T(8,128)(2,1)}, bf16[128,2048]{1,0:T(8,128)(2,1)}, u32[]{:S(2)}, u32[]{:S(2)}) collective-permute-start(bf16[128,2048]{1,0:T(8,128)(2,1)} %get-tuple-element.48), channel_id=1, source_target_pairs={{0,2},{1,3},{2,0},{3,1},{4,6},{5,7},{6,4},{7,5},{8,10},{9,11},{10,... | collective-permute-start | bytes 1572872 | tf_op jit(solution)/shard_map/ppermute | solution.py:561
  14.9 31.4 %collective-permute-start.3 = (bf16[128,2048]{1,0:T(8,128)(2,1)}, bf16[128,2048]{1,0:T(8,128)(2,1)}, u32[]{:S(2)}, u32[]{:S(2)}) collective-permute-start(bf16[128,2048]{1,0:T(8,128)(2,1)} %get-tuple-element.49), channel_id=1, source_target_pairs={{0,3},{1,2},{2,1},{3,0},{4,7},{5,6},{6,5},{7,4},{8,11},{9,10},{10,... | collective-permute-start | bytes 1572872 | tf_op jit(solution)/shard_map/ppermute | solution.py:561
  46.3 16.0 %collective-permute-start.4 = (bf16[256,1024]{1,0:T(8,128)(2,1)}, bf16[256,1024]{1,0:T(8,128)(2,1)S(1)}, u32[]{:S(2)}, u32[]{:S(2)}) collective-permute-start(bf16[256,1024]{1,0:T(8,128)(2,1)} %get-tuple-element.50), channel_id=1, source_target_pairs={{0,1},{1,0},{2,3},{3,2},{4,5},{5,4},{6,7},{7,6},{8,9},{9,8},{10,11... | collective-permute-start | bytes 1572872 | tf_op jit(solution)/shard_map/ppermute | solution.py:561
  46.8 15.5 %collective-permute-start.5 = (bf16[256,1024]{1,0:T(8,128)(2,1)}, bf16[256,1024]{1,0:T(8,128)(2,1)S(1)}, u32[]{:S(2)}, u32[]{:S(2)}) collective-permute-start(bf16[256,1024]{1,0:T(8,128)(2,1)} %get-tuple-element.51), channel_id=1, source_target_pairs={{0,2},{1,3},{2,0},{3,1},{4,6},{5,7},{6,4},{7,5},{8,10},{9,11},{10,... | collective-permute-start | bytes 1572872 | tf_op jit(solution)/shard_map/ppermute | solution.py:561
  47.2 27.0 %collective-permute-start.6 = (bf16[256,1024]{1,0:T(8,128)(2,1)}, bf16[256,1024]{1,0:T(8,128)(2,1)}, u32[]{:S(2)}, u32[]{:S(2)}) collective-permute-start(bf16[256,1024]{1,0:T(8,128)(2,1)} %get-tuple-element.52), channel_id=1, source_target_pairs={{0,3},{1,2},{2,1},{3,0},{4,7},{5,6},{6,5},{7,4},{8,11},{9,10},{10,... | collective-permute-start | bytes 1572872 | tf_op jit(solution)/shard_map/ppermute | solution.py:561
  61.3 16.3 %collective-permute-start.8 = (bf16[128,1024]{1,0:T(8,128)(2,1)S(1)}, bf16[128,1024]{1,0:T(8,128)(2,1)S(1)}, u32[]{:S(2)}, u32[]{:S(2)}) collective-permute-start(bf16[128,1024]{1,0:T(8,128)(2,1)S(1)} %get-tuple-element.60), channel_id=1, source_target_pairs={{0,1},{1,0},{2,3},{3,2},{4,5},{5,4},{6,7},{7,6},{8,9},{9,8},{10,11... | collective-permute-start | bytes 786440 | tf_op jit(solution)/shard_map/ppermute | solution.py:561
  62.0 16.8 %collective-permute-start.9 = (bf16[128,1024]{1,0:T(8,128)(2,1)S(1)}, bf16[128,1024]{1,0:T(8,128)(2,1)S(1)}, u32[]{:S(2)}, u32[]{:S(2)}) collective-permute-start(bf16[128,1024]{1,0:T(8,128)(2,1)S(1)} %get-tuple-element.61), channel_id=1, source_target_pairs={{0,2},{1,3},{2,0},{3,1},{4,6},{5,7},{6,4},{7,5},{8,10},{9,11},{10,... | collective-permute-start | bytes 786440 | tf_op jit(solution)/shard_map/ppermute | solution.py:561
  74.2 12.9 %collective-permute-start.7 = (bf16[512,256]{1,0:T(8,128)(2,1)S(1)}, bf16[512,256]{1,0:T(8,128)(2,1)S(1)}, u32[]{:S(2)}, u32[]{:S(2)}) collective-permute-start(bf16[512,256]{1,0:T(8,128)(2,1)S(1)} %get-tuple-element.58), channel_id=1, source_target_pairs={{4,0},{5,1},{6,2},{7,3},{12,8},{13,9},{14,10},{15,11},{20,16},{21,... | collective-permute-start | bytes 786440 | tf_op jit(solution)/shard_map/ppermute | solution.py:588
  87.2 8.0 %collective-permute-start.13 = (bf16[512,256]{1,0:T(8,128)(2,1)S(1)}, bf16[512,256]{1,0:T(8,128)(2,1)S(1)}, u32[]{:S(2)}, u32[]{:S(2)}) collective-permute-start(bf16[512,256]{1,0:T(8,128)(2,1)S(1)} %add_convert_fusion.refs_0_), channel_id=1, source_target_pairs={{0,3},{1,2},{2,1},{3,0},{4,7},{5,6},{6,5},{7,4},{8,11},{9,10},{10,... | collective-permute-start | bytes 786440 | tf_op jit(solution)/shard_map/ppermute | solution.py:561
  87.3 10.3 %collective-permute-start.12 = (bf16[512,256]{1,0:T(8,128)(2,1)S(1)}, bf16[512,256]{1,0:T(8,128)(2,1)S(1)}, u32[]{:S(2)}, u32[]{:S(2)}) collective-permute-start(bf16[512,256]{1,0:T(8,128)(2,1)S(1)} %add_convert_fusion.refs_0_), channel_id=1, source_target_pairs={{0,2},{1,3},{2,0},{3,1},{4,6},{5,7},{6,4},{7,5},{8,10},{9,11},{10,... | collective-permute-start | bytes 786440 | tf_op jit(solution)/shard_map/ppermute | solution.py:561
  89.7 8.2 %collective-permute-start.11 = (bf16[512,256]{1,0:T(8,128)(2,1)S(1)}, bf16[512,256]{1,0:T(8,128)(2,1)S(1)}, u32[]{:S(2)}, u32[]{:S(2)}) collective-permute-start(bf16[512,256]{1,0:T(8,128)(2,1)S(1)} %add_convert_fusion.refs_0_), channel_id=1, source_target_pairs={{0,1},{1,0},{2,3},{3,2},{4,5},{5,4},{6,7},{7,6},{8,9},{9,8},{10,11... | collective-permute-start | bytes 786440 | tf_op jit(solution)/shard_map/ppermute | solution.py:561
  90.7 8.0 %collective-permute-start.14 = (bf16[512,256]{1,0:T(8,128)(2,1)S(1)}, bf16[512,256]{1,0:T(8,128)(2,1)S(1)}, u32[]{:S(2)}, u32[]{:S(2)}) collective-permute-start(bf16[512,256]{1,0:T(8,128)(2,1)S(1)} %add_convert_fusion.refs_0_), channel_id=1, source_target_pairs={{0,8},{8,0},{16,24},{24,16},{1,9},{9,1},{17,25},{25,17},{2,10},{10... | collective-permute-start | bytes 786440 | tf_op jit(solution)/shard_map/ppermute | solution.py:564
  95.2 3.5 %collective-permute-start.17 = (bf16[512,256]{1,0:T(8,128)(2,1)S(1)}, bf16[512,256]{1,0:T(8,128)(2,1)S(1)}, u32[]{:S(2)}, u32[]{:S(2)}) collective-permute-start(bf16[512,256]{1,0:T(8,128)(2,1)S(1)} %collective-permute-done.13.refs_3_), channel_id=1, source_target_pairs={{0,8},{8,0},{16,24},{24,16},{1,9},{9,1},{17,25},{25,17},{2,10},{10... | collective-permute-start | bytes 786440 | tf_op jit(solution)/shard_map/ppermute | solution.py:564
  97.5 1.5 %collective-permute-start.16 = (bf16[512,256]{1,0:T(8,128)(2,1)S(1)}, bf16[512,256]{1,0:T(8,128)(2,1)S(1)}, u32[]{:S(2)}, u32[]{:S(2)}) collective-permute-start(bf16[512,256]{1,0:T(8,128)(2,1)S(1)} %collective-permute-done.12.refs_2_), channel_id=1, source_target_pairs={{0,8},{8,0},{16,24},{24,16},{1,9},{9,1},{17,25},{25,17},{2,10},{10... | collective-permute-start | bytes 786440 | tf_op jit(solution)/shard_map/ppermute | solution.py:564
  97.9 1.5 %collective-permute-start.15 = (bf16[512,256]{1,0:T(8,128)(2,1)S(1)}, bf16[512,256]{1,0:T(8,128)(2,1)S(1)}, u32[]{:S(2)}, u32[]{:S(2)}) collective-permute-start(bf16[512,256]{1,0:T(8,128)(2,1)S(1)} %collective-permute-done.11.refs_1_), channel_id=1, source_target_pairs={{0,8},{8,0},{16,24},{24,16},{1,9},{9,1},{17,25},{25,17},{2,10},{10... | collective-permute-start | bytes 786440 | tf_op jit(solution)/shard_map/ppermute | solution.py:564
  98.0 10.8 %collective-permute-start.10 = (bf16[128,1024]{1,0:T(8,128)(2,1)S(1)}, bf16[128,1024]{1,0:T(8,128)(2,1)S(1)}, u32[]{:S(2)}, u32[]{:S(2)}) collective-permute-start(bf16[128,1024]{1,0:T(8,128)(2,1)S(1)} %get-tuple-element.65), channel_id=1, source_target_pairs={{0,3},{1,2},{2,1},{3,0},{4,7},{5,6},{6,5},{7,4},{8,11},{9,10},{10,... | collective-permute-start | bytes 786440 | tf_op jit(solution)/shard_map/ppermute | solution.py:561
  102.3 9.1 %collective-permute-start.19 = (bf16[256,512]{1,0:T(8,128)(2,1)S(1)}, bf16[256,512]{1,0:T(8,128)(2,1)S(1)}, u32[]{:S(2)}, u32[]{:S(2)}) collective-permute-start(bf16[256,512]{1,0:T(8,128)(2,1)S(1)} %get-tuple-element.77), channel_id=1, source_target_pairs={{0,16},{8,24},{16,0},{24,8},{1,17},{9,25},{17,1},{25,9},{2,18},{10... | collective-permute-start | bytes 786440 | tf_op jit(solution)/shard_map/ppermute | solution.py:608
  103.9 13.2 %collective-permute-start.21 = (bf16[256,512]{1,0:T(8,128)(2,1)S(1)}, bf16[256,512]{1,0:T(8,128)(2,1)S(1)}, u32[]{:S(2)}, u32[]{:S(2)}) collective-permute-start(bf16[256,512]{1,0:T(8,128)(2,1)S(1)} %get-tuple-element.79), channel_id=1, source_target_pairs={{0,16},{8,24},{16,0},{24,8},{1,17},{9,25},{17,1},{25,9},{2,18},{10... | collective-permute-start | bytes 786440 | tf_op jit(solution)/shard_map/ppermute | solution.py:608
  107.2 28.8 %collective-permute-start.18 = (bf16[256,1024]{1,0:T(8,128)(2,1)S(1)}, bf16[256,1024]{1,0:T(8,128)(2,1)S(1)}, u32[]{:S(2)}, u32[]{:S(2)}) collective-permute-start(bf16[256,1024]{1,0:T(8,128)(2,1)S(1)} %get-tuple-element.76), channel_id=1, source_target_pairs={{0,16},{8,24},{16,0},{24,8},{1,17},{9,25},{17,1},{25,9},{2,18},{10... | collective-permute-start | bytes 1572872 | tf_op jit(solution)/shard_map/ppermute | solution.py:608
  111.5 19.6 %collective-permute-start.20 = (bf16[256,512]{1,0:T(8,128)(2,1)S(1)}, bf16[256,512]{1,0:T(8,128)(2,1)S(1)}, u32[]{:S(2)}, u32[]{:S(2)}) collective-permute-start(bf16[256,512]{1,0:T(8,128)(2,1)S(1)} %sequences_added.2), channel_id=1, source_target_pairs={{0,4},{1,5},{2,6},{3,7},{4,0},{5,1},{6,2},{7,3},{8,12},{9,13},{10,... | collective-permute-start | bytes 786440 | tf_op jit(solution)/shard_map/ppermute | solution.py:561
  117.1 18.9 %collective-permute-start.22 = (bf16[256,512]{1,0:T(8,128)(2,1)S(1)}, bf16[256,512]{1,0:T(8,128)(2,1)S(1)}, u32[]{:S(2)}, u32[]{:S(2)}) collective-permute-start(bf16[256,512]{1,0:T(8,128)(2,1)S(1)} %sequences_added.3), channel_id=1, source_target_pairs={{0,4},{1,5},{2,6},{3,7},{4,0},{5,1},{6,2},{7,3},{8,12},{9,13},{10,... | collective-permute-start | bytes 786440 | tf_op jit(solution)/shard_map/ppermute | solution.py:561
  (3 other events, 95.1 us)
